TPU v7x, 32 devices: a whole 2x2x4 slice. The times are simulated.
32 devices in a mesh: gx: 8 (over y, x, core), gy: 4 (over z).
Axes of the slice: x: 2, y: 2, z: 4, core: 2. Of those that a mesh axis runs over, the one named last changes fastest.
Arguments:
- velocity: float32 [3, 256, 256, 256], P(None, 'gx', 'gy'), may hold values from -4 to 4
- fluid_noise: float32 [3, 256, 256, 256], P(None, 'gx', 'gy'), may hold values from -3 to 3
- cell: int32 [3, 4096], P(None, ('gx', 'gy')), may hold values from 0 to 255, as said below
- offset: float32 [3, 4096], P(None, ('gx', 'gy')), may hold values from 0 to 1
- colloid_velocity: float32 [3, 4096], P(None, ('gx', 'gy')), may hold values from -5 to 5
- particle_noise: float32 [3, 4096], P(None, ('gx', 'gy')), may hold values from -5 to 5
- counts: int32 [32], P(('gx', 'gy')), may hold values from 32 to 128, as said below
Outputs:
- new_velocity: float32 [3, 256, 256, 256], P(None, 'gx', 'gy')
- colloid_force: float32 [3, 4096], P(None, ('gx', 'gy'))
- colloid_drift: float32 [3, 4096], P(None, ('gx', 'gy'))
Inputs may be any that keep to these rules, and one draw needn't show every extreme that they name: `cell`: rows b * 128 to (b + 1) * 128 - 1 form block b. Their first coordinate lies from (b // 4) * 32 up to 32 more, their second from (b mod (4)) * 64 up to 64 more. `counts`: rows of a block at or beyond its count are padding. One block is full in every draw.
All inputs are finite; a program needn't handle non-finite values.
Results may differ from a plain program's by a relative error of at most 0.0003.
Values sent between devices are 32-bit elements; how exact they have to be, the bound alone decides.
No kernel may reach another device: no remote copies, remote signals or barrier semaphores. Data moves between devices by JAX's collectives and lax.ppermute only.
A program may use at most 192 MiB of HBM per device.

v0:
```python
import math

import jax
import jax.numpy as jnp
import numpy as np
from jax import lax
from jax.experimental import pallas as pl
from jax.experimental.pallas import tpu as pltpu
from jax.sharding import PartitionSpec as P

drag_rate = 1.0
time_step = 0.5
viscosity = 2.0


def padded(cells, sides, width):
    for axis, dim in sides:
        count = lax.axis_size(axis)
        head = lax.slice_in_dim(cells, 0, width, axis=dim)
        tail = lax.slice_in_dim(cells, cells.shape[dim] - width, cells.shape[dim], axis=dim)
        cells = jnp.concatenate(
            [
                lax.ppermute(tail, axis, [(i, (i + 1) % count) for i in range(count)]),
                cells,
                lax.ppermute(head, axis, [((i + 1) % count, i) for i in range(count)]),
            ],
            axis=dim,
        )
    return cells


def peskin(gap):
    distance = jnp.abs(gap)
    inner_dist = jnp.minimum(distance, 1.0)
    outer_dist = jnp.clip(distance, 1.0, 2.0)
    near_part = (
        3.0 - 2.0 * inner_dist + jnp.sqrt(1.0 + 4.0 * inner_dist - 4.0 * inner_dist * inner_dist)
    ) / 8.0
    far_part = (
        5.0 - 2.0 * outer_dist - jnp.sqrt(-7.0 + 12.0 * outer_dist - 4.0 * outer_dist * outer_dist)
    ) / 8.0
    return jnp.where(distance < 1.0, near_part, far_part)


f32 = jnp.float32
bf16 = jnp.bfloat16
lanes = 128
shift_term = 1.0 / (time_step * viscosity)


class Plan:
    def __init__(self, slab, pencil, grid, gx, gy):
        self.slab, self.pencil, self.grid, self.gx, self.gy = slab, pencil, grid, gx, gy
        self.slots = grid // 2 // gx
        self.chunks = max(1, self.slots // 8)
        self.kh = self.slots // self.chunks
        self.kk = 2 * self.kh
        self.yb = lanes // slab
        self.y_hi = pencil // self.yb
        self.y_block = max(min(16, pencil), self.yb)
        self.y_sub = self.y_block // self.yb
        self.groups = lanes // slab
        self.y_part = max(self.y_block, pencil // 2)


def split_three(value, axis):
    high = value.astype(bf16)
    low = (value - high.astype(f32)).astype(bf16)
    return jnp.concatenate([high, low, high], axis=axis)


def table_three(table, axis):
    table = jnp.asarray(np.asarray(table, np.float32))
    high = table.astype(bf16)
    low = (table - high.astype(f32)).astype(bf16)
    return jnp.concatenate([high, high, low], axis=axis)


def circle(rows, columns, length):
    angle = (np.outer(rows, columns) % length) * (2.0 * np.pi / length)
    cosine, sine = np.cos(angle), np.sin(angle)
    cosine[np.abs(cosine) < 1e-12] = 0.0
    sine[np.abs(sine) < 1e-12] = 0.0
    return cosine, sine


def cost(plan, giga_flops, mega_bytes):
    scale = plan.slab * plan.pencil * plan.grid / 2.0**19
    return pl.CostEstimate(
        flops=int(giga_flops * 1e9 * scale),
        bytes_accessed=int(mega_bytes * 1e6 * scale),
        transcendentals=0,
    )


def z_tables(plan):
    n = plan.grid
    cosine, sine = circle(np.arange(n // 2), np.arange(n), n)
    real_rows, imag_rows = cosine, -sine
    imag_rows[0] = 1.0 - 2.0 * (np.arange(n) % 2)
    back_scale = np.full((n // 2, 1), 2.0 / n)
    back_scale[0] = 1.0 / n
    order_shape = (plan.gx, plan.chunks, plan.kh)
    forward = np.stack([real_rows.reshape(order_shape + (n,)), imag_rows.reshape(order_shape + (n,))])
    backward = forward * np.stack([back_scale.reshape(order_shape + (1,))] * 2)
    forward = forward.transpose(2, 1, 0, 3, 4).reshape(n, n)
    backward = backward.transpose(2, 1, 0, 3, 4).reshape(n, n)
    return forward, backward


def x_tables(plan):
    n = plan.grid
    cosine, sine = circle(np.arange(n), np.arange(n), n)
    return np.concatenate([cosine, sine], axis=1), np.concatenate([cosine, sine], axis=0) / n


def half_sine(freq, length):
    return jnp.sin(freq.astype(f32) * (math.pi / length))


def coefficients(plan, chunk):
    n = plan.grid
    first = lax.axis_index("gx") * plan.slots + chunk * plan.kh
    slot = first + lax.broadcasted_iota(jnp.int32, (plan.kh, n), 0)
    kx = lax.broadcasted_iota(jnp.int32, (plan.kh, n), 1)
    half = n // 2
    special = slot == 0
    edge = special & ((kx == 0) | (kx == half))
    low = special & (kx > 0) & (kx < half)
    high = special & (kx > half)
    kz_real = jnp.where(high, half, slot)
    kz_imag = jnp.where(high | edge, half, slot)
    wave = half_sine(kx, n)
    dx_real = 2.0 * wave * wave
    dx_imag = jnp.where(kx == half, 0.0, jnp.sin(kx.astype(f32) * (2.0 * math.pi / n)))
    dz_imag = jnp.where(
        (kz_real == half) | edge, 0.0, jnp.sin(kz_real.astype(f32) * (2.0 * math.pi / n))
    )
    rows = [dx_real, dx_imag, dz_imag]
    weights = []
    for kz in (kz_real, kz_imag):
        depth = half_sine(kz, n)
        dz_real = 2.0 * depth * depth
        base = 2.0 * dx_real + 2.0 * dz_real
        flat = (base == 0.0).astype(f32)
        parts = [dz_real, 1.0 - flat]
        for step in (shift_term, 0.0):
            inner = base + step
            root = jnp.sqrt(inner * (4.0 + inner))
            singular = flat if step == 0.0 else jnp.zeros_like(flat)
            ratio = jnp.where(singular > 0.0, 1.0, 2.0 / (2.0 + inner + root))
            gain = jnp.where(singular > 0.0, 0.0, 1.0 / jnp.where(singular > 0.0, 1.0, root))
            if step != 0.0:
                gain = gain * step
            parts += [ratio, gain]
            weights.append((ratio, singular))
        rows += parts
    rows += [low.astype(f32), high.astype(f32), edge.astype(f32)]
    return jnp.stack(rows), weights


DXR, DXI, DZI = 0, 1, 2
DZR, SY, R1, C1, R0, C0 = 3, 4, 5, 6, 7, 8
PER_PART = 6
LOW, HIGH, EDGE = 15, 16, 17


def incoming(plan, ends, weights):
    gy, n, pencil = plan.gy, plan.grid, plan.pencil
    passed = [ends] + [
        lax.ppermute(ends, "gy", [(i, (i + hop) % gy) for i in range(gy)]) for hop in range(1, gy)
    ]
    factors = []
    for ratio, singular in weights:
        log_ratio = jnp.log(ratio)
        closing = 1.0 / jnp.where(singular > 0.0, 1.0, 1.0 - jnp.exp(log_ratio * n))
        factors.append((log_ratio, closing))
    (step1_r, step0_r, step1_i, step0_i) = factors
    per_row = [step1_r, step1_i] * 3 + [step0_r, step0_i]
    logs = jnp.stack([item[0] for item in per_row])
    closes = jnp.stack([item[1] for item in per_row])
    left = 0.0
    right = 0.0
    for hop in range(gy):
        back = ((hop - 1) % gy) * pencil
        ahead = ((-hop - 1) % gy) * pencil
        left = left + jnp.exp(logs * back) * passed[hop][:8]
        right = right + jnp.exp(logs * ahead) * passed[hop][8:]
    return jnp.concatenate([left * closes, right * closes])


def group_transpose(pieces, slab):
    pieces = list(pieces)
    count = len(pieces)
    lane = lax.broadcasted_iota(jnp.int32, pieces[0].shape, pieces[0].ndim - 1) // slab
    half = count // 2
    while half >= 1:
        upper = (lane // half) % 2 == 1
        for a in range(count):
            if (a // half) % 2 == 0:
                b = a + half
                first, second = pieces[a], pieces[b]
                axis = first.ndim - 1
                pieces[a] = jnp.where(upper, pltpu.roll(second, half * slab, axis), first)
                pieces[b] = jnp.where(upper, second, pltpu.roll(first, lanes - half * slab, axis))
        half //= 2
    return pieces


LAST = ((1,), (1,))


def shifted(component, dim):
    return jnp.where(component == dim, 1, 0)


def depth_forward_kernel(plan, refs, outs):
    velocity, noise, own, sides, table, side_rows, spread = refs
    rows8, slab, n = 8, plan.slab, plan.grid

    def product(plane, high, low):
        weight = jnp.concatenate([high, high, low], axis=1)
        return lax.dot_general(
            split_three(plane, 1), weight, (LAST, ((), ())), preferred_element_type=f32
        )

    @pl.when(pl.program_id(1) == 0)
    def _():
        wx, wy, wz_high, wz_low, force = sides
        for which, at in enumerate((0, slab - rows8)):
            lanes_of = slice(which * 3 * lanes, (which + 1) * 3 * lanes)
            across = wx[0, at : at + rows8, lanes_of] * (force[0, :, lanes_of] * time_step)
            plane = wy[0, :, lanes_of][:, None, :] * across[None, :, :]
            side_rows[which] = product(
                plane.reshape(plan.pencil * rows8, 3 * lanes),
                wz_high[0, :, lanes_of],
                wz_low[0, :, lanes_of],
            ).reshape(plan.pencil, rows8, n)

    wx, wy, wz_high, wz_low, force = own

    def block_step(index, carry):
        start = pl.multiple_of(index * plan.y_block, plan.y_block)
        place = pl.program_id(1) * (plan.y_part // plan.y_block) + index
        y_at = pl.multiple_of(place * plan.y_block, plan.y_block)

        def own_slab(group):
            lanes_of = slice(group * lanes, (group + 1) * lanes)
            across = wx[0, :slab, lanes_of] * (force[0, :, lanes_of] * time_step)
            along = wy[0, pl.ds(y_at, plan.y_block), lanes_of]
            plane = (along[:, None, :] * across[None, :, :]).reshape(plan.y_block * slab, lanes)
            return product(plane, wz_high[0, :, lanes_of], wz_low[0, :, lanes_of])

        spread[...] = own_slab(1)

        @pl.when(place == 0)
        def _():
            spread[...] += own_slab(0)

        @pl.when(place == plan.pencil // plan.y_block - 1)
        def _():
            spread[...] += own_slab(2)

        rhs = velocity[0, :, pl.ds(start, plan.y_block), :]
        rhs = rhs + noise[0, :, pl.ds(start, plan.y_block), :]
        rows = jnp.swapaxes(rhs, 0, 1) + spread[...].reshape(plan.y_block, slab, n)
        for which, at in enumerate((0, slab - rows8)):
            extra = side_rows[which, pl.ds(y_at, plan.y_block)]
            pieces = [rows[:, :at], rows[:, at : at + rows8] + extra, rows[:, at + rows8 :]]
            rows = jnp.concatenate([p for p in pieces if p.shape[1] > 0], axis=1)
        rows = rows.reshape(plan.y_block * slab, n)
        result = lax.dot_general(
            table[...], split_three(rows, 1), (LAST, ((), ())), preferred_element_type=f32
        )
        count = plan.gx * plan.kk
        for chunk, out in enumerate(outs):
            part = result[chunk * count : (chunk + 1) * count]
            for sub in range(plan.y_sub):
                out[:, 0, index * plan.y_sub + sub] = part[
                    :, sub * lanes : (sub + 1) * lanes
                ].reshape(plan.gx, plan.kk, lanes)
        return carry

    lax.fori_loop(0, plan.y_part // plan.y_block, block_step, 0)


def weight_blocks(plan, weights, wide):
    return [
        pl.BlockSpec((1, weights[0].shape[1], wide), lambda c, *y: (shifted(c, 0), 0, 0)),
        pl.BlockSpec((1, plan.pencil, wide), lambda c, *y: (shifted(c, 1), 0, 0)),
        pl.BlockSpec((1, plan.grid, wide), lambda c, *y: (shifted(c, 2), 0, 0)),
        pl.BlockSpec((1, plan.grid, wide), lambda c, *y: (shifted(c, 2), 0, 0)),
    ]


def depth_forward(plan, velocity, noise, own, sides):
    forward, _ = z_tables(plan)
    table = table_three(forward, 1)
    block = pl.BlockSpec((1, plan.slab, plan.y_part, plan.grid), lambda c, y: (c, 0, y, 0))
    out_shape = jax.ShapeDtypeStruct((plan.gx, 3, plan.y_hi, plan.kk, lanes), f32)
    out_block = pl.BlockSpec(
        (plan.gx, 1, plan.y_part // plan.yb, plan.kk, lanes), lambda c, y: (0, c, y, 0, 0)
    )
    blocks = []
    for group in (own, sides):
        wide = group[-1].shape[-1]
        blocks += weight_blocks(plan, group, wide)
        blocks.append(pl.BlockSpec((1, 1, wide), lambda c, y: (c, 0, 0)))
    first_out = 13
    after = first_out + plan.chunks
    return pl.pallas_call(
        lambda *refs: depth_forward_kernel(
            plan,
            (refs[0], refs[1], refs[2:7], refs[7:12], refs[12]) + refs[after:],
            refs[first_out:after],
        ),
        grid=(3, plan.pencil // plan.y_part),
        in_specs=[block, block] + blocks + [pl.BlockSpec(table.shape, lambda c, y: (0, 0))],
        out_specs=[out_block] * plan.chunks,
        out_shape=[out_shape] * plan.chunks,
        scratch_shapes=[
            pltpu.VMEM((2, plan.pencil, 8, plan.grid), f32),
            pltpu.VMEM((plan.y_block * plan.slab, plan.grid), f32),
        ],
        name="depth_forward",
        cost_estimate=cost(plan, 20, 8),
    )(velocity, noise, *own, *sides, table)


def depth_backward_kernel(plan, *refs):
    parts, table, out = refs[: plan.chunks], refs[plan.chunks], refs[plan.chunks + 1]

    def block_step(index, carry):
        columns = []
        for sub in range(plan.y_sub):
            columns.append(
                jnp.concatenate(
                    [
                        part[:, 0, index * plan.y_sub + sub].reshape(plan.gx * plan.kk, lanes)
                        for part in parts
                    ],
                    axis=0,
                )
            )
        spectrum = jnp.concatenate(columns, axis=1) if len(columns) > 1 else columns[0]
        rows = split_three(spectrum.T, 1)
        result = jnp.dot(rows, table[...], preferred_element_type=f32)
        start = pl.multiple_of(index * plan.y_block, plan.y_block)
        out[0, :, pl.ds(start, plan.y_block), :] = jnp.swapaxes(
            result.reshape(plan.y_block, plan.slab, plan.grid), 0, 1
        )
        return carry

    lax.fori_loop(0, plan.y_part // plan.y_block, block_step, 0)


def depth_backward(plan, parts):
    _, backward = z_tables(plan)
    table = table_three(backward, 0)
    in_block = pl.BlockSpec(
        (plan.gx, 1, plan.y_part // plan.yb, plan.kk, lanes), lambda c, y: (0, c, y, 0, 0)
    )
    return pl.pallas_call(
        lambda *refs: depth_backward_kernel(plan, *refs),
        grid=(3, plan.pencil // plan.y_part),
        in_specs=[in_block] * plan.chunks + [pl.BlockSpec(table.shape, lambda c, y: (0, 0))],
        out_specs=pl.BlockSpec(
            (1, plan.slab, plan.y_part, plan.grid), lambda c, y: (c, 0, y, 0)
        ),
        out_shape=jax.ShapeDtypeStruct((3, plan.slab, plan.pencil, plan.grid), f32),
        name="depth_backward",
        cost_estimate=cost(plan, 16, 6),
    )(*parts, table)


def sample_kernel(plan, field, below, above, wx, wy, wz_high, wz_low, out):
    slab, pencil, n = plan.slab, plan.pencil, plan.grid
    x_step = min(16, slab)

    for group in range(3):
        lanes_of = slice(group * lanes, (group + 1) * lanes)
        high, low = wz_high[0, :, lanes_of], wz_low[0, :, lanes_of]
        weight = jnp.concatenate([high, high, low], axis=0)

        def gathered(rows, along, across):
            count_x, count_y = rows.shape[0], rows.shape[1]
            line = jnp.dot(
                split_three(rows.reshape(count_x * count_y, n), 1),
                weight,
                preferred_element_type=f32,
            )
            line = jnp.sum(line.reshape(count_x, count_y, lanes) * along, axis=1)
            return jnp.sum(line * across, axis=0, keepdims=True)

        y_first = {0: 0, 1: 0, 2: pencil - 8}[group]
        ys = slice(y_first, y_first + (pencil if group == 1 else 8))
        along = wy[0, ys, lanes_of]
        ends = jnp.concatenate([below[0, :, ys, :], above[0, :, ys, :]], axis=0)
        if group == 1:

            def x_block(index, total):
                start = pl.multiple_of(index * x_step, x_step)
                across = wx[0, pl.ds(start, x_step), lanes_of]
                return total + gathered(field[0, pl.ds(start, x_step)], along, across)

            total = lax.fori_loop(0, slab // x_step, x_block, jnp.zeros((1, lanes), f32))
            total = total + gathered(ends, along, wx[0, slab : slab + 4, lanes_of])
        else:
            rows = jnp.concatenate([field[0, :, ys, :], ends], axis=0)
            total = gathered(rows, along, wx[0, : slab + 4, lanes_of])
        out[0, :, lanes_of] = total


def sample(plan, field, column):
    gx = plan.gx
    below = lax.ppermute(field[:, -2:], "gx", [(i, (i + 1) % gx) for i in range(gx)])
    above = lax.ppermute(field[:, :2], "gx", [((i + 1) % gx, i) for i in range(gx)])
    layers = pl.BlockSpec((1, 2, plan.pencil, plan.grid), lambda c: (c, 0, 0, 0))
    wide = 3 * lanes
    found = pl.pallas_call(
        lambda *refs: sample_kernel(plan, *refs),
        grid=(3,),
        in_specs=[
            pl.BlockSpec((1, plan.slab, plan.pencil, plan.grid), lambda c: (c, 0, 0, 0)),
            layers,
            layers,
        ]
        + weight_blocks(plan, column, wide),
        out_specs=pl.BlockSpec((1, 1, wide), lambda c: (c, 0, 0)),
        out_shape=jax.ShapeDtypeStruct((3, 1, wide), f32),
        name="sample",
        cost_estimate=cost(plan, 6, 8),
    )(field, below, above, *column)[:, 0]
    return found


def brought_home(plan, found):
    gy = plan.gy
    from_below = lax.ppermute(found[:, 2 * lanes :], "gy", [(i, (i + 1) % gy) for i in range(gy)])
    from_above = lax.ppermute(found[:, :lanes], "gy", [((i + 1) % gy, i) for i in range(gy)])
    return found[:, lanes : 2 * lanes] + from_below + from_above


def beside(plan, values):
    gx = plan.gx
    before = lax.ppermute(values, "gx", [(i, (i + 1) % gx) for i in range(gx)])
    after = lax.ppermute(values, "gx", [((i + 1) % gx, i) for i in range(gx)])
    return before, after


def weights_of(plan, spots):
    x_first = lax.axis_index("gx") * plan.slab
    y_first = lax.axis_index("gy") * plan.pencil
    row = jnp.arange(plan.slab + 8, dtype=jnp.int32)
    layer = jnp.where(
        row < plan.slab, row, jnp.where(row < plan.slab + 2, row - plan.slab - 2, row - 2)
    )
    nodes = (
        x_first + layer,
        y_first + jnp.arange(plan.pencil, dtype=jnp.int32),
        jnp.arange(plan.grid, dtype=jnp.int32),
    )
    found = []
    for axis_id in range(3):
        per_shift = []
        for shift in (0.0, 0.5):
            node = nodes[axis_id].astype(f32)[:, None] + shift
            gap = (
                jnp.mod(spots[axis_id][None, :] - node + 0.5 * plan.grid, plan.grid)
                - 0.5 * plan.grid
            )
            per_shift.append(peskin(gap))
        found.append(jnp.stack(per_shift))
    coarse = lax.reduce_precision(found[2], 8, 7)
    return found[0], found[1], coarse.astype(bf16), (found[2] - coarse).astype(bf16)


def part_rows(coef, part):
    base = PER_PART * part
    return [coef[base + row] for row in (DZR, SY, R1, C1, R0, C0)]


def divergence(coef, fields, previous):
    (xr, xi), (yr, yi), (zr, zi) = fields
    dzr_r, sy_r = coef[DZR], coef[SY]
    dzr_i, sy_i = coef[DZR + PER_PART], coef[SY + PER_PART]
    real = coef[DXR] * xr - coef[DXI] * xi + dzr_r * zr - coef[DZI] * zi + yr
    imag = coef[DXR] * xi + coef[DXI] * xr + dzr_i * zi + coef[DZI] * zr + yi
    if previous is not None:
        real = real - sy_r * previous[0]
        imag = imag - sy_i * previous[1]
    return real, imag


def line_forward_kernel(plan, chunk, yh_step, spectrum, coef, table, out, ends, powers, before):
    step = pl.program_id(0)
    n, kh, kk = plan.grid, plan.kh, plan.kk
    ys = yh_step * plan.yb

    @pl.when(step == 0)
    def _():
        ends[...] = jnp.zeros_like(ends)
        powers[...] = jnp.ones_like(powers)
        before[...] = jnp.zeros_like(before)

    rows = []
    for hi in range(yh_step):
        for c in range(3):
            columns = [
                group_transpose(
                    [spectrum[v * plan.groups + i, c, hi] for i in range(plan.groups)], plan.slab
                )
                for v in range(n // lanes)
            ]
            for q in range(plan.yb):
                rows.append(jnp.concatenate([column[q] for column in columns], axis=1))
    stacked = jnp.concatenate(rows, axis=0)
    result = jnp.dot(split_three(stacked, 1), table[...], preferred_element_type=f32)
    for hi in range(yh_step):
        for q in range(plan.yb):
            fields = []
            for c in range(3):
                at = ((hi * 3 + c) * plan.yb + q) * kk
                cos_r, sin_r = result[at : at + kh, :n], result[at : at + kh, n:]
                cos_i, sin_i = result[at + kh : at + kk, :n], result[at + kh : at + kk, n:]
                real = cos_r + sin_i
                imag = cos_i - sin_r
                if chunk == 0:
                    low, high = coef[LOW] > 0.5, coef[HIGH] > 0.5
                    real = jnp.where(low, cos_r, jnp.where(high, cos_i, real))
                    imag = jnp.where(low, -sin_r, jnp.where(high, -sin_i, imag))
                y = hi * plan.yb + q
                out[c, y, 0] = real
                out[c, y, 1] = imag
                fields.append((real, imag))
            div = divergence(coef, fields, (before[0], before[1]))
            for part in range(2):
                r1, r0 = coef[R1 + PER_PART * part], coef[R0 + PER_PART * part]
                p1, p0 = powers[part], powers[2 + part]
                for c in range(3):
                    row = 2 * c + part
                    value = fields[c][part]
                    ends[row] = ends[row] * r1 + value
                    ends[8 + row] = ends[8 + row] + p1 * value
                row = 6 + part
                ends[row] = ends[row] * r0 + div[part]
                ends[8 + row] = ends[8 + row] + p0 * div[part]
                powers[part] = p1 * r1
                powers[2 + part] = p0 * r0
                before[part] = fields[1][part]

    @pl.when(step == pl.num_programs(0) - 1)
    def _():
        for part in range(2):
            r0, sy = coef[R0 + PER_PART * part], coef[SY + PER_PART * part]
            spill = -sy * before[part]
            row = 6 + part
            ends[row] = ends[row] * r0 + spill
            ends[8 + row] = ends[8 + row] + powers[2 + part] * spill


def line_forward(plan, chunk, spectrum, coef):
    n, kh = plan.grid, plan.kh
    forward, _ = x_tables(plan)
    table = table_three(forward, 0)
    yh_step = 2 if plan.y_hi % 2 == 0 else 1
    ys = yh_step * plan.yb
    return pl.pallas_call(
        lambda *refs: line_forward_kernel(plan, chunk, yh_step, *refs),
        grid=(plan.y_hi // yh_step,),
        in_specs=[
            pl.BlockSpec((plan.gx, 3, yh_step, plan.kk, lanes), lambda s: (0, 0, s, 0, 0)),
            pl.BlockSpec(coef.shape, lambda s: (0, 0, 0)),
            pl.BlockSpec(table.shape, lambda s: (0, 0)),
        ],
        out_specs=[
            pl.BlockSpec((3, ys, 2, kh, n), lambda s: (0, s, 0, 0, 0)),
            pl.BlockSpec((16, kh, n), lambda s: (0, 0, 0)),
        ],
        out_shape=[
            jax.ShapeDtypeStruct((3, plan.pencil, 2, kh, n), f32),
            jax.ShapeDtypeStruct((16, kh, n), f32),
        ],
        scratch_shapes=[pltpu.VMEM((4, kh, n), f32), pltpu.VMEM((2, kh, n), f32)],
        name="line_forward",
        cost_estimate=cost(plan, 16 // plan.chunks, 20 // plan.chunks),
    )(spectrum, coef, table)


def line_backward_kernel(plan, chunk, yh_step, field, coef, entering, table, out, rest1, rest0, solved):
    n, kh, kk, length = plan.grid, plan.kh, plan.kk, plan.pencil
    parts = (0, 1)
    r1 = [coef[R1 + PER_PART * part] for part in parts]
    r0 = [coef[R0 + PER_PART * part] for part in parts]
    c1 = [coef[C1 + PER_PART * part] for part in parts]
    c0 = [coef[C0 + PER_PART * part] for part in parts]
    sy = [coef[SY + PER_PART * part] for part in parts]

    def fields_at(y):
        return [(field[c, y, 0], field[c, y, 1]) for c in range(3)]

    last = fields_at(length - 1)
    spill = [-sy[part] * last[1][part] for part in parts]
    start1 = [[entering[8 + 2 * c + part] * r1[part] for part in parts] for c in range(3)]
    start0 = [(entering[14 + part] + spill[part]) * r0[part] for part in parts]

    def upward(index, carry):
        after1, after0 = carry
        y = length - 1 - index
        values = fields_at(y)
        previous = jnp.maximum(y - 1, 0)
        keep = jnp.where(y > 0, 1.0, 0.0)
        div = divergence(
            coef, values, (field[1, previous, 0] * keep, field[1, previous, 1] * keep)
        )
        next1 = []
        for c in range(3):
            row = []
            for part in parts:
                rest1[c, y, part] = after1[c][part]
                row.append(r1[part] * (after1[c][part] + values[c][part]))
            next1.append(row)
        next0 = []
        for part in parts:
            rest0[y, part] = after0[part]
            next0.append(r0[part] * (after0[part] + div[part]))
        return next1, next0

    before1, _ = lax.fori_loop(0, length, upward, (start1, start0))

    left1 = [[entering[2 * c + part] for part in parts] for c in range(3)]
    first = [c1[part] * (left1[1][part] + before1[1][part]) for part in parts]
    zero = jnp.zeros_like(first[0])

    def settle(pressure_now, pressure_next, values, y):
        (xr, xi), (yr, yi), (zr, zi) = values
        pr, pi = pressure_now
        dxr, dxi, dzi = coef[DXR], coef[DXI], coef[DZI]
        xr = xr - dxr * pr - dxi * pi
        xi = xi - dxr * pi + dxi * pr
        zr = zr - coef[DZR] * pr - dzi * pi
        zi = zi - coef[DZR + PER_PART] * pi + dzi * pr
        out_y = []
        for part, value in ((0, yr), (1, yi)):
            value = value + pressure_next[part] - pressure_now[part]
            flat = 1.0 - sy[part]
            out_y.append(jnp.where(flat > 0.5, entering[6 + part] * (1.0 / n), value))
        solved[0, y, 0] = xr
        solved[0, y, 1] = xi
        solved[1, y, 0] = out_y[0]
        solved[1, y, 1] = out_y[1]
        solved[2, y, 0] = zr
        solved[2, y, 1] = zi

    def pressure_at(smooth, smooth_before, total0):
        around = divergence_plain(coef, smooth, smooth_before)
        return [c0[part] * total0[part] - around[part] for part in parts]

    def row_step(y, left1, left0, f_before):
        values = fields_at(y)
        div = divergence(coef, values, f_before)
        new1, smooth = [], []
        for c in range(3):
            row, out_row = [], []
            for part in parts:
                value = r1[part] * left1[c][part] + values[c][part]
                row.append(value)
                out_row.append(c1[part] * (value + rest1[c, y, part]))
            new1.append(row)
            smooth.append(out_row)
        new0 = [left0[part] + div[part] for part in parts]
        total0 = [new0[part] + rest0[y, part] for part in parts]
        carried0 = [r0[part] * new0[part] for part in parts]
        return values, new1, smooth, carried0, total0

    values, left1, smooth, left0, total0 = row_step(
        0, left1, [entering[6 + part] for part in parts], None
    )
    pressure = pressure_at(smooth, first, total0)

    def downward(y, carry):
        left1, left0, f_before, smooth_before, pressure_before = carry
        values, left1, smooth, left0, total0 = row_step(y, left1, left0, f_before)
        pressure = pressure_at(smooth, smooth_before[1], total0)
        settle(pressure_before, pressure, smooth_before, y - 1)
        return left1, left0, list(values[1]), smooth, pressure

    left1, left0, f_before, smooth, pressure = lax.fori_loop(
        1, length, downward, (left1, left0, list(values[1]), smooth, pressure)
    )
    end_smooth = [
        [c1[part] * (r1[part] * left1[c][part] + entering[8 + 2 * c + part]) for part in parts]
        for c in range(3)
    ]
    end_total = [left0[part] + spill[part] + entering[14 + part] for part in parts]
    end_pressure = pressure_at(end_smooth, smooth[1], end_total)
    settle(pressure, end_pressure, smooth, length - 1)

    def transform(group, carry):
        rows = []
        for hi in range(yh_step):
            for c in range(3):
                for q in range(plan.yb):
                    y = (group * yh_step + hi) * plan.yb + q
                    real, imag = solved[c, y, 0], solved[c, y, 1]
                    if chunk == 0:
                        low, high, edge = coef[LOW] > 0.5, coef[HIGH] > 0.5, coef[EDGE] > 0.5
                        any_special = low | high | edge
                        real_cos = jnp.where(low, 2.0 * real, jnp.where(high, 0.0, real))
                        real_sin = jnp.where(
                            low, 2.0 * imag, jnp.where(any_special, 0.0, imag)
                        )
                        imag_cos = jnp.where(
                            high, 2.0 * real, jnp.where(low, 0.0, imag)
                        )
                        imag_sin = jnp.where(
                            high, -2.0 * imag, jnp.where(any_special, 0.0, real)
                        )
                    else:
                        real_cos, real_sin, imag_cos, imag_sin = real, imag, imag, real
                    rows.append(jnp.concatenate([real_cos, -real_sin], axis=1))
                    rows.append(jnp.concatenate([imag_cos, imag_sin], axis=1))
        stacked = jnp.concatenate(rows, axis=0)
        result = jnp.dot(split_three(stacked, 1), table[...], preferred_element_type=f32)
        for hi in range(yh_step):
            for c in range(3):
                base = (hi * 3 + c) * plan.yb
                for v in range(n // lanes):
                    pieces = [
                        result[
                            (base + q) * kk : (base + q + 1) * kk, v * lanes : (v + 1) * lanes
                        ]
                        for q in range(plan.yb)
                    ]
                    for i, piece in enumerate(group_transpose(pieces, plan.slab)):
                        out[v * plan.groups + i, c, group * yh_step + hi] = piece
        return carry

    lax.fori_loop(0, plan.y_hi // yh_step, transform, 0)


def divergence_plain(coef, fields, previous):
    (xr, xi), (yr, yi), (zr, zi) = fields
    real = coef[DXR] * xr - coef[DXI] * xi + coef[DZR] * zr - coef[DZI] * zi + yr - previous[0]
    imag = (
        coef[DXR] * xi
        + coef[DXI] * xr
        + coef[DZR + PER_PART] * zi
        + coef[DZI] * zr
        + yi
        - previous[1]
    )
    return real, imag


def line_backward(plan, chunk, field, coef, entering):
    n, kh, length = plan.grid, plan.kh, plan.pencil
    _, backward = x_tables(plan)
    table = table_three(backward, 0)
    yh_step = 2 if plan.y_hi % 2 == 0 else 1
    whole = pl.BlockSpec(memory_space=pltpu.VMEM)
    return pl.pallas_call(
        lambda *refs: line_backward_kernel(plan, chunk, yh_step, *refs),
        in_specs=[whole] * 4,
        out_specs=whole,
        out_shape=jax.ShapeDtypeStruct((plan.gx, 3, plan.y_hi, plan.kk, lanes), f32),
        scratch_shapes=[
            pltpu.VMEM((3, length, 2, kh, n), f32),
            pltpu.VMEM((length, 2, kh, n), f32),
            pltpu.VMEM((3, length, 2, kh, n), f32),
        ],
        name="line_backward",
        cost_estimate=cost(plan, 24 // plan.chunks, 24 // plan.chunks),
        compiler_params=pltpu.CompilerParams(vmem_limit_bytes=48 * 1024 * 1024),
    )(field, coef, entering, table)


def project(plan, spectra):
    back = []
    for chunk, spectrum in enumerate(spectra):
        coef, weights = coefficients(plan, chunk)
        received = lax.all_to_all(spectrum, "gx", split_axis=0, concat_axis=0, tiled=True)
        field, ends = line_forward(plan, chunk, received, coef)
        entering = incoming(plan, ends, weights)
        solved = line_backward(plan, chunk, field, coef, entering)
        back.append(lax.all_to_all(solved, "gx", split_axis=0, concat_axis=0, tiled=True))
    return back


def per_device(velocity, fluid_noise, cell, offset, colloid_velocity, particle_noise, counts):
    plan = Plan(
        velocity.shape[1],
        velocity.shape[2],
        velocity.shape[3],
        lax.axis_size("gx"),
        lax.axis_size("gy"),
    )
    block_rows = cell.shape[1]
    places = cell.astype(f32) + offset
    live = (jnp.arange(block_rows, dtype=jnp.int32) < counts[0]).astype(f32)
    column_places = padded(places, (("gy", 1),), block_rows)
    column = weights_of(plan, column_places)
    found = sample(plan, velocity, column)
    before, after = beside(plan, column_places)
    side_places, found = lax.optimization_barrier((jnp.concatenate([before, after], axis=1), found))
    side_weights = weights_of(plan, side_places)
    sampled = brought_home(plan, found)
    colloid_force = live * (drag_rate * (colloid_velocity - sampled) + particle_noise)
    column_force = padded(colloid_force, (("gy", 1),), block_rows)
    side_force = jnp.concatenate(beside(plan, column_force), axis=1)
    spectra = depth_forward(
        plan,
        velocity,
        fluid_noise,
        column + (column_force[:, None, :],),
        side_weights + (side_force[:, None, :],),
    )
    new_velocity = depth_backward(plan, project(plan, spectra))
    colloid_drift = live * brought_home(plan, sample(plan, new_velocity, column))
    return (new_velocity, colloid_force, colloid_drift)


def solution(mesh):
    placed = (
        P(None, "gx", "gy", None),
        P(None, "gx", "gy", None),
        P(None, ("gx", "gy")),
        P(None, ("gx", "gy")),
        P(None, ("gx", "gy")),
        P(None, ("gx", "gy")),
        P(("gx", "gy")),
    )
    return jax.shard_map(
        per_device,
        mesh=mesh,
        in_specs=placed,
        out_specs=(P(None, "gx", "gy", None), P(None, ("gx", "gy")), P(None, ("gx", "gy"))),
        check_vma=False,
    )
```

profile of v0, /device:TPU:0, one launch (start us, length us, event | category | flops | bytes accessed | tf_op | source)
XLA Modules:
  0.0 277.3 jit_solution(3272984134607060859)
XLA Ops:
  1.3 5.1 %collective-permute-start.1 = (f32[3,128]{1,0:T(4,128)S(1)}, f32[3,128]{1,0:T(4,128)S(1)}, u32[]{:S(2)}, u32[]{:S(2)}) collective-permute-start(f32[3,128]{1,0:T(4,128)S(1)} %convert_add_fusion), channel_id=1, source_target_pairs={{1,0},{2,1},{3,2},{0,3},{5,4},{6,5},{7,6},{4,7},{9,8},{10,9},{11,1... | collective-permute-start | bytes 4616 | tf_op jit(solution)/shard_map/ppermute | solution.py:25
  6.4 1.2 fusion.239
  7.6 1.7 collective-permute-start.5
  12.7 2.7 collective-permute-start.3
  16.1 1.4 fusion.34
  18.3 1.0 fusion.1
  21.1 8.3 %sample.2 = f32[3,1,384]{2,1,0:T(1,128)} custom-call(f32[3,32,64,256]{3,2,1,0:T(8,128)} %refs_0_.3, f32[3,2,64,256]{3,2,1,0:T(8,128)} %copy-done.17, f32[3,2,64,256]{3,2,1,0:T(8,128)} %copy-done.16, f32[2,40,384]{2,1,0:T(8,128)} %pad_maximum_fusion.7.refs_3_.refs_2_, f32[2,64,384]{2,1,0:T(8,128)} %pad_maximum_fusion.4.refs_4_.refs_3_, ...), custom_call_target="tpu_custom_call" | custom-call | flops 6000000000 | bytes 8000000 | tf_op jit(solution)/shard_map/sample/pallas_call | solution.py:420
  30.3 3.9 %collective-permute-start.7 = (f32[3,128]{1,0:T(4,128)S(1)}, f32[3,128]{1,0:T(4,128)S(1)}, u32[]{:S(2)}, u32[]{:S(2)}) collective-permute-start(f32[3,128]{1,0:T(4,128)S(1)} %get-tuple-element.42), channel_id=1, source_target_pairs={{1,0},{2,1},{3,2},{0,3},{5,4},{6,5},{7,6},{4,7},{9,8},{10,9},{11,1... | collective-permute-start | bytes 4616 | tf_op jit(solution)/shard_map/ppermute | solution.py:440
  35.4 2.8 %fusion.6 = (f32[1,256,768]{2,1,0:T(8,128)S(1)}, f32[1,256,768]{2,1,0:T(8,128)S(1)}) fusion(f32[256]{0:T(256)S(1)} %iota_convert_fusion, f32[768]{0:T(1024)S(1)} %get-tuple-element.19, f32[256]{0:T(256)S(1)} %fusion.234), kind=kLoop, calls=%fused_computation.19 | loop fusion | flops 12189696 | bytes 1577984 | tf_op jit(solution)/shard_map/jit(_where)/select_n | solution.py:42
  38.2 1.4 fusion
  39.7 2.0 collective-permute-start.9
  41.7 0.8 pad_maximum_fusion.2.refs_8_
  42.5 0.8 collective-permute-done.9
  43.3 3.8 %collective-permute-done.8 = f32[3,128]{1,0:T(4,128)S(1)} collective-permute-done((f32[3,128]{1,0:T(4,128)S(1)}, f32[3,128]{1,0:T(4,128)S(1)}, u32[]{:S(2)}, u32[]{:S(2)}) %collective-permute-start.8) | collective-permute-done | bytes 1568 | tf_op jit(solution)/shard_map/ppermute | solution.py:23
  47.1 2.6 collective-permute-start.11
  51.7 19.0 %depth_forward.1 = (f32[8,3,16,16,128]{4,3,2,1,0:T(8,128)}, f32[8,3,16,16,128]{4,3,2,1,0:T(8,128)}) custom-call(f32[3,32,64,256]{3,2,1,0:T(8,128)} %refs_0_.3, f32[3,32,64,256]{3,2,1,0:T(8,128)} %refs_1_.1, f32[2,40,384]{2,1,0:T(8,128)} %pad_maximum_fusion.7.refs_3_.refs_2_, f32[2,64,384]{2,1,0:T(8,128)} %pad_maximum_fusion.4.refs_4_.refs_3_, ...), custom_call_target="tpu_custom_call" | custom-call | flops 20000000000 | bytes 8000000 | tf_op jit(solution)/shard_map/depth_forward/pallas_call | solution.py:311
  70.7 3.9 %all-to-all-start = ((f32[8,3,16,16,128]{4,3,2,1,0:T(8,128)}), f32[8,3,16,16,128]{4,3,2,1,0:T(8,128)S(1)}, u32[]{:S(2)}, u32[]{:S(2)}) async-start(f32[8,3,16,16,128]{4,3,2,1,0:T(8,128)} %get-tuple-element.13), calls=%async_computation | async-start | bytes 6291456 | tf_op jit(solution)/shard_map/all_to_all | solution.py:782
  74.6 0.8 constant_dynamic-update-slice_fusion.53
  76.1 0.8 constant_dynamic-update-slice_fusion.27
  76.9 0.8 constant_dynamic-update-slice_fusion.26
  78.3 34.2 %all-to-all-done.refs_0_ = f32[8,3,16,16,128]{4,3,2,1,0:T(8,128)S(1)} async-done(((f32[8,3,16,16,128]{4,3,2,1,0:T(8,128)}), f32[8,3,16,16,128]{4,3,2,1,0:T(8,128)S(1)}, u32[]{:S(2)}, u32[]{:S(2)}) %all-to-all-start) | async-done | bytes 3145760 | tf_op jit(solution)/shard_map/all_to_all | solution.py:782
  112.5 1.7 copy-done.6
  114.1 4.5 %all-to-all-start.2 = ((f32[8,3,16,16,128]{4,3,2,1,0:T(8,128)}), f32[8,3,16,16,128]{4,3,2,1,0:T(8,128)}, u32[]{:S(2)}, u32[]{:S(2)}) async-start(f32[8,3,16,16,128]{4,3,2,1,0:T(8,128)} %get-tuple-element.16), calls=%async_computation.2 | async-start | bytes 6291456 | tf_op jit(solution)/shard_map/all_to_all | solution.py:782
  119.4 9.6 %line_forward.2 = (f32[3,64,2,8,256]{4,3,2,1,0:T(8,128)}, f32[16,8,256]{2,1,0:T(8,128)}) custom-call(f32[8,3,16,16,128]{4,3,2,1,0:T(8,128)} %copy-done.6, f32[18,8,256]{2,1,0:T(8,128)} %copy-done.2, bf16[768,512]{1,0:T(8,128)(2,1)} %constant.226.refs_2_), custom_call_target="tpu_custom_call" | custom-call | flops 8000000000 | bytes 10000000 | tf_op jit(solution)/shard_map/line_forward/pallas_call | solution.py:568
  129.1 1.9 collective-permute-start.12
  131.0 5.1 %collective-permute-done.14 = f32[16,8,256]{2,1,0:T(8,128)S(1)} collective-permute-done((f32[16,8,256]{2,1,0:T(8,128)}, f32[16,8,256]{2,1,0:T(8,128)S(1)}, u32[]{:S(2)}, u32[]{:S(2)}) %collective-permute-start.14) | collective-permute-done | bytes 131104 | tf_op jit(solution)/shard_map/ppermute | solution.py:171
  136.2 5.5 %collective-permute-done.13 = f32[16,8,256]{2,1,0:T(8,128)S(1)} collective-permute-done((f32[16,8,256]{2,1,0:T(8,128)}, f32[16,8,256]{2,1,0:T(8,128)S(1)}, u32[]{:S(2)}, u32[]{:S(2)}) %collective-permute-start.13) | collective-permute-done | bytes 131104 | tf_op jit(solution)/shard_map/ppermute | solution.py:171
  141.7 0.9 fusion.155
  142.7 0.9 copy-done.3
  143.6 12.6 %line_backward.2 = f32[8,3,16,16,128]{4,3,2,1,0:T(8,128)} custom-call(f32[3,64,2,8,256]{4,3,2,1,0:T(8,128)} %get-tuple-element.14.refs_0_, f32[18,8,256]{2,1,0:T(8,128)S(1)} %copy-done.3, f32[16,8,256]{2,1,0:T(8,128)S(1)} %pad_maximum_fusion.5.refs_2_, bf16[1536,256]{1,0:T(8,128)(2,1)S(1)} %copy-done.4), custom_call_target="tpu_custom_call" | custom-call | flops 12000000000 | bytes 12000000 | tf_op jit(solution)/shard_map/line_backward/pallas_call | solution.py:762
  156.5 4.5 %all-to-all-start.1 = ((f32[8,3,16,16,128]{4,3,2,1,0:T(8,128)}), f32[8,3,16,16,128]{4,3,2,1,0:T(8,128)}, u32[]{:S(2)}, u32[]{:S(2)}) async-start(f32[8,3,16,16,128]{4,3,2,1,0:T(8,128)} %line_backward.2), calls=%async_computation.1 | async-start | bytes 6291456 | tf_op jit(solution)/shard_map/all_to_all | solution.py:786
  161.0 9.4 %line_forward.3 = (f32[3,64,2,8,256]{4,3,2,1,0:T(8,128)}, f32[16,8,256]{2,1,0:T(8,128)}) custom-call(f32[8,3,16,16,128]{4,3,2,1,0:T(8,128)} %all-to-all-done.2.refs_0_, f32[18,8,256]{2,1,0:T(8,128)} %copy-done, bf16[768,512]{1,0:T(8,128)(2,1)} %constant.226.refs_2_), custom_call_target="tpu_custom_call" | custom-call | flops 8000000000 | bytes 10000000 | tf_op jit(solution)/shard_map/line_forward/pallas_call | solution.py:568
  170.3 0.8 collective-permute-start.17
  171.2 1.9 collective-permute-start.16
  173.1 2.0 collective-permute-start.15
  175.0 1.3 collective-permute-done.17
  176.3 9.4 %collective-permute-done.16 = f32[16,8,256]{2,1,0:T(8,128)S(1)} collective-permute-done((f32[16,8,256]{2,1,0:T(8,128)}, f32[16,8,256]{2,1,0:T(8,128)S(1)}, u32[]{:S(2)}, u32[]{:S(2)}) %collective-permute-start.16) | collective-permute-done | bytes 131104 | tf_op jit(solution)/shard_map/ppermute | solution.py:171
  185.7 0.9 fusion.147
  186.7 1.1 copy-done.5
  187.8 10.8 %line_backward.3 = f32[8,3,16,16,128]{4,3,2,1,0:T(8,128)S(1)} custom-call(f32[3,64,2,8,256]{4,3,2,1,0:T(8,128)} %get-tuple-element.17.refs_0_, f32[18,8,256]{2,1,0:T(8,128)S(1)} %copy-done.1, f32[16,8,256]{2,1,0:T(8,128)S(1)} %pad_maximum_fusion.6.refs_2_, bf16[1536,256]{1,0:T(8,128)(2,1)S(1)} %copy-done.5), custom_call_target="tpu_custom_call" | custom-call | flops 12000000000 | bytes 12000000 | tf_op jit(solution)/shard_map/line_backward/pallas_call | solution.py:762
  198.8 41.3 %all_to_all.20.refs_1_ = f32[8,3,16,16,128]{4,3,2,1,0:T(8,128)} all-to-all(f32[8,3,16,16,128]{4,3,2,1,0:T(8,128)S(1)} %line_backward.3), channel_id=1, replica_groups=mesh['gx'=8,'gy'=4] {'gx'}, dimensions={0} | all-to-all | bytes 6291456 | tf_op jit(solution)/shard_map/all_to_all | solution.py:786
  240.1 9.3 %depth_backward.1.refs_0_ = f32[3,32,64,256]{3,2,1,0:T(8,128)} custom-call(f32[8,3,16,16,128]{4,3,2,1,0:T(8,128)} %all-to-all-done.1.refs_0_, f32[8,3,16,16,128]{4,3,2,1,0:T(8,128)} %all_to_all.20.refs_1_, bf16[768,256]{1,0:T(8,128)(2,1)} %constant.236.refs_2_), custom_call_target="tpu_custom_call" | custom-call | flops 16000000000 | bytes 6000000 | tf_op jit(solution)/shard_map/depth_backward/pallas_call | solution.py:363
  249.4 1.2 fusion.238
  251.1 8.7 %collective-permute-done.19.refs_2_ = f32[3,2,64,256]{3,2,1,0:T(8,128)S(1)} collective-permute-done((f32[3,2,64,256]{3,2,1,0:T(8,128)S(1)}, f32[3,2,64,256]{3,2,1,0:T(8,128)S(1)}, u32[]{:S(2)}, u32[]{:S(2)}) %collective-permute-start.19) | collective-permute-done | bytes 393248 | tf_op jit(solution)/shard_map/ppermute | solution.py:417
  259.8 1.7 collective-permute-done.18.refs_1_
  262.3 8.3 %sample.3 = f32[3,1,384]{2,1,0:T(1,128)} custom-call(f32[3,32,64,256]{3,2,1,0:T(8,128)} %depth_backward.1.refs_0_, f32[3,2,64,256]{3,2,1,0:T(8,128)} %copy-done.19, f32[3,2,64,256]{3,2,1,0:T(8,128)} %copy-done.18, f32[2,40,384]{2,1,0:T(8,128)} %pad_maximum_fusion.7.refs_3_.refs_2_, f32[2,64,384]{2,1,0:T(8,128)} %pad_maximum_fusion.4.refs_4_.refs_3_, ...), custom_call_target="tpu_custom_call" | custom-call | flops 6000000000 | bytes 8000000 | tf_op jit(solution)/shard_map/sample/pallas_call | solution.py:420
  271.8 3.3 %collective-permute-start.21 = (f32[3,128]{1,0:T(4,128)S(1)}, f32[3,128]{1,0:T(4,128)S(1)}, u32[]{:S(2)}, u32[]{:S(2)}) collective-permute-start(f32[3,128]{1,0:T(4,128)S(1)} %get-tuple-element.38), channel_id=1, source_target_pairs={{1,0},{2,1},{3,2},{0,3},{5,4},{6,5},{7,6},{4,7},{9,8},{10,9},{11,1... | collective-permute-start | bytes 4616 | tf_op jit(solution)/shard_map/ppermute | solution.py:440
  275.1 1.6 collective-permute-done.20
  (130 shorter events, 16.5 us)
Async XLA Ops:
  1.3 11.3 %collective-permute-start.1 = (f32[3,128]{1,0:T(4,128)S(1)}, f32[3,128]{1,0:T(4,128)S(1)}, u32[]{:S(2)}, u32[]{:S(2)}) collective-permute-start(f32[3,128]{1,0:T(4,128)S(1)} %convert_add_fusion), channel_id=1, source_target_pairs={{1,0},{2,1},{3,2},{0,3},{5,4},{6,5},{7,6},{4,7},{9,8},{10,9},{11,1... | collective-permute-start | bytes 4616 | tf_op jit(solution)/shard_map/ppermute | solution.py:25
  6.4 6.2 %collective-permute-start = (f32[3,128]{1,0:T(4,128)S(1)}, f32[3,128]{1,0:T(4,128)S(1)}, u32[]{:S(2)}, u32[]{:S(2)}) collective-permute-start(f32[3,128]{1,0:T(4,128)S(1)} %convert_add_fusion), channel_id=1, source_target_pairs={{0,1},{1,2},{2,3},{3,0},{4,5},{5,6},{6,7},{7,4},{8,9},{9,10},{10,1... | collective-permute-start | bytes 4616 | tf_op jit(solution)/shard_map/ppermute | solution.py:23
  7.6 12.6 %collective-permute-start.5 = (f32[3,2,64,256]{3,2,1,0:T(8,128)S(1)}, f32[3,2,64,256]{3,2,1,0:T(8,128)S(1)}, u32[]{:S(2)}, u32[]{:S(2)}) collective-permute-start(f32[3,2,64,256]{3,2,1,0:T(8,128)S(1)} %get-tuple-element.27), channel_id=1, source_target_pairs={{4,0},{8,4},{12,8},{16,12},{20,16},{24,20},{28,24},{0,28},{5,1},{9... | collective-permute-start | bytes 1179656 | tf_op jit(solution)/shard_map/ppermute | solution.py:417
  9.3 11.0 %collective-permute-start.4 = (f32[3,2,64,256]{3,2,1,0:T(8,128)S(1)}, f32[3,2,64,256]{3,2,1,0:T(8,128)S(1)}, u32[]{:S(2)}, u32[]{:S(2)}) collective-permute-start(f32[3,2,64,256]{3,2,1,0:T(8,128)S(1)} %get-tuple-element.28), channel_id=1, source_target_pairs={{0,4},{4,8},{8,12},{12,16},{16,20},{20,24},{24,28},{28,0},{1,5},{5... | collective-permute-start | bytes 1179656 | tf_op jit(solution)/shard_map/ppermute | solution.py:416
  11.4 4.7 %copy-start.9 = (f32[8,8,256]{2,1,0:T(8,128)}, f32[8,8,256]{2,1,0:T(8,128)S(1)}, u32[]{:S(2)}) copy-start(f32[8,8,256]{2,1,0:T(8,128)S(1)} %get-tuple-element.52) | copy-start | bytes 196612
  12.6 3.5 %copy-start.7 = (f32[8,8,256]{2,1,0:T(8,128)}, f32[8,8,256]{2,1,0:T(8,128)S(1)}, u32[]{:S(2)}) copy-start(f32[8,8,256]{2,1,0:T(8,128)S(1)} %get-tuple-element.59) | copy-start | bytes 196612
  12.6 3.5 %copy-start.11 = (f32[8,8,256]{2,1,0:T(8,128)}, f32[8,8,256]{2,1,0:T(8,128)S(1)}, u32[]{:S(2)}) copy-start(f32[8,8,256]{2,1,0:T(8,128)S(1)} %get-tuple-element.58) | copy-start | bytes 196612
  12.7 7.3 %collective-permute-start.3 = (f32[3,384]{1,0:T(4,128)S(1)}, f32[3,384]{1,0:T(4,128)S(1)}, u32[]{:S(2)}, u32[]{:S(2)}) collective-permute-start(f32[3,384]{1,0:T(4,128)S(1)} %pad_maximum_fusion.9), channel_id=1, source_target_pairs={{4,0},{8,4},{12,8},{16,12},{20,16},{24,20},{28,24},{0,28},{5,1},{9... | collective-permute-start | bytes 13832 | tf_op jit(solution)/shard_map/ppermute | solution.py:447
  15.4 4.8 %collective-permute-start.2 = (f32[3,384]{1,0:T(4,128)S(1)}, f32[3,384]{1,0:T(4,128)S(1)}, u32[]{:S(2)}, u32[]{:S(2)}) collective-permute-start(f32[3,384]{1,0:T(4,128)S(1)} %pad_maximum_fusion.9), channel_id=1, source_target_pairs={{0,4},{4,8},{8,12},{12,16},{16,20},{20,24},{24,28},{28,0},{1,5},{5... | collective-permute-start | bytes 13832 | tf_op jit(solution)/shard_map/ppermute | solution.py:446
  20.2 0.8 copy-start.16
  20.2 0.9 copy-start.17
  29.4 10.2 %copy-start.14 = (f32[3,128]{1,0:T(4,128)S(1)}, f32[3,128]{1,0:T(4,128)}, u32[]{:S(2)}) copy-start(f32[3,128]{1,0:T(4,128)} %param.18) | copy-start | bytes 4612
  29.4 10.2 %copy-start.15 = (f32[3,128]{1,0:T(4,128)S(1)}, f32[3,128]{1,0:T(4,128)}, u32[]{:S(2)}) copy-start(f32[3,128]{1,0:T(4,128)} %param.17) | copy-start | bytes 4612
  30.2 9.4 %collective-permute-start.6 = (f32[3,128]{1,0:T(4,128)S(1)}, f32[3,128]{1,0:T(4,128)S(1)}, u32[]{:S(2)}, u32[]{:S(2)}) collective-permute-start(f32[3,128]{1,0:T(4,128)S(1)} %get-tuple-element.41), channel_id=1, source_target_pairs={{0,1},{1,2},{2,3},{3,0},{4,5},{5,6},{6,7},{7,4},{8,9},{9,10},{10,1... | collective-permute-start | bytes 4616 | tf_op jit(solution)/shard_map/ppermute | solution.py:439
  30.3 9.3 %collective-permute-start.7 = (f32[3,128]{1,0:T(4,128)S(1)}, f32[3,128]{1,0:T(4,128)S(1)}, u32[]{:S(2)}, u32[]{:S(2)}) collective-permute-start(f32[3,128]{1,0:T(4,128)S(1)} %get-tuple-element.42), channel_id=1, source_target_pairs={{1,0},{2,1},{3,2},{0,3},{5,4},{6,5},{7,6},{4,7},{9,8},{10,9},{11,1... | collective-permute-start | bytes 4616 | tf_op jit(solution)/shard_map/ppermute | solution.py:440
  39.6 31.1 %copy-start.13 = (f32[3,128]{1,0:T(4,128)}, f32[3,128]{1,0:T(4,128)S(1)}, u32[]{:S(2)}) copy-start(f32[3,128]{1,0:T(4,128)S(1)} %add_multiply_fusion.6) | copy-start | bytes 4612
  39.7 3.6 %collective-permute-start.9 = (f32[3,128]{1,0:T(4,128)S(1)}, f32[3,128]{1,0:T(4,128)S(1)}, u32[]{:S(2)}, u32[]{:S(2)}) collective-permute-start(f32[3,128]{1,0:T(4,128)S(1)} %add_multiply_fusion.6), channel_id=1, source_target_pairs={{1,0},{2,1},{3,2},{0,3},{5,4},{6,5},{7,6},{4,7},{9,8},{10,9},{11,1... | collective-permute-start | bytes 4616 | tf_op jit(solution)/shard_map/ppermute | solution.py:25
  41.7 5.4 %collective-permute-start.8 = (f32[3,128]{1,0:T(4,128)S(1)}, f32[3,128]{1,0:T(4,128)S(1)}, u32[]{:S(2)}, u32[]{:S(2)}) collective-permute-start(f32[3,128]{1,0:T(4,128)S(1)} %add_multiply_fusion.6), channel_id=1, source_target_pairs={{0,1},{1,2},{2,3},{3,0},{4,5},{5,6},{6,7},{7,4},{8,9},{9,10},{10,1... | collective-permute-start | bytes 4616 | tf_op jit(solution)/shard_map/ppermute | solution.py:23
  47.1 4.0 %collective-permute-start.10 = (f32[3,384]{1,0:T(4,128)S(1)}, f32[3,384]{1,0:T(4,128)S(1)}, u32[]{:S(2)}, u32[]{:S(2)}) collective-permute-start(f32[3,384]{1,0:T(4,128)S(1)} %get-tuple-element.39), channel_id=1, source_target_pairs={{0,4},{4,8},{8,12},{12,16},{16,20},{20,24},{24,28},{28,0},{1,5},{5... | collective-permute-start | bytes 13832 | tf_op jit(solution)/shard_map/ppermute | solution.py:446
  47.1 4.0 %collective-permute-start.11 = (f32[3,384]{1,0:T(4,128)S(1)}, f32[3,384]{1,0:T(4,128)S(1)}, u32[]{:S(2)}, u32[]{:S(2)}) collective-permute-start(f32[3,384]{1,0:T(4,128)S(1)} %get-tuple-element.39), channel_id=1, source_target_pairs={{4,0},{8,4},{12,8},{16,12},{20,16},{24,20},{28,24},{0,28},{5,1},{9... | collective-permute-start | bytes 13832 | tf_op jit(solution)/shard_map/ppermute | solution.py:447
  70.7 41.7 %all-to-all-start = ((f32[8,3,16,16,128]{4,3,2,1,0:T(8,128)}), f32[8,3,16,16,128]{4,3,2,1,0:T(8,128)S(1)}, u32[]{:S(2)}, u32[]{:S(2)}) async-start(f32[8,3,16,16,128]{4,3,2,1,0:T(8,128)} %get-tuple-element.13), calls=%async_computation | async-start | bytes 6291456 | tf_op jit(solution)/shard_map/all_to_all | solution.py:782
  112.5 1.7 copy-start.6
  114.1 42.3 %all-to-all-start.2 = ((f32[8,3,16,16,128]{4,3,2,1,0:T(8,128)}), f32[8,3,16,16,128]{4,3,2,1,0:T(8,128)}, u32[]{:S(2)}, u32[]{:S(2)}) async-start(f32[8,3,16,16,128]{4,3,2,1,0:T(8,128)} %get-tuple-element.16), calls=%async_computation.2 | async-start | bytes 6291456 | tf_op jit(solution)/shard_map/all_to_all | solution.py:782
  118.8 0.7 copy-start.2
  118.8 10.2 %copy-start = (f32[18,8,256]{2,1,0:T(8,128)}, f32[18,8,256]{2,1,0:T(8,128)S(1)}, u32[]{:S(2)}) copy-start(f32[18,8,256]{2,1,0:T(8,128)S(1)} %get-tuple-element.114.refs_1_) | copy-start | bytes 442372
  119.4 22.3 %copy-start.8 = (f32[8,8,256]{2,1,0:T(8,128)S(1)}, f32[8,8,256]{2,1,0:T(8,128)}, u32[]{:S(2)}) copy-start(f32[8,8,256]{2,1,0:T(8,128)} %get-tuple-element.65) | copy-start | bytes 196612
  119.4 22.3 %copy-start.12 = (f32[8,8,256]{2,1,0:T(8,128)S(1)}, f32[8,8,256]{2,1,0:T(8,128)}, u32[]{:S(2)}) copy-start(f32[8,8,256]{2,1,0:T(8,128)} %copy-done.11) | copy-start | bytes 196612
  119.4 23.2 %copy-start.4 = (bf16[1536,256]{1,0:T(8,128)(2,1)S(1)}, bf16[1536,256]{1,0:T(8,128)(2,1)}, u32[]{:S(2)}) copy-start(bf16[1536,256]{1,0:T(8,128)(2,1)} %constant.231.refs_3_) | copy-start | bytes 2359300
  129.0 7.2 %collective-permute-start.14 = (f32[16,8,256]{2,1,0:T(8,128)}, f32[16,8,256]{2,1,0:T(8,128)S(1)}, u32[]{:S(2)}, u32[]{:S(2)}) collective-permute-start(f32[16,8,256]{2,1,0:T(8,128)} %get-tuple-element.15), channel_id=1, source_target_pairs={{0,3},{1,0},{2,1},{3,2},{4,7},{5,4},{6,5},{7,6},{8,11},{9,8},{10,9... | collective-permute-start | bytes 393224 | tf_op jit(solution)/shard_map/ppermute | solution.py:171
  129.1 12.6 %collective-permute-start.13 = (f32[16,8,256]{2,1,0:T(8,128)}, f32[16,8,256]{2,1,0:T(8,128)S(1)}, u32[]{:S(2)}, u32[]{:S(2)}) collective-permute-start(f32[16,8,256]{2,1,0:T(8,128)} %get-tuple-element.15), channel_id=1, source_target_pairs={{0,2},{1,3},{2,0},{3,1},{4,6},{5,7},{6,4},{7,5},{8,10},{9,11},{10,... | collective-permute-start | bytes 393224 | tf_op jit(solution)/shard_map/ppermute | solution.py:171
  129.1 12.5 %collective-permute-start.12 = (f32[16,8,256]{2,1,0:T(8,128)}, f32[16,8,256]{2,1,0:T(8,128)S(1)}, u32[]{:S(2)}, u32[]{:S(2)}) collective-permute-start(f32[16,8,256]{2,1,0:T(8,128)} %get-tuple-element.15), channel_id=1, source_target_pairs={{0,1},{1,2},{2,3},{3,0},{4,5},{5,6},{6,7},{7,4},{8,9},{9,10},{10,1... | collective-permute-start | bytes 393224 | tf_op jit(solution)/shard_map/ppermute | solution.py:171
  142.6 0.9 copy-start.3
  156.5 42.3 %all-to-all-start.1 = ((f32[8,3,16,16,128]{4,3,2,1,0:T(8,128)}), f32[8,3,16,16,128]{4,3,2,1,0:T(8,128)}, u32[]{:S(2)}, u32[]{:S(2)}) async-start(f32[8,3,16,16,128]{4,3,2,1,0:T(8,128)} %line_backward.2), calls=%async_computation.1 | async-start | bytes 6291456 | tf_op jit(solution)/shard_map/all_to_all | solution.py:786
  160.9 24.7 %copy-start.10 = (f32[8,8,256]{2,1,0:T(8,128)S(1)}, f32[8,8,256]{2,1,0:T(8,128)}, u32[]{:S(2)}) copy-start(f32[8,8,256]{2,1,0:T(8,128)} %get-tuple-element.87) | copy-start | bytes 196612
  160.9 25.7 %copy-start.1 = (f32[18,8,256]{2,1,0:T(8,128)S(1)}, f32[18,8,256]{2,1,0:T(8,128)}, u32[]{:S(2)}) copy-start(f32[18,8,256]{2,1,0:T(8,128)} %copy-done) | copy-start | bytes 442372
  170.3 6.0 %collective-permute-start.17 = (f32[16,8,256]{2,1,0:T(8,128)}, f32[16,8,256]{2,1,0:T(8,128)S(1)}, u32[]{:S(2)}, u32[]{:S(2)}) collective-permute-start(f32[16,8,256]{2,1,0:T(8,128)} %get-tuple-element.18), channel_id=1, source_target_pairs={{0,3},{1,0},{2,1},{3,2},{4,7},{5,4},{6,5},{7,6},{8,11},{9,8},{10,9... | collective-permute-start | bytes 393224 | tf_op jit(solution)/shard_map/ppermute | solution.py:171
  171.2 14.5 %collective-permute-start.16 = (f32[16,8,256]{2,1,0:T(8,128)}, f32[16,8,256]{2,1,0:T(8,128)S(1)}, u32[]{:S(2)}, u32[]{:S(2)}) collective-permute-start(f32[16,8,256]{2,1,0:T(8,128)} %get-tuple-element.18), channel_id=1, source_target_pairs={{0,2},{1,3},{2,0},{3,1},{4,6},{5,7},{6,4},{7,5},{8,10},{9,11},{10,... | collective-permute-start | bytes 393224 | tf_op jit(solution)/shard_map/ppermute | solution.py:171
  173.1 12.6 %collective-permute-start.15 = (f32[16,8,256]{2,1,0:T(8,128)}, f32[16,8,256]{2,1,0:T(8,128)S(1)}, u32[]{:S(2)}, u32[]{:S(2)}) collective-permute-start(f32[16,8,256]{2,1,0:T(8,128)} %get-tuple-element.18), channel_id=1, source_target_pairs={{0,1},{1,2},{2,3},{3,0},{4,5},{5,6},{6,7},{7,4},{8,9},{9,10},{10,1... | collective-permute-start | bytes 393224 | tf_op jit(solution)/shard_map/ppermute | solution.py:171
  186.7 1.1 copy-start.5
  250.6 9.2 %collective-permute-start.19 = (f32[3,2,64,256]{3,2,1,0:T(8,128)S(1)}, f32[3,2,64,256]{3,2,1,0:T(8,128)S(1)}, u32[]{:S(2)}, u32[]{:S(2)}) collective-permute-start(f32[3,2,64,256]{3,2,1,0:T(8,128)S(1)} %get-tuple-element.25), channel_id=1, source_target_pairs={{4,0},{8,4},{12,8},{16,12},{20,16},{24,20},{28,24},{0,28},{5,1},{9... | collective-permute-start | bytes 1179656 | tf_op jit(solution)/shard_map/ppermute | solution.py:417
  250.6 10.9 %collective-permute-start.18 = (f32[3,2,64,256]{3,2,1,0:T(8,128)S(1)}, f32[3,2,64,256]{3,2,1,0:T(8,128)S(1)}, u32[]{:S(2)}, u32[]{:S(2)}) collective-permute-start(f32[3,2,64,256]{3,2,1,0:T(8,128)S(1)} %get-tuple-element.26), channel_id=1, source_target_pairs={{0,4},{4,8},{8,12},{12,16},{16,20},{20,24},{24,28},{28,0},{1,5},{5... | collective-permute-start | bytes 1179656 | tf_op jit(solution)/shard_map/ppermute | solution.py:416
  259.8 1.7 copy-start.18
  261.5 0.8 copy-start.19
  271.3 5.4 %collective-permute-start.20 = (f32[3,128]{1,0:T(4,128)S(1)}, f32[3,128]{1,0:T(4,128)S(1)}, u32[]{:S(2)}, u32[]{:S(2)}) collective-permute-start(f32[3,128]{1,0:T(4,128)S(1)} %get-tuple-element.37), channel_id=1, source_target_pairs={{0,1},{1,2},{2,3},{3,0},{4,5},{5,6},{6,7},{7,4},{8,9},{9,10},{10,1... | collective-permute-start | bytes 4616 | tf_op jit(solution)/shard_map/ppermute | solution.py:439
  271.8 4.9 %collective-permute-start.21 = (f32[3,128]{1,0:T(4,128)S(1)}, f32[3,128]{1,0:T(4,128)S(1)}, u32[]{:S(2)}, u32[]{:S(2)}) collective-permute-start(f32[3,128]{1,0:T(4,128)S(1)} %get-tuple-element.38), channel_id=1, source_target_pairs={{1,0},{2,1},{3,2},{0,3},{5,4},{6,5},{7,6},{4,7},{9,8},{10,9},{11,1... | collective-permute-start | bytes 4616 | tf_op jit(solution)/shard_map/ppermute | solution.py:440
where the time goes:
time: 279 us; the launch traced here: 277 us
  Pallas kernels  87.3 us (31%)
  waiting for transfers between devices  72.7 us (26%)
  starting transfers between devices  42 us (15%)
  blocking collectives  41.3 us (15%)
  other arithmetic  20.9 us (7%)
  local copies, waits for them, and re-layouts  11.1 us (4%)
    all_to_all x1, blocking collectives, project(): lax.all_to_all(solved, 'gx', split_axis=0, concat_axis=0, tiled=True)  41.3 us
    all_to_all x2, waiting for transfers between devices, project(): lax.all_to_all(spectrum, 'gx', split_axis=0, concat_axis=0, tiled=True)  34.5 us
    pallas_call x2, Pallas kernels, line_backward(): pl.pallas_call(lambda *refs: line_backward_kernel(plan, chunk, yh_step, *...  23.4 us
    ppermute x6, waiting for transfers between devices, incoming(): lax.ppermute(ends, 'gy', [(i, (i + hop) % gy) for i in range(gy)])  21.2 us
    pallas_call x1, Pallas kernels, depth_forward(): pl.pallas_call(lambda *refs: depth_forward_kernel(plan, (refs[0], refs[1]...  19 us
    pallas_call x2, Pallas kernels, line_forward(): pl.pallas_call(lambda *refs: line_forward_kernel(plan, chunk, yh_step, *r...  18.9 us
    pallas_call x2, Pallas kernels, sample(): pl.pallas_call(lambda *refs: sample_kernel(plan, *refs), grid=(3,), in_sp...  16.7 us
    pallas_call x1, Pallas kernels, depth_backward(): pl.pallas_call(lambda *refs: depth_backward_kernel(plan, *refs), grid=(3,...  9.25 us
  transfers between devices with their start and end apart: 25, of which 13 were waited for; matrix products, arithmetic and copies ran while one was open for 8% of the time, Pallas kernels for 15%

commit v1 on v0

--- a/solution.py
+++ b/solution.py
@@ -57,7 +57,7 @@
         self.kk = 2 * self.kh
         self.yb = lanes // slab
         self.y_hi = pencil // self.yb
-        self.y_block = max(min(16, pencil), self.yb)
+        self.y_block = max(min(32, pencil), self.yb)
         self.y_sub = self.y_block // self.yb
         self.groups = lanes // slab
         self.y_part = max(self.y_block, pencil // 2)
@@ -69,11 +69,15 @@
     return jnp.concatenate([high, low, high], axis=axis)
 
 
-def table_three(table, axis):
-    table = jnp.asarray(np.asarray(table, np.float32))
+def table_parts(table):
+    table = np.asarray(table, np.float32)
     high = table.astype(bf16)
-    low = (table - high.astype(f32)).astype(bf16)
-    return jnp.concatenate([high, high, low], axis=axis)
+    low = (table - high.astype(np.float32)).astype(bf16)
+    return high, low
+
+
+def stacked_three(high, low, axis):
+    return jnp.asarray(np.concatenate([high, high, low], axis=axis))
 
 
 def circle(rows, columns, length):
@@ -98,20 +102,31 @@
     cosine, sine = circle(np.arange(n // 2), np.arange(n), n)
     real_rows, imag_rows = cosine, -sine
     imag_rows[0] = 1.0 - 2.0 * (np.arange(n) % 2)
-    back_scale = np.full((n // 2, 1), 2.0 / n)
-    back_scale[0] = 1.0 / n
     order_shape = (plan.gx, plan.chunks, plan.kh)
     forward = np.stack([real_rows.reshape(order_shape + (n,)), imag_rows.reshape(order_shape + (n,))])
-    backward = forward * np.stack([back_scale.reshape(order_shape + (1,))] * 2)
-    forward = forward.transpose(2, 1, 0, 3, 4).reshape(n, n)
-    backward = backward.transpose(2, 1, 0, 3, 4).reshape(n, n)
-    return forward, backward
-
-
-def x_tables(plan):
+    return stacked_three(*table_parts(forward.transpose(2, 1, 0, 3, 4).reshape(n, n)), 1)
+
+
+def z_table_back(plan, ahead):
     n = plan.grid
-    cosine, sine = circle(np.arange(n), np.arange(n), n)
-    return np.concatenate([cosine, sine], axis=1), np.concatenate([cosine, sine], axis=0) / n
+    row = lax.broadcasted_iota(jnp.int32, (n, 1), 0)
+    single = (row == 0) | (row == plan.kh)
+    scale = jnp.where(single, 1.0 / n, 2.0 / n).astype(bf16)
+    high, low = ahead[:, :n] * scale, ahead[:, 2 * n :] * scale
+    return jnp.concatenate([high, high, low], axis=0)
+
+
+def x_table_parts(plan):
+    n = plan.grid
+    return table_parts(np.stack(circle(np.arange(n), np.arange(n), n)))
+
+
+def x_tables(plan, high, low):
+    def stacked(parts, axis):
+        return jnp.concatenate([jnp.concatenate([p[0], p[1]], axis=axis) for p in parts], axis=0)
+
+    scale = jnp.asarray(1.0 / plan.grid, bf16)
+    return stacked((high, high, low), 1), stacked((high, high, low), 0) * scale
 
 
 def half_sine(freq, length):
@@ -208,13 +223,14 @@
 
 
 LAST = ((1,), (1,))
+YH = 4
 
 
 def shifted(component, dim):
     return jnp.where(component == dim, 1, 0)
 
 
-def depth_forward_kernel(plan, refs, outs):
+def depth_forward_kernel(plan, refs, out):
     velocity, noise, own, sides, table, side_rows, spread = refs
     rows8, slab, n = 8, plan.slab, plan.grid
 
@@ -272,13 +288,10 @@
         result = lax.dot_general(
             table[...], split_three(rows, 1), (LAST, ((), ())), preferred_element_type=f32
         )
-        count = plan.gx * plan.kk
-        for chunk, out in enumerate(outs):
-            part = result[chunk * count : (chunk + 1) * count]
-            for sub in range(plan.y_sub):
-                out[:, 0, index * plan.y_sub + sub] = part[
-                    :, sub * lanes : (sub + 1) * lanes
-                ].reshape(plan.gx, plan.kk, lanes)
+        for sub in range(plan.y_sub):
+            out[:, 0, index * plan.y_sub + sub] = result[
+                :, sub * lanes : (sub + 1) * lanes
+            ].reshape(plan.gx, plan.kk, lanes)
         return carry
 
     lax.fori_loop(0, plan.y_part // plan.y_block, block_step, 0)
@@ -293,9 +306,7 @@
     ]
 
 
-def depth_forward(plan, velocity, noise, own, sides):
-    forward, _ = z_tables(plan)
-    table = table_three(forward, 1)
+def depth_forward(plan, chunk, velocity, noise, own, sides, table):
     block = pl.BlockSpec((1, plan.slab, plan.y_part, plan.grid), lambda c, y: (c, 0, y, 0))
     out_shape = jax.ShapeDtypeStruct((plan.gx, 3, plan.y_hi, plan.kk, lanes), f32)
     out_block = pl.BlockSpec(
@@ -306,24 +317,22 @@
         wide = group[-1].shape[-1]
         blocks += weight_blocks(plan, group, wide)
         blocks.append(pl.BlockSpec((1, 1, wide), lambda c, y: (c, 0, 0)))
-    first_out = 13
-    after = first_out + plan.chunks
     return pl.pallas_call(
         lambda *refs: depth_forward_kernel(
             plan,
-            (refs[0], refs[1], refs[2:7], refs[7:12], refs[12]) + refs[after:],
-            refs[first_out:after],
+            (refs[0], refs[1], refs[2:7], refs[7:12], refs[12]) + refs[14:],
+            refs[13],
         ),
         grid=(3, plan.pencil // plan.y_part),
         in_specs=[block, block] + blocks + [pl.BlockSpec(table.shape, lambda c, y: (0, 0))],
-        out_specs=[out_block] * plan.chunks,
-        out_shape=[out_shape] * plan.chunks,
+        out_specs=out_block,
+        out_shape=out_shape,
         scratch_shapes=[
             pltpu.VMEM((2, plan.pencil, 8, plan.grid), f32),
             pltpu.VMEM((plan.y_block * plan.slab, plan.grid), f32),
         ],
         name="depth_forward",
-        cost_estimate=cost(plan, 20, 8),
+        cost_estimate=cost(plan, 20, 20),
     )(velocity, noise, *own, *sides, table)
 
 
@@ -354,9 +363,7 @@
     lax.fori_loop(0, plan.y_part // plan.y_block, block_step, 0)
 
 
-def depth_backward(plan, parts):
-    _, backward = z_tables(plan)
-    table = table_three(backward, 0)
+def depth_backward(plan, parts, table):
     in_block = pl.BlockSpec(
         (plan.gx, 1, plan.y_part // plan.yb, plan.kk, lanes), lambda c, y: (0, c, y, 0, 0)
     )
@@ -373,22 +380,72 @@
     )(*parts, table)
 
 
+def depth_edges_kernel(plan, *refs):
+    parts, table, head, tail = refs[: plan.chunks], refs[plan.chunks], refs[-2], refs[-1]
+    slab, n = plan.slab, plan.grid
+
+    def block_step(index, carry):
+        columns = []
+        for sub in range(plan.y_sub):
+            columns.append(
+                jnp.concatenate(
+                    [
+                        part[:, 0, index * plan.y_sub + sub].reshape(plan.gx * plan.kk, lanes)
+                        for part in parts
+                    ],
+                    axis=0,
+                )
+            )
+        spectrum = jnp.concatenate(columns, axis=1) if len(columns) > 1 else columns[0]
+        rows = spectrum.T.reshape(plan.y_block, slab, n)
+        rows = jnp.concatenate([rows[:, :8], rows[:, slab - 8 :]], axis=1)
+        result = jnp.dot(
+            split_three(rows.reshape(plan.y_block * 16, n), 1),
+            table[...],
+            preferred_element_type=f32,
+        )
+        result = jnp.swapaxes(result.reshape(plan.y_block, 16, n), 0, 1)
+        ys = pl.ds(pl.multiple_of(index * plan.y_block, plan.y_block), plan.y_block)
+        head[0, :, ys, :] = result[:2]
+        tail[0, :, ys, :] = result[14:]
+        return carry
+
+    lax.fori_loop(0, plan.y_part // plan.y_block, block_step, 0)
+
+
+def depth_edges(plan, parts, table):
+    in_block = pl.BlockSpec(
+        (plan.gx, 1, plan.y_part // plan.yb, plan.kk, lanes), lambda c, y: (0, c, y, 0, 0)
+    )
+    layers = pl.BlockSpec((1, 2, plan.y_part, plan.grid), lambda c, y: (c, 0, y, 0))
+    return pl.pallas_call(
+        lambda *refs: depth_edges_kernel(plan, *refs),
+        grid=(3, plan.pencil // plan.y_part),
+        in_specs=[in_block] * plan.chunks + [pl.BlockSpec(table.shape, lambda c, y: (0, 0))],
+        out_specs=[layers, layers],
+        out_shape=[jax.ShapeDtypeStruct((3, 2, plan.pencil, plan.grid), f32)] * 2,
+        name="depth_edges",
+        cost_estimate=cost(plan, 8, 6),
+    )(*parts, table)
+
+
 def sample_kernel(plan, field, below, above, wx, wy, wz_high, wz_low, out):
     slab, pencil, n = plan.slab, plan.pencil, plan.grid
-    x_step = min(16, slab)
+    x_step = min(32, slab)
 
     for group in range(3):
         lanes_of = slice(group * lanes, (group + 1) * lanes)
         high, low = wz_high[0, :, lanes_of], wz_low[0, :, lanes_of]
-        weight = jnp.concatenate([high, high, low], axis=0)
+        both = jnp.concatenate([high, low], axis=1)
 
         def gathered(rows, along, across):
             count_x, count_y = rows.shape[0], rows.shape[1]
-            line = jnp.dot(
-                split_three(rows.reshape(count_x * count_y, n), 1),
-                weight,
-                preferred_element_type=f32,
-            )
+            flat = rows.reshape(count_x * count_y, n)
+            top = flat.astype(bf16)
+            rest = (flat - top.astype(f32)).astype(bf16)
+            line = jnp.dot(top, both, preferred_element_type=f32)
+            line = line[:, :lanes] + line[:, lanes:]
+            line = line + jnp.dot(rest, high, preferred_element_type=f32)
             line = jnp.sum(line.reshape(count_x, count_y, lanes) * along, axis=1)
             return jnp.sum(line * across, axis=0, keepdims=True)
 
@@ -411,10 +468,10 @@
         out[0, :, lanes_of] = total
 
 
-def sample(plan, field, column):
+def sample(plan, field, head, tail, column):
     gx = plan.gx
-    below = lax.ppermute(field[:, -2:], "gx", [(i, (i + 1) % gx) for i in range(gx)])
-    above = lax.ppermute(field[:, :2], "gx", [((i + 1) % gx, i) for i in range(gx)])
+    below = lax.ppermute(tail, "gx", [(i, (i + 1) % gx) for i in range(gx)])
+    above = lax.ppermute(head, "gx", [((i + 1) % gx, i) for i in range(gx)])
     layers = pl.BlockSpec((1, 2, plan.pencil, plan.grid), lambda c: (c, 0, 0, 0))
     wide = 3 * lanes
     found = pl.pallas_call(
@@ -559,11 +616,9 @@
             ends[8 + row] = ends[8 + row] + powers[2 + part] * spill
 
 
-def line_forward(plan, chunk, spectrum, coef):
+def line_forward(plan, chunk, spectrum, coef, table):
     n, kh = plan.grid, plan.kh
-    forward, _ = x_tables(plan)
-    table = table_three(forward, 0)
-    yh_step = 2 if plan.y_hi % 2 == 0 else 1
+    yh_step = math.gcd(plan.y_hi, YH)
     ys = yh_step * plan.yb
     return pl.pallas_call(
         lambda *refs: line_forward_kernel(plan, chunk, yh_step, *refs),
@@ -753,11 +808,9 @@
     return real, imag
 
 
-def line_backward(plan, chunk, field, coef, entering):
+def line_backward(plan, chunk, field, coef, entering, table):
     n, kh, length = plan.grid, plan.kh, plan.pencil
-    _, backward = x_tables(plan)
-    table = table_three(backward, 0)
-    yh_step = 2 if plan.y_hi % 2 == 0 else 1
+    yh_step = math.gcd(plan.y_hi, YH)
     whole = pl.BlockSpec(memory_space=pltpu.VMEM)
     return pl.pallas_call(
         lambda *refs: line_backward_kernel(plan, chunk, yh_step, *refs),
@@ -775,14 +828,15 @@
     )(field, coef, entering, table)
 
 
-def project(plan, spectra):
+def project(plan, spectra, tables):
+    ahead, backward = tables
     back = []
     for chunk, spectrum in enumerate(spectra):
         coef, weights = coefficients(plan, chunk)
         received = lax.all_to_all(spectrum, "gx", split_axis=0, concat_axis=0, tiled=True)
-        field, ends = line_forward(plan, chunk, received, coef)
+        field, ends = line_forward(plan, chunk, received, coef, ahead)
         entering = incoming(plan, ends, weights)
-        solved = line_backward(plan, chunk, field, coef, entering)
+        solved = line_backward(plan, chunk, field, coef, entering, backward)
         back.append(lax.all_to_all(solved, "gx", split_axis=0, concat_axis=0, tiled=True))
     return back
 
@@ -800,23 +854,39 @@
     live = (jnp.arange(block_rows, dtype=jnp.int32) < counts[0]).astype(f32)
     column_places = padded(places, (("gy", 1),), block_rows)
     column = weights_of(plan, column_places)
-    found = sample(plan, velocity, column)
-    before, after = beside(plan, column_places)
-    side_places, found = lax.optimization_barrier((jnp.concatenate([before, after], axis=1), found))
-    side_weights = weights_of(plan, side_places)
+    found = sample(plan, velocity, velocity[:, :2], velocity[:, -2:], column)
+    found, late_places = lax.optimization_barrier((found, column_places))
+    before, after = beside(plan, late_places)
     sampled = brought_home(plan, found)
     colloid_force = live * (drag_rate * (colloid_velocity - sampled) + particle_noise)
+    side_places, colloid_force = lax.optimization_barrier(
+        (jnp.concatenate([before, after], axis=1), colloid_force)
+    )
+    side_weights = weights_of(plan, side_places)
     column_force = padded(colloid_force, (("gy", 1),), block_rows)
     side_force = jnp.concatenate(beside(plan, column_force), axis=1)
-    spectra = depth_forward(
-        plan,
-        velocity,
-        fluid_noise,
-        column + (column_force[:, None, :],),
-        side_weights + (side_force[:, None, :],),
-    )
-    new_velocity = depth_backward(plan, project(plan, spectra))
-    colloid_drift = live * brought_home(plan, sample(plan, new_velocity, column))
+    z_ahead = z_tables(plan)
+    rows = plan.gx * plan.kk
+    spectra = [
+        depth_forward(
+            plan,
+            chunk,
+            velocity,
+            fluid_noise,
+            column + (column_force[:, None, :],),
+            side_weights + (side_force[:, None, :],),
+            z_ahead[chunk * rows : (chunk + 1) * rows],
+        )
+        for chunk in range(plan.chunks)
+    ]
+    late, spectra[0] = lax.optimization_barrier(
+        ((z_ahead,) + tuple(jnp.asarray(part) for part in x_table_parts(plan)), spectra[0])
+    )
+    z_back = z_table_back(plan, late[0])
+    back = project(plan, spectra, x_tables(plan, late[1], late[2]))
+    head, tail = depth_edges(plan, back, z_back)
+    new_velocity = depth_backward(plan, back, z_back)
+    colloid_drift = live * brought_home(plan, sample(plan, new_velocity, head, tail, column))
     return (new_velocity, colloid_force, colloid_drift)
 
 

time: 279 us -> 275 us (0.986)
  blocking collectives: 41.3 us -> 0 us
  Pallas kernels: 87.3 us -> 100 us
  waiting for transfers between devices: 72.7 us -> 84.6 us
  starting transfers between devices: 42 us -> 51.9 us
    all_to_all x1 -> x0, blocking collectives: 41.3 us -> none  [project(): lax.all_to_all(solved, 'gx', split_axis=0, concat_axis=0, tiled=True)]
    all_to_all x1 -> x2, waiting for transfers between devices: 0.22 us -> 41.1 us  [project(): lax.all_to_all(solved, 'gx', split_axis=0, concat_axis=0, tiled=True)]
    pallas_call x1 -> x2, Pallas kernels: 19 us -> 34.4 us  [depth_forward(): pl.pallas_call(lambda *refs: depth_forward_kernel(plan, (refs[0], refs[1]...]
    all_to_all x2, waiting for transfers between devices: 34.5 us -> 20.3 us  [project(): lax.all_to_all(spectrum, 'gx', split_axis=0, concat_axis=0, tiled=True)]
    ppermute x4, waiting for transfers between devices: 10.4 us -> 1.58 us  [the longest x2 1.57 us: sample(): below = lax.ppermute(tail, 'gx', [(i, (i + 1) % gx) for i in range(gx)])]
    pallas_call x0 -> x1, Pallas kernels: none -> 6.88 us  [depth_edges(): pl.pallas_call(lambda *refs: depth_edges_kernel(plan, *refs), grid=(3, pl...]
    pallas_call x2, Pallas kernels: 16.7 us -> 12.5 us  [sample(): pl.pallas_call(lambda *refs: sample_kernel(plan, *refs), grid=(3,), in_sp...]
    all_to_all x1 -> x2, starting transfers between devices: 4.46 us -> 8.34 us  [project(): lax.all_to_all(solved, 'gx', split_axis=0, concat_axis=0, tiled=True)]
  transfers between devices with their start and end apart: 25 -> 26, of which waited for: 13 -> 11; matrix products, arithmetic and copies ran while one was open for 8% -> 9% of each run, Pallas kernels for 15% -> 23%
where the time goes in v1:
time: 275 us; the launch traced here: 273 us
  Pallas kernels  100 us (36%)
  waiting for transfers between devices  84.6 us (31%)
  starting transfers between devices  51.9 us (19%)
  other arithmetic  23 us (8%)
  local copies, waits for them, and re-layouts  11.5 us (4%)
    all_to_all x2, waiting for transfers between devices, project(): lax.all_to_all(solved, 'gx', split_axis=0, concat_axis=0, tiled=True)  41.1 us
    pallas_call x2, Pallas kernels, depth_forward(): pl.pallas_call(lambda *refs: depth_forward_kernel(plan, (refs[0], refs[1]...  34.4 us
    pallas_call x2, Pallas kernels, line_backward(): pl.pallas_call(lambda *refs: line_backward_kernel(plan, chunk, yh_step, *...  23.1 us
    all_to_all x2, waiting for transfers between devices, project(): lax.all_to_all(spectrum, 'gx', split_axis=0, concat_axis=0, tiled=True)  20.3 us
    ppermute x6, waiting for transfers between devices, incoming(): lax.ppermute(ends, 'gy', [(i, (i + hop) % gy) for i in range(gy)])  18.7 us
    pallas_call x2, Pallas kernels, line_forward(): pl.pallas_call(lambda *refs: line_forward_kernel(plan, chunk, yh_step, *r...  15.2 us
    pallas_call x2, Pallas kernels, sample(): pl.pallas_call(lambda *refs: sample_kernel(plan, *refs), grid=(3,), in_sp...  12.5 us
    all_to_all x2, starting transfers between devices, project(): lax.all_to_all(spectrum, 'gx', split_axis=0, concat_axis=0, tiled=True)  8.63 us
  transfers between devices with their start and end apart: 26, of which 11 were waited for; matrix products, arithmetic and copies ran while one was open for 9% of the time, Pallas kernels for 23%

profile of v1, /device:TPU:0, one launch (start us, length us, event | category | flops | bytes accessed | tf_op | source)
XLA Modules:
  0.0 273.4 jit_solution(15768086569523606708)
XLA Ops:
  1.3 3.1 %collective-permute-start = (f32[3,128]{1,0:T(4,128)S(1)}, f32[3,128]{1,0:T(4,128)S(1)}, u32[]{:S(2)}, u32[]{:S(2)}) collective-permute-start(f32[3,128]{1,0:T(4,128)S(1)} %convert_add_fusion), channel_id=1, source_target_pairs={{0,1},{1,2},{2,3},{3,0},{4,5},{5,6},{6,7},{7,4},{8,9},{9,10},{10,1... | collective-permute-start | bytes 4616 | tf_op jit(solution)/shard_map/ppermute | solution.py:23
  4.4 2.0 collective-permute-start.1
  6.4 1.2 fusion.239
  7.7 2.6 collective-permute-start.3
  17.9 1.4 fusion.34
  19.3 1.0 fusion.1
  21.3 6.2 %sample.2 = f32[3,1,384]{2,1,0:T(1,128)} custom-call(f32[3,32,64,256]{3,2,1,0:T(8,128)} %refs_0_.5, f32[3,2,64,256]{3,2,1,0:T(8,128)} %copy-done.24, f32[3,2,64,256]{3,2,1,0:T(8,128)} %copy-done.25, f32[2,40,384]{2,1,0:T(8,128)} %pad_maximum_fusion.8.refs_3_.refs_2_, f32[2,64,384]{2,1,0:T(8,128)} %pad_maximum_fusion.5.refs_4_.refs_3_, ...), custom_call_target="tpu_custom_call" | custom-call | flops 6000000000 | bytes 8000000 | tf_op jit(solution)/shard_map/sample/pallas_call | solution.py:477
  28.2 3.8 %collective-permute-start.7 = (f32[3,128]{1,0:T(4,128)S(1)}, f32[3,128]{1,0:T(4,128)S(1)}, u32[]{:S(2)}, u32[]{:S(2)}) collective-permute-start(f32[3,128]{1,0:T(4,128)S(1)} %get-tuple-element.56), channel_id=1, source_target_pairs={{1,0},{2,1},{3,2},{0,3},{5,4},{6,5},{7,6},{4,7},{9,8},{10,9},{11,1... | collective-permute-start | bytes 4616 | tf_op jit(solution)/shard_map/ppermute | solution.py:497
  32.0 2.6 collective-permute-start.5
  34.7 1.3 collective-permute-done.4
  36.1 3.8 %collective-permute-start.9 = (f32[3,128]{1,0:T(4,128)S(1)}, f32[3,128]{1,0:T(4,128)S(1)}, u32[]{:S(2)}, u32[]{:S(2)}) collective-permute-start(f32[3,128]{1,0:T(4,128)S(1)} %add_multiply_fusion.6), channel_id=1, source_target_pairs={{1,0},{2,1},{3,2},{0,3},{5,4},{6,5},{7,6},{4,7},{9,8},{10,9},{11,1... | collective-permute-start | bytes 4616 | tf_op jit(solution)/shard_map/ppermute | solution.py:25
  39.9 2.8 %fusion.6 = (f32[1,256,768]{2,1,0:T(8,128)S(1)}, f32[1,256,768]{2,1,0:T(8,128)S(1)}) fusion(f32[256]{0:T(256)S(1)} %iota_convert_fusion, f32[768]{0:T(1024)S(1)} %get-tuple-element.31, f32[256]{0:T(256)S(1)} %fusion.236), kind=kLoop, calls=%fused_computation.19 | loop fusion | flops 12189696 | bytes 1577984 | tf_op jit(solution)/shard_map/jit(_where)/select_n | solution.py:42
  44.0 1.4 fusion
  46.3 2.6 collective-permute-start.11
  50.9 17.2 %depth_forward.3 = f32[8,3,16,16,128]{4,3,2,1,0:T(8,128)} custom-call(f32[3,32,64,256]{3,2,1,0:T(8,128)} %refs_0_.5, f32[3,32,64,256]{3,2,1,0:T(8,128)} %refs_1_.3, f32[2,40,384]{2,1,0:T(8,128)} %pad_maximum_fusion.8.refs_3_.refs_2_, f32[2,64,384]{2,1,0:T(8,128)} %pad_maximum_fusion.5.refs_4_.refs_3_, ...), custom_call_target="tpu_custom_call" | custom-call | flops 20000000000 | bytes 20000000 | tf_op jit(solution)/shard_map/depth_forward/pallas_call | solution.py:320
  68.1 4.2 %all-to-all-start.2 = ((f32[8,3,16,16,128]{4,3,2,1,0:T(8,128)}), f32[8,3,16,16,128]{4,3,2,1,0:T(8,128)S(1)}, u32[]{:S(2)}, u32[]{:S(2)}) async-start(f32[8,3,16,16,128]{4,3,2,1,0:T(8,128)} %depth_forward.3), calls=%async_computation.2 | async-start | bytes 6291456 | tf_op jit(solution)/shard_map/all_to_all | solution.py:836
  72.2 17.2 %depth_forward.2 = f32[8,3,16,16,128]{4,3,2,1,0:T(8,128)} custom-call(f32[3,32,64,256]{3,2,1,0:T(8,128)} %refs_0_.5, f32[3,32,64,256]{3,2,1,0:T(8,128)} %refs_1_.3, f32[2,40,384]{2,1,0:T(8,128)} %pad_maximum_fusion.8.refs_3_.refs_2_, f32[2,64,384]{2,1,0:T(8,128)} %pad_maximum_fusion.5.refs_4_.refs_3_, ...), custom_call_target="tpu_custom_call" | custom-call | flops 20000000000 | bytes 20000000 | tf_op jit(solution)/shard_map/depth_forward/pallas_call | solution.py:320
  89.5 1.9 slice_multiply_fusion.1
  91.4 0.9 copy-done.7
  92.3 0.9 slice_bitcast_fusion.1
  93.2 16.9 %all-to-all-done.2.refs_0_ = f32[8,3,16,16,128]{4,3,2,1,0:T(8,128)S(1)} async-done(((f32[8,3,16,16,128]{4,3,2,1,0:T(8,128)}), f32[8,3,16,16,128]{4,3,2,1,0:T(8,128)S(1)}, u32[]{:S(2)}, u32[]{:S(2)}) %all-to-all-start.2) | async-done | bytes 3145760 | tf_op jit(solution)/shard_map/all_to_all | solution.py:836
  110.1 1.7 copy-done.4
  111.8 4.5 %all-to-all-start = ((f32[8,3,16,16,128]{4,3,2,1,0:T(8,128)}), f32[8,3,16,16,128]{4,3,2,1,0:T(8,128)}, u32[]{:S(2)}, u32[]{:S(2)}) async-start(f32[8,3,16,16,128]{4,3,2,1,0:T(8,128)} %depth_forward.2), calls=%async_computation | async-start | bytes 6291456 | tf_op jit(solution)/shard_map/all_to_all | solution.py:836
  116.2 2.0 maximum_maximum_fusion.refs_2_
  118.3 7.5 %line_forward.3 = (f32[3,64,2,8,256]{4,3,2,1,0:T(8,128)}, f32[16,8,256]{2,1,0:T(8,128)}) custom-call(f32[8,3,16,16,128]{4,3,2,1,0:T(8,128)} %copy-done.4, f32[18,8,256]{2,1,0:T(8,128)} %copy-done, bf16[768,512]{1,0:T(8,128)(2,1)} %maximum_maximum_fusion.refs_2_), custom_call_target="tpu_custom_call" | custom-call | flops 8000000000 | bytes 10000000 | tf_op jit(solution)/shard_map/line_forward/pallas_call | solution.py:623
  126.4 3.3 %collective-permute-start.17 = (f32[16,8,256]{2,1,0:T(8,128)}, f32[16,8,256]{2,1,0:T(8,128)S(1)}, u32[]{:S(2)}, u32[]{:S(2)}) collective-permute-start(f32[16,8,256]{2,1,0:T(8,128)} %get-tuple-element.27), channel_id=1, source_target_pairs={{0,3},{1,0},{2,1},{3,2},{4,7},{5,4},{6,5},{7,6},{8,11},{9,8},{10,9... | collective-permute-start | bytes 393224 | tf_op jit(solution)/shard_map/ppermute | solution.py:186
  129.8 4.6 %collective-permute-done.15 = f32[16,8,256]{2,1,0:T(8,128)S(1)} collective-permute-done((f32[16,8,256]{2,1,0:T(8,128)}, f32[16,8,256]{2,1,0:T(8,128)S(1)}, u32[]{:S(2)}, u32[]{:S(2)}) %collective-permute-start.15) | collective-permute-done | bytes 131104 | tf_op jit(solution)/shard_map/ppermute | solution.py:186
  134.4 4.7 %collective-permute-done.16 = f32[16,8,256]{2,1,0:T(8,128)S(1)} collective-permute-done((f32[16,8,256]{2,1,0:T(8,128)}, f32[16,8,256]{2,1,0:T(8,128)S(1)}, u32[]{:S(2)}, u32[]{:S(2)}) %collective-permute-start.16) | collective-permute-done | bytes 131104 | tf_op jit(solution)/shard_map/ppermute | solution.py:186
  139.2 11.5 %line_backward.3 = f32[8,3,16,16,128]{4,3,2,1,0:T(8,128)} custom-call(f32[3,64,2,8,256]{4,3,2,1,0:T(8,128)} %get-tuple-element.26.refs_0_, f32[18,8,256]{2,1,0:T(8,128)S(1)} %copy-done.1, f32[16,8,256]{2,1,0:T(8,128)S(1)} %pad_maximum_fusion.7.refs_2_, bf16[1536,256]{1,0:T(8,128)(2,1)S(1)} %broadcast_multiply_fusion.refs_3_), custom_call_target="tpu_custom_call" | custom-call | flops 12000000000 | bytes 12000000 | tf_op jit(solution)/shard_map/line_backward/pallas_call | solution.py:815
  150.7 3.4 %all-to-all-done.refs_0_ = f32[8,3,16,16,128]{4,3,2,1,0:T(8,128)} async-done(((f32[8,3,16,16,128]{4,3,2,1,0:T(8,128)}), f32[8,3,16,16,128]{4,3,2,1,0:T(8,128)}, u32[]{:S(2)}, u32[]{:S(2)}) %all-to-all-start) | async-done | bytes 3145760 | tf_op jit(solution)/shard_map/all_to_all | solution.py:836
  154.1 4.5 %all-to-all-start.3 = ((f32[8,3,16,16,128]{4,3,2,1,0:T(8,128)}), f32[8,3,16,16,128]{4,3,2,1,0:T(8,128)}, u32[]{:S(2)}, u32[]{:S(2)}) async-start(f32[8,3,16,16,128]{4,3,2,1,0:T(8,128)} %line_backward.3), calls=%async_computation.3 | async-start | bytes 6291456 | tf_op jit(solution)/shard_map/all_to_all | solution.py:840
  158.6 7.7 %line_forward.2 = (f32[3,64,2,8,256]{4,3,2,1,0:T(8,128)}, f32[16,8,256]{2,1,0:T(8,128)}) custom-call(f32[8,3,16,16,128]{4,3,2,1,0:T(8,128)} %all-to-all-done.refs_0_, f32[18,8,256]{2,1,0:T(8,128)} %copy-done.2, bf16[768,512]{1,0:T(8,128)(2,1)} %maximum_maximum_fusion.refs_2_), custom_call_target="tpu_custom_call" | custom-call | flops 8000000000 | bytes 10000000 | tf_op jit(solution)/shard_map/line_forward/pallas_call | solution.py:623
  166.9 3.3 %collective-permute-start.14 = (f32[16,8,256]{2,1,0:T(8,128)}, f32[16,8,256]{2,1,0:T(8,128)S(1)}, u32[]{:S(2)}, u32[]{:S(2)}) collective-permute-start(f32[16,8,256]{2,1,0:T(8,128)} %get-tuple-element.25), channel_id=1, source_target_pairs={{0,3},{1,0},{2,1},{3,2},{4,7},{5,4},{6,5},{7,6},{8,11},{9,8},{10,9... | collective-permute-start | bytes 393224 | tf_op jit(solution)/shard_map/ppermute | solution.py:186
  170.1 4.7 %collective-permute-done.12 = f32[16,8,256]{2,1,0:T(8,128)S(1)} collective-permute-done((f32[16,8,256]{2,1,0:T(8,128)}, f32[16,8,256]{2,1,0:T(8,128)S(1)}, u32[]{:S(2)}, u32[]{:S(2)}) %collective-permute-start.12) | collective-permute-done | bytes 131104 | tf_op jit(solution)/shard_map/ppermute | solution.py:186
  174.8 4.7 %collective-permute-done.13 = f32[16,8,256]{2,1,0:T(8,128)S(1)} collective-permute-done((f32[16,8,256]{2,1,0:T(8,128)}, f32[16,8,256]{2,1,0:T(8,128)S(1)}, u32[]{:S(2)}, u32[]{:S(2)}) %collective-permute-start.13) | collective-permute-done | bytes 131104 | tf_op jit(solution)/shard_map/ppermute | solution.py:186
  179.5 0.9 fusion.155
  180.5 11.6 %line_backward.2 = f32[8,3,16,16,128]{4,3,2,1,0:T(8,128)} custom-call(f32[3,64,2,8,256]{4,3,2,1,0:T(8,128)} %get-tuple-element.24.refs_0_, f32[18,8,256]{2,1,0:T(8,128)S(1)} %copy-done.3, f32[16,8,256]{2,1,0:T(8,128)S(1)} %pad_maximum_fusion.6.refs_2_, bf16[1536,256]{1,0:T(8,128)(2,1)S(1)} %broadcast_multiply_fusion.refs_3_), custom_call_target="tpu_custom_call" | custom-call | flops 12000000000 | bytes 12000000 | tf_op jit(solution)/shard_map/line_backward/pallas_call | solution.py:815
  192.1 4.3 %all-to-all-done.3.refs_1_ = f32[8,3,16,16,128]{4,3,2,1,0:T(8,128)} async-done(((f32[8,3,16,16,128]{4,3,2,1,0:T(8,128)}), f32[8,3,16,16,128]{4,3,2,1,0:T(8,128)}, u32[]{:S(2)}, u32[]{:S(2)}) %all-to-all-start.3) | async-done | bytes 3145760 | tf_op jit(solution)/shard_map/all_to_all | solution.py:840
  196.4 3.9 %all-to-all-start.1 = ((f32[8,3,16,16,128]{4,3,2,1,0:T(8,128)}), f32[8,3,16,16,128]{4,3,2,1,0:T(8,128)S(1)}, u32[]{:S(2)}, u32[]{:S(2)}) async-start(f32[8,3,16,16,128]{4,3,2,1,0:T(8,128)} %line_backward.2), calls=%async_computation.1 | async-start | bytes 6291456 | tf_op jit(solution)/shard_map/all_to_all | solution.py:840
  201.1 36.8 %all-to-all-done.1.refs_0_ = f32[8,3,16,16,128]{4,3,2,1,0:T(8,128)S(1)} async-done(((f32[8,3,16,16,128]{4,3,2,1,0:T(8,128)}), f32[8,3,16,16,128]{4,3,2,1,0:T(8,128)S(1)}, u32[]{:S(2)}, u32[]{:S(2)}) %all-to-all-start.1) | async-done | bytes 3145760 | tf_op jit(solution)/shard_map/all_to_all | solution.py:840
  237.9 1.7 copy-done.5
  239.5 6.9 %depth_edges.1 = (f32[3,2,64,256]{3,2,1,0:T(8,128)}, f32[3,2,64,256]{3,2,1,0:T(8,128)}) custom-call(f32[8,3,16,16,128]{4,3,2,1,0:T(8,128)} %copy-done.5, f32[8,3,16,16,128]{4,3,2,1,0:T(8,128)} %all-to-all-done.3.refs_1_, bf16[768,256]{1,0:T(8,128)(2,1)} %pad_maximum_fusion.3.refs_2_), custom_call_target="tpu_custom_call" | custom-call | flops 8000000000 | bytes 6000000 | tf_op jit(solution)/shard_map/depth_edges/pallas_call | solution.py:421
  246.4 2.6 collective-permute-start.19
  249.1 8.3 %depth_backward.1.refs_0_ = f32[3,32,64,256]{3,2,1,0:T(8,128)} custom-call(f32[8,3,16,16,128]{4,3,2,1,0:T(8,128)} %copy-done.5, f32[8,3,16,16,128]{4,3,2,1,0:T(8,128)} %all-to-all-done.3.refs_1_, bf16[768,256]{1,0:T(8,128)(2,1)} %pad_maximum_fusion.3.refs_2_), custom_call_target="tpu_custom_call" | custom-call | flops 16000000000 | bytes 6000000 | tf_op jit(solution)/shard_map/depth_backward/pallas_call | solution.py:370
  257.4 1.6 collective-permute-done.18.refs_1_
  260.4 6.3 %sample.3 = f32[3,1,384]{2,1,0:T(1,128)} custom-call(f32[3,32,64,256]{3,2,1,0:T(8,128)} %depth_backward.1.refs_0_, f32[3,2,64,256]{3,2,1,0:T(8,128)} %copy-done.26, f32[3,2,64,256]{3,2,1,0:T(8,128)} %copy-done.27, f32[2,40,384]{2,1,0:T(8,128)} %pad_maximum_fusion.8.refs_3_.refs_2_, f32[2,64,384]{2,1,0:T(8,128)} %pad_maximum_fusion.5.refs_4_.refs_3_, ...), custom_call_target="tpu_custom_call" | custom-call | flops 6000000000 | bytes 8000000 | tf_op jit(solution)/shard_map/sample/pallas_call | solution.py:477
  267.4 3.8 %collective-permute-start.21 = (f32[3,128]{1,0:T(4,128)S(1)}, f32[3,128]{1,0:T(4,128)S(1)}, u32[]{:S(2)}, u32[]{:S(2)}) collective-permute-start(f32[3,128]{1,0:T(4,128)S(1)} %get-tuple-element.54), channel_id=1, source_target_pairs={{1,0},{2,1},{3,2},{0,3},{5,4},{6,5},{7,6},{4,7},{9,8},{10,9},{11,1... | collective-permute-start | bytes 4616 | tf_op jit(solution)/shard_map/ppermute | solution.py:497
  271.2 1.6 collective-permute-done.20
  (161 shorter events, 18.2 us)
Async XLA Ops:
  1.3 14.4 %collective-permute-start = (f32[3,128]{1,0:T(4,128)S(1)}, f32[3,128]{1,0:T(4,128)S(1)}, u32[]{:S(2)}, u32[]{:S(2)}) collective-permute-start(f32[3,128]{1,0:T(4,128)S(1)} %convert_add_fusion), channel_id=1, source_target_pairs={{0,1},{1,2},{2,3},{3,0},{4,5},{5,6},{6,7},{7,4},{8,9},{9,10},{10,1... | collective-permute-start | bytes 4616 | tf_op jit(solution)/shard_map/ppermute | solution.py:23
  4.4 11.4 %collective-permute-start.1 = (f32[3,128]{1,0:T(4,128)S(1)}, f32[3,128]{1,0:T(4,128)S(1)}, u32[]{:S(2)}, u32[]{:S(2)}) collective-permute-start(f32[3,128]{1,0:T(4,128)S(1)} %convert_add_fusion), channel_id=1, source_target_pairs={{1,0},{2,1},{3,2},{0,3},{5,4},{6,5},{7,6},{4,7},{9,8},{10,9},{11,1... | collective-permute-start | bytes 4616 | tf_op jit(solution)/shard_map/ppermute | solution.py:25
  7.6 12.8 %collective-permute-start.2 = (f32[3,2,64,256]{3,2,1,0:T(8,128)S(1)}, f32[3,2,64,256]{3,2,1,0:T(8,128)S(1)}, u32[]{:S(2)}, u32[]{:S(2)}) collective-permute-start(f32[3,2,64,256]{3,2,1,0:T(8,128)S(1)} %get-tuple-element.38), channel_id=1, source_target_pairs={{0,4},{4,8},{8,12},{12,16},{16,20},{20,24},{24,28},{28,0},{1,5},{5... | collective-permute-start | bytes 1179656 | tf_op jit(solution)/shard_map/ppermute | solution.py:473
  7.7 12.7 %collective-permute-start.3 = (f32[3,2,64,256]{3,2,1,0:T(8,128)S(1)}, f32[3,2,64,256]{3,2,1,0:T(8,128)S(1)}, u32[]{:S(2)}, u32[]{:S(2)}) collective-permute-start(f32[3,2,64,256]{3,2,1,0:T(8,128)S(1)} %get-tuple-element.37), channel_id=1, source_target_pairs={{4,0},{8,4},{12,8},{16,12},{20,16},{24,20},{28,24},{0,28},{5,1},{9... | collective-permute-start | bytes 1179656 | tf_op jit(solution)/shard_map/ppermute | solution.py:474
  13.0 7.4 %copy-start.19 = (f32[8,8,256]{2,1,0:T(8,128)}, f32[8,8,256]{2,1,0:T(8,128)S(1)}, u32[]{:S(2)}) copy-start(f32[8,8,256]{2,1,0:T(8,128)S(1)} %get-tuple-element.72) | copy-start | bytes 196612
  14.1 6.3 %copy-start.17 = (f32[8,8,256]{2,1,0:T(8,128)}, f32[8,8,256]{2,1,0:T(8,128)S(1)}, u32[]{:S(2)}) copy-start(f32[8,8,256]{2,1,0:T(8,128)S(1)} %get-tuple-element.101) | copy-start | bytes 196612
  14.3 6.1 %copy-start.15 = (f32[8,8,256]{2,1,0:T(8,128)}, f32[8,8,256]{2,1,0:T(8,128)S(1)}, u32[]{:S(2)}) copy-start(f32[8,8,256]{2,1,0:T(8,128)S(1)} %get-tuple-element.79) | copy-start | bytes 196612
  15.0 5.3 %copy-start = (f32[18,8,256]{2,1,0:T(8,128)}, f32[18,8,256]{2,1,0:T(8,128)S(1)}, u32[]{:S(2)}) copy-start(f32[18,8,256]{2,1,0:T(8,128)S(1)} %get-tuple-element.128.refs_1_) | copy-start | bytes 442372
  15.0 5.3 %copy-start.2 = (f32[18,8,256]{2,1,0:T(8,128)}, f32[18,8,256]{2,1,0:T(8,128)S(1)}, u32[]{:S(2)}) copy-start(f32[18,8,256]{2,1,0:T(8,128)S(1)} %get-tuple-element.129.refs_1_) | copy-start | bytes 442372
  21.3 13.4 %copy-start.22 = (f32[3,128]{1,0:T(4,128)S(1)}, f32[3,128]{1,0:T(4,128)}, u32[]{:S(2)}) copy-start(f32[3,128]{1,0:T(4,128)} %param.15) | copy-start | bytes 4612
  21.3 13.4 %copy-start.23 = (f32[3,128]{1,0:T(4,128)S(1)}, f32[3,128]{1,0:T(4,128)}, u32[]{:S(2)}) copy-start(f32[3,128]{1,0:T(4,128)} %param.14) | copy-start | bytes 4612
  28.2 6.5 %collective-permute-start.6 = (f32[3,128]{1,0:T(4,128)S(1)}, f32[3,128]{1,0:T(4,128)S(1)}, u32[]{:S(2)}, u32[]{:S(2)}) collective-permute-start(f32[3,128]{1,0:T(4,128)S(1)} %get-tuple-element.55), channel_id=1, source_target_pairs={{0,1},{1,2},{2,3},{3,0},{4,5},{5,6},{6,7},{7,4},{8,9},{9,10},{10,1... | collective-permute-start | bytes 4616 | tf_op jit(solution)/shard_map/ppermute | solution.py:496
  28.2 6.5 %collective-permute-start.7 = (f32[3,128]{1,0:T(4,128)S(1)}, f32[3,128]{1,0:T(4,128)S(1)}, u32[]{:S(2)}, u32[]{:S(2)}) collective-permute-start(f32[3,128]{1,0:T(4,128)S(1)} %get-tuple-element.56), channel_id=1, source_target_pairs={{1,0},{2,1},{3,2},{0,3},{5,4},{6,5},{7,6},{4,7},{9,8},{10,9},{11,1... | collective-permute-start | bytes 4616 | tf_op jit(solution)/shard_map/ppermute | solution.py:497
  32.0 4.0 %collective-permute-start.4 = (f32[3,384]{1,0:T(4,128)S(1)}, f32[3,384]{1,0:T(4,128)S(1)}, u32[]{:S(2)}, u32[]{:S(2)}) collective-permute-start(f32[3,384]{1,0:T(4,128)S(1)} %pad_maximum_fusion.10), channel_id=1, source_target_pairs={{0,4},{4,8},{8,12},{12,16},{16,20},{20,24},{24,28},{28,0},{1,5},{5... | collective-permute-start | bytes 13832 | tf_op jit(solution)/shard_map/ppermute | solution.py:503
  32.0 4.0 %collective-permute-start.5 = (f32[3,384]{1,0:T(4,128)S(1)}, f32[3,384]{1,0:T(4,128)S(1)}, u32[]{:S(2)}, u32[]{:S(2)}) collective-permute-start(f32[3,384]{1,0:T(4,128)S(1)} %pad_maximum_fusion.10), channel_id=1, source_target_pairs={{4,0},{8,4},{12,8},{16,12},{20,16},{24,20},{28,24},{0,28},{5,1},{9... | collective-permute-start | bytes 13832 | tf_op jit(solution)/shard_map/ppermute | solution.py:504
  34.7 11.5 %copy-start.21 = (f32[3,128]{1,0:T(4,128)}, f32[3,128]{1,0:T(4,128)S(1)}, u32[]{:S(2)}) copy-start(f32[3,128]{1,0:T(4,128)S(1)} %add_multiply_fusion.6) | copy-start | bytes 4612
  36.0 10.1 %collective-permute-start.8 = (f32[3,128]{1,0:T(4,128)S(1)}, f32[3,128]{1,0:T(4,128)S(1)}, u32[]{:S(2)}, u32[]{:S(2)}) collective-permute-start(f32[3,128]{1,0:T(4,128)S(1)} %add_multiply_fusion.6), channel_id=1, source_target_pairs={{0,1},{1,2},{2,3},{3,0},{4,5},{5,6},{6,7},{7,4},{8,9},{9,10},{10,1... | collective-permute-start | bytes 4616 | tf_op jit(solution)/shard_map/ppermute | solution.py:23
  36.1 10.1 %collective-permute-start.9 = (f32[3,128]{1,0:T(4,128)S(1)}, f32[3,128]{1,0:T(4,128)S(1)}, u32[]{:S(2)}, u32[]{:S(2)}) collective-permute-start(f32[3,128]{1,0:T(4,128)S(1)} %add_multiply_fusion.6), channel_id=1, source_target_pairs={{1,0},{2,1},{3,2},{0,3},{5,4},{6,5},{7,6},{4,7},{9,8},{10,9},{11,1... | collective-permute-start | bytes 4616 | tf_op jit(solution)/shard_map/ppermute | solution.py:25
  46.2 4.0 %collective-permute-start.10 = (f32[3,384]{1,0:T(4,128)S(1)}, f32[3,384]{1,0:T(4,128)S(1)}, u32[]{:S(2)}, u32[]{:S(2)}) collective-permute-start(f32[3,384]{1,0:T(4,128)S(1)} %constant_dynamic-update-slice_fusion), channel_id=1, source_target_pairs={{0,4},{4,8},{8,12},{12,16},{16,20},{20,24},{24,28},{28,0},{1,5},{5... | collective-permute-start | bytes 13832 | tf_op jit(solution)/shard_map/ppermute | solution.py:503
  46.3 4.0 %collective-permute-start.11 = (f32[3,384]{1,0:T(4,128)S(1)}, f32[3,384]{1,0:T(4,128)S(1)}, u32[]{:S(2)}, u32[]{:S(2)}) collective-permute-start(f32[3,384]{1,0:T(4,128)S(1)} %constant_dynamic-update-slice_fusion), channel_id=1, source_target_pairs={{4,0},{8,4},{12,8},{16,12},{20,16},{24,20},{28,24},{0,28},{5,1},{9... | collective-permute-start | bytes 13832 | tf_op jit(solution)/shard_map/ppermute | solution.py:504
  68.1 42.0 %all-to-all-start.2 = ((f32[8,3,16,16,128]{4,3,2,1,0:T(8,128)}), f32[8,3,16,16,128]{4,3,2,1,0:T(8,128)S(1)}, u32[]{:S(2)}, u32[]{:S(2)}) async-start(f32[8,3,16,16,128]{4,3,2,1,0:T(8,128)} %depth_forward.3), calls=%async_computation.2 | async-start | bytes 6291456 | tf_op jit(solution)/shard_map/all_to_all | solution.py:836
  72.2 17.2 %copy-start.6 = (bf16[2,256,256]{2,1,0:T(8,128)(2,1)S(1)}, bf16[2,256,256]{2,1,0:T(8,128)(2,1)}, u32[]{:S(2)}) copy-start(bf16[2,256,256]{2,1,0:T(8,128)(2,1)} %constant.219.clone) | copy-start | bytes 786436
  89.4 1.9 copy-start.9
  93.2 23.1 %copy-start.12 = (bf16[256,256]{1,0:T(8,128)(2,1)S(1)}, bf16[256,256]{1,0:T(8,128)(2,1)}, u32[]{:S(2)}) copy-start(bf16[256,256]{1,0:T(8,128)(2,1)} %get-tuple-element.51) | copy-start | bytes 393220
  93.2 23.1 %copy-start.13 = (bf16[256,256]{1,0:T(8,128)(2,1)S(1)}, bf16[256,256]{1,0:T(8,128)(2,1)}, u32[]{:S(2)}) copy-start(bf16[256,256]{1,0:T(8,128)(2,1)} %get-tuple-element.52) | copy-start | bytes 393220
  110.1 1.7 copy-start.4
  111.8 42.3 %all-to-all-start = ((f32[8,3,16,16,128]{4,3,2,1,0:T(8,128)}), f32[8,3,16,16,128]{4,3,2,1,0:T(8,128)}, u32[]{:S(2)}, u32[]{:S(2)}) async-start(f32[8,3,16,16,128]{4,3,2,1,0:T(8,128)} %depth_forward.2), calls=%async_computation | async-start | bytes 6291456 | tf_op jit(solution)/shard_map/all_to_all | solution.py:836
  118.3 11.4 %copy-start.8 = (bf16[1536,256]{1,0:T(8,128)(2,1)S(1)}, bf16[1536,256]{1,0:T(8,128)(2,1)}, u32[]{:S(2)}) copy-start(bf16[1536,256]{1,0:T(8,128)(2,1)} %copy-done.7) | copy-start | bytes 2359300
  125.8 13.3 %copy-start.14 = (f32[16,8,256]{2,1,0:T(8,128)S(1)}, f32[16,8,256]{2,1,0:T(8,128)}, u32[]{:S(2)}) copy-start(f32[16,8,256]{2,1,0:T(8,128)} %get-tuple-element.27) | copy-start | bytes 393220
  125.8 13.3 %copy-start.18 = (f32[8,8,256]{2,1,0:T(8,128)S(1)}, f32[8,8,256]{2,1,0:T(8,128)}, u32[]{:S(2)}) copy-start(f32[8,8,256]{2,1,0:T(8,128)} %copy-done.17) | copy-start | bytes 196612
  125.8 13.4 %copy-start.1 = (f32[18,8,256]{2,1,0:T(8,128)S(1)}, f32[18,8,256]{2,1,0:T(8,128)}, u32[]{:S(2)}) copy-start(f32[18,8,256]{2,1,0:T(8,128)} %copy-done) | copy-start | bytes 442372
  125.8 8.6 %collective-permute-start.15 = (f32[16,8,256]{2,1,0:T(8,128)}, f32[16,8,256]{2,1,0:T(8,128)S(1)}, u32[]{:S(2)}, u32[]{:S(2)}) collective-permute-start(f32[16,8,256]{2,1,0:T(8,128)} %get-tuple-element.27), channel_id=1, source_target_pairs={{0,1},{1,2},{2,3},{3,0},{4,5},{5,6},{6,7},{7,4},{8,9},{9,10},{10,1... | collective-permute-start | bytes 393224 | tf_op jit(solution)/shard_map/ppermute | solution.py:186
  125.9 13.2 %collective-permute-start.16 = (f32[16,8,256]{2,1,0:T(8,128)}, f32[16,8,256]{2,1,0:T(8,128)S(1)}, u32[]{:S(2)}, u32[]{:S(2)}) collective-permute-start(f32[16,8,256]{2,1,0:T(8,128)} %get-tuple-element.27), channel_id=1, source_target_pairs={{0,2},{1,3},{2,0},{3,1},{4,6},{5,7},{6,4},{7,5},{8,10},{9,11},{10,... | collective-permute-start | bytes 393224 | tf_op jit(solution)/shard_map/ppermute | solution.py:186
  126.4 12.7 %collective-permute-start.17 = (f32[16,8,256]{2,1,0:T(8,128)}, f32[16,8,256]{2,1,0:T(8,128)S(1)}, u32[]{:S(2)}, u32[]{:S(2)}) collective-permute-start(f32[16,8,256]{2,1,0:T(8,128)} %get-tuple-element.27), channel_id=1, source_target_pairs={{0,3},{1,0},{2,1},{3,2},{4,7},{5,4},{6,5},{7,6},{8,11},{9,8},{10,9... | collective-permute-start | bytes 393224 | tf_op jit(solution)/shard_map/ppermute | solution.py:186
  154.1 42.3 %all-to-all-start.3 = ((f32[8,3,16,16,128]{4,3,2,1,0:T(8,128)}), f32[8,3,16,16,128]{4,3,2,1,0:T(8,128)}, u32[]{:S(2)}, u32[]{:S(2)}) async-start(f32[8,3,16,16,128]{4,3,2,1,0:T(8,128)} %line_backward.3), calls=%async_computation.3 | async-start | bytes 6291456 | tf_op jit(solution)/shard_map/all_to_all | solution.py:840
  158.6 20.9 %copy-start.16 = (f32[8,8,256]{2,1,0:T(8,128)S(1)}, f32[8,8,256]{2,1,0:T(8,128)}, u32[]{:S(2)}) copy-start(f32[8,8,256]{2,1,0:T(8,128)} %copy-done.15) | copy-start | bytes 196612
  158.6 20.9 %copy-start.20 = (f32[8,8,256]{2,1,0:T(8,128)S(1)}, f32[8,8,256]{2,1,0:T(8,128)}, u32[]{:S(2)}) copy-start(f32[8,8,256]{2,1,0:T(8,128)} %copy-done.19) | copy-start | bytes 196612
  158.6 21.9 %copy-start.3 = (f32[18,8,256]{2,1,0:T(8,128)S(1)}, f32[18,8,256]{2,1,0:T(8,128)}, u32[]{:S(2)}) copy-start(f32[18,8,256]{2,1,0:T(8,128)} %copy-done.2) | copy-start | bytes 442372
  166.3 8.5 %collective-permute-start.12 = (f32[16,8,256]{2,1,0:T(8,128)}, f32[16,8,256]{2,1,0:T(8,128)S(1)}, u32[]{:S(2)}, u32[]{:S(2)}) collective-permute-start(f32[16,8,256]{2,1,0:T(8,128)} %get-tuple-element.25), channel_id=1, source_target_pairs={{0,1},{1,2},{2,3},{3,0},{4,5},{5,6},{6,7},{7,4},{8,9},{9,10},{10,1... | collective-permute-start | bytes 393224 | tf_op jit(solution)/shard_map/ppermute | solution.py:186
  166.3 13.2 %collective-permute-start.13 = (f32[16,8,256]{2,1,0:T(8,128)}, f32[16,8,256]{2,1,0:T(8,128)S(1)}, u32[]{:S(2)}, u32[]{:S(2)}) collective-permute-start(f32[16,8,256]{2,1,0:T(8,128)} %get-tuple-element.25), channel_id=1, source_target_pairs={{0,2},{1,3},{2,0},{3,1},{4,6},{5,7},{6,4},{7,5},{8,10},{9,11},{10,... | collective-permute-start | bytes 393224 | tf_op jit(solution)/shard_map/ppermute | solution.py:186
  166.9 12.6 %collective-permute-start.14 = (f32[16,8,256]{2,1,0:T(8,128)}, f32[16,8,256]{2,1,0:T(8,128)S(1)}, u32[]{:S(2)}, u32[]{:S(2)}) collective-permute-start(f32[16,8,256]{2,1,0:T(8,128)} %get-tuple-element.25), channel_id=1, source_target_pairs={{0,3},{1,0},{2,1},{3,2},{4,7},{5,4},{6,5},{7,6},{8,11},{9,8},{10,9... | collective-permute-start | bytes 393224 | tf_op jit(solution)/shard_map/ppermute | solution.py:186
  192.1 8.2 %copy-start.10 = (bf16[256,256]{1,0:T(8,128)(2,1)S(1)}, bf16[256,256]{1,0:T(8,128)(2,1)}, u32[]{:S(2)}) copy-start(bf16[256,256]{1,0:T(8,128)(2,1)} %get-tuple-element.47) | copy-start | bytes 393220
  192.1 8.2 %copy-start.11 = (bf16[256,256]{1,0:T(8,128)(2,1)S(1)}, bf16[256,256]{1,0:T(8,128)(2,1)}, u32[]{:S(2)}) copy-start(bf16[256,256]{1,0:T(8,128)(2,1)} %get-tuple-element.48) | copy-start | bytes 393220
  196.4 41.4 %all-to-all-start.1 = ((f32[8,3,16,16,128]{4,3,2,1,0:T(8,128)}), f32[8,3,16,16,128]{4,3,2,1,0:T(8,128)S(1)}, u32[]{:S(2)}, u32[]{:S(2)}) async-start(f32[8,3,16,16,128]{4,3,2,1,0:T(8,128)} %line_backward.2), calls=%async_computation.1 | async-start | bytes 6291456 | tf_op jit(solution)/shard_map/all_to_all | solution.py:840
  246.4 12.5 %collective-permute-start.18 = (f32[3,2,64,256]{3,2,1,0:T(8,128)}, f32[3,2,64,256]{3,2,1,0:T(8,128)S(1)}, u32[]{:S(2)}, u32[]{:S(2)}) collective-permute-start(f32[3,2,64,256]{3,2,1,0:T(8,128)} %get-tuple-element.29), channel_id=1, source_target_pairs={{0,4},{4,8},{8,12},{12,16},{16,20},{20,24},{24,28},{28,0},{1,5},{5... | collective-permute-start | bytes 1179656 | tf_op jit(solution)/shard_map/ppermute | solution.py:473
  246.4 12.5 %collective-permute-start.19 = (f32[3,2,64,256]{3,2,1,0:T(8,128)}, f32[3,2,64,256]{3,2,1,0:T(8,128)S(1)}, u32[]{:S(2)}, u32[]{:S(2)}) collective-permute-start(f32[3,2,64,256]{3,2,1,0:T(8,128)} %get-tuple-element.30), channel_id=1, source_target_pairs={{4,0},{8,4},{12,8},{16,12},{20,16},{24,20},{28,24},{0,28},{5,1},{9... | collective-permute-start | bytes 1179656 | tf_op jit(solution)/shard_map/ppermute | solution.py:474
  267.4 5.4 %collective-permute-start.20 = (f32[3,128]{1,0:T(4,128)S(1)}, f32[3,128]{1,0:T(4,128)S(1)}, u32[]{:S(2)}, u32[]{:S(2)}) collective-permute-start(f32[3,128]{1,0:T(4,128)S(1)} %get-tuple-element.53), channel_id=1, source_target_pairs={{0,1},{1,2},{2,3},{3,0},{4,5},{5,6},{6,7},{7,4},{8,9},{9,10},{10,1... | collective-permute-start | bytes 4616 | tf_op jit(solution)/shard_map/ppermute | solution.py:496
  267.4 5.4 %collective-permute-start.21 = (f32[3,128]{1,0:T(4,128)S(1)}, f32[3,128]{1,0:T(4,128)S(1)}, u32[]{:S(2)}, u32[]{:S(2)}) collective-permute-start(f32[3,128]{1,0:T(4,128)S(1)} %get-tuple-element.54), channel_id=1, source_target_pairs={{1,0},{2,1},{3,2},{0,3},{5,4},{6,5},{7,6},{4,7},{9,8},{10,9},{11,1... | collective-permute-start | bytes 4616 | tf_op jit(solution)/shard_map/ppermute | solution.py:497
  (6 other events, 5.7 us)

commit v2 on v1

--- a/solution.py
+++ b/solution.py
@@ -133,9 +133,9 @@
     return jnp.sin(freq.astype(f32) * (math.pi / length))
 
 
-def coefficients(plan, chunk):
+def coefficients(plan, chunk, place):
     n = plan.grid
-    first = lax.axis_index("gx") * plan.slots + chunk * plan.kh
+    first = place * plan.slots + chunk * plan.kh
     slot = first + lax.broadcasted_iota(jnp.int32, (plan.kh, n), 0)
     kx = lax.broadcasted_iota(jnp.int32, (plan.kh, n), 1)
     half = n // 2
@@ -340,12 +340,13 @@
     parts, table, out = refs[: plan.chunks], refs[plan.chunks], refs[plan.chunks + 1]
 
     def block_step(index, carry):
+        y_first = pl.program_id(1) * (plan.y_part // plan.yb) + index * plan.y_sub
         columns = []
         for sub in range(plan.y_sub):
             columns.append(
                 jnp.concatenate(
                     [
-                        part[:, 0, index * plan.y_sub + sub].reshape(plan.gx * plan.kk, lanes)
+                        part[:, pl.program_id(0), y_first + sub].reshape(plan.gx * plan.kk, lanes)
                         for part in parts
                     ],
                     axis=0,
@@ -364,18 +365,16 @@
 
 
 def depth_backward(plan, parts, table):
-    in_block = pl.BlockSpec(
-        (plan.gx, 1, plan.y_part // plan.yb, plan.kk, lanes), lambda c, y: (0, c, y, 0, 0)
-    )
     return pl.pallas_call(
         lambda *refs: depth_backward_kernel(plan, *refs),
         grid=(3, plan.pencil // plan.y_part),
-        in_specs=[in_block] * plan.chunks + [pl.BlockSpec(table.shape, lambda c, y: (0, 0))],
+        in_specs=[pl.BlockSpec(memory_space=pltpu.VMEM)] * plan.chunks + [pl.BlockSpec(table.shape, lambda c, y: (0, 0))],
         out_specs=pl.BlockSpec(
             (1, plan.slab, plan.y_part, plan.grid), lambda c, y: (c, 0, y, 0)
         ),
         out_shape=jax.ShapeDtypeStruct((3, plan.slab, plan.pencil, plan.grid), f32),
         name="depth_backward",
+        compiler_params=pltpu.CompilerParams(vmem_limit_bytes=20 * 1024 * 1024),
         cost_estimate=cost(plan, 16, 6),
     )(*parts, table)
 
@@ -385,12 +384,13 @@
     slab, n = plan.slab, plan.grid
 
     def block_step(index, carry):
+        y_first = pl.program_id(1) * (plan.y_part // plan.yb) + index * plan.y_sub
         columns = []
         for sub in range(plan.y_sub):
             columns.append(
                 jnp.concatenate(
                     [
-                        part[:, 0, index * plan.y_sub + sub].reshape(plan.gx * plan.kk, lanes)
+                        part[:, pl.program_id(0), y_first + sub].reshape(plan.gx * plan.kk, lanes)
                         for part in parts
                     ],
                     axis=0,
@@ -414,17 +414,15 @@
 
 
 def depth_edges(plan, parts, table):
-    in_block = pl.BlockSpec(
-        (plan.gx, 1, plan.y_part // plan.yb, plan.kk, lanes), lambda c, y: (0, c, y, 0, 0)
-    )
     layers = pl.BlockSpec((1, 2, plan.y_part, plan.grid), lambda c, y: (c, 0, y, 0))
     return pl.pallas_call(
         lambda *refs: depth_edges_kernel(plan, *refs),
         grid=(3, plan.pencil // plan.y_part),
-        in_specs=[in_block] * plan.chunks + [pl.BlockSpec(table.shape, lambda c, y: (0, 0))],
+        in_specs=[pl.BlockSpec(memory_space=pltpu.VMEM)] * plan.chunks + [pl.BlockSpec(table.shape, lambda c, y: (0, 0))],
         out_specs=[layers, layers],
         out_shape=[jax.ShapeDtypeStruct((3, 2, plan.pencil, plan.grid), f32)] * 2,
         name="depth_edges",
+        compiler_params=pltpu.CompilerParams(vmem_limit_bytes=20 * 1024 * 1024),
         cost_estimate=cost(plan, 8, 6),
     )(*parts, table)
 
@@ -565,7 +563,11 @@
         for c in range(3):
             columns = [
                 group_transpose(
-                    [spectrum[v * plan.groups + i, c, hi] for i in range(plan.groups)], plan.slab
+                    [
+                        spectrum[v * plan.groups + i, c, step * yh_step + hi]
+                        for i in range(plan.groups)
+                    ],
+                    plan.slab,
                 )
                 for v in range(n // lanes)
             ]
@@ -624,7 +626,7 @@
         lambda *refs: line_forward_kernel(plan, chunk, yh_step, *refs),
         grid=(plan.y_hi // yh_step,),
         in_specs=[
-            pl.BlockSpec((plan.gx, 3, yh_step, plan.kk, lanes), lambda s: (0, 0, s, 0, 0)),
+            pl.BlockSpec(memory_space=pltpu.VMEM),
             pl.BlockSpec(coef.shape, lambda s: (0, 0, 0)),
             pl.BlockSpec(table.shape, lambda s: (0, 0)),
         ],
@@ -638,6 +640,7 @@
         ],
         scratch_shapes=[pltpu.VMEM((4, kh, n), f32), pltpu.VMEM((2, kh, n), f32)],
         name="line_forward",
+        compiler_params=pltpu.CompilerParams(vmem_limit_bytes=20 * 1024 * 1024),
         cost_estimate=cost(plan, 16 // plan.chunks, 20 // plan.chunks),
     )(spectrum, coef, table)
 
@@ -828,11 +831,11 @@
     )(field, coef, entering, table)
 
 
-def project(plan, spectra, tables):
+def project(plan, spectra, tables, place):
     ahead, backward = tables
     back = []
     for chunk, spectrum in enumerate(spectra):
-        coef, weights = coefficients(plan, chunk)
+        coef, weights = coefficients(plan, chunk, place)
         received = lax.all_to_all(spectrum, "gx", split_axis=0, concat_axis=0, tiled=True)
         field, ends = line_forward(plan, chunk, received, coef, ahead)
         entering = incoming(plan, ends, weights)
@@ -879,11 +882,12 @@
         )
         for chunk in range(plan.chunks)
     ]
-    late, spectra[0] = lax.optimization_barrier(
-        ((z_ahead,) + tuple(jnp.asarray(part) for part in x_table_parts(plan)), spectra[0])
-    )
+    begun = spectra[-1][0, 0, 0, 0, 0] > jnp.inf
+    place = lax.axis_index("gx") + begun.astype(jnp.int32)
+    parts = (z_ahead,) + tuple(jnp.asarray(part) for part in x_table_parts(plan))
+    late = [part + begun.astype(bf16) for part in parts]
     z_back = z_table_back(plan, late[0])
-    back = project(plan, spectra, x_tables(plan, late[1], late[2]))
+    back = project(plan, spectra, x_tables(plan, late[1], late[2]), place)
     head, tail = depth_edges(plan, back, z_back)
     new_velocity = depth_backward(plan, back, z_back)
     colloid_drift = live * brought_home(plan, sample(plan, new_velocity, head, tail, column))

time: 275 us -> 269 us (0.978)
  Pallas kernels: 100 us -> 91.7 us
  local copies, waits for them, and re-layouts: 11.5 us -> 16.2 us
  other arithmetic: 23 us -> 20 us
    pallas_call x2, Pallas kernels: 23.1 us -> 19.8 us  [line_backward(): pl.pallas_call(lambda *refs: line_backward_kernel(plan, chunk, yh_step, *...]
    unnamed x66 -> x57, local copies, waits for them, and re-layouts: 8.14 us -> 11.1 us
    pallas_call x2, Pallas kernels: 15.2 us -> 12.3 us  [line_forward(): pl.pallas_call(lambda *refs: line_forward_kernel(plan, chunk, yh_step, *r...]
  transfers between devices with their start and end apart: 26 -> 26, of which waited for: 11 -> 13; matrix products, arithmetic and copies ran while one was open for 9% -> 8% of each run, Pallas kernels for 23% -> 21%
where the time goes in v2:
time: 269 us; the launch traced here: 268 us
  Pallas kernels  91.7 us (34%)
  waiting for transfers between devices  84.8 us (32%)
  starting transfers between devices  52.9 us (20%)
  other arithmetic  20 us (7%)
  local copies, waits for them, and re-layouts  16.2 us (6%)
    all_to_all x2, waiting for transfers between devices, project(): lax.all_to_all(solved, 'gx', split_axis=0, concat_axis=0, tiled=True)  40.5 us
    pallas_call x2, Pallas kernels, depth_forward(): pl.pallas_call(lambda *refs: depth_forward_kernel(plan, (refs[0], refs[1]...  34.3 us
    pallas_call x2, Pallas kernels, line_backward(): pl.pallas_call(lambda *refs: line_backward_kernel(plan, chunk, yh_step, *...  19.8 us
    all_to_all x2, waiting for transfers between devices, project(): lax.all_to_all(spectrum, 'gx', split_axis=0, concat_axis=0, tiled=True)  18.6 us
    ppermute x6, waiting for transfers between devices, incoming(): lax.ppermute(ends, 'gy', [(i, (i + hop) % gy) for i in range(gy)])  18.1 us
    pallas_call x2, Pallas kernels, sample(): pl.pallas_call(lambda *refs: sample_kernel(plan, *refs), grid=(3,), in_sp...  12.6 us
    pallas_call x2, Pallas kernels, line_forward(): pl.pallas_call(lambda *refs: line_forward_kernel(plan, chunk, yh_step, *r...  12.3 us
    unnamed x57, local copies, waits for them, and re-layouts  11.1 us
  transfers between devices with their start and end apart: 26, of which 13 were waited for; matrix products, arithmetic and copies ran while one was open for 8% of the time, Pallas kernels for 21%

profile of v2, /device:TPU:0, one launch (start us, length us, event | category | flops | bytes accessed | tf_op | source)
XLA Modules:
  0.0 268.2 jit_solution(14371789914395495527)
XLA Ops:
  1.3 3.1 %collective-permute-start = (f32[3,128]{1,0:T(4,128)S(1)}, f32[3,128]{1,0:T(4,128)S(1)}, u32[]{:S(2)}, u32[]{:S(2)}) collective-permute-start(f32[3,128]{1,0:T(4,128)S(1)} %convert_add_fusion), channel_id=1, source_target_pairs={{0,1},{1,2},{2,3},{3,0},{4,5},{5,6},{6,7},{7,4},{8,9},{9,10},{10,1... | collective-permute-start | bytes 4616 | tf_op jit(solution)/shard_map/ppermute | solution.py:23
  4.4 2.0 collective-permute-start.1
  6.4 1.2 fusion.239
  7.7 2.6 collective-permute-start.3
  13.3 1.4 fusion.34
  15.8 2.1 collective-permute-done.2.refs_1_
  19.1 6.3 %sample.2 = f32[3,1,384]{2,1,0:T(1,128)} custom-call(f32[3,32,64,256]{3,2,1,0:T(8,128)} %refs_0_.5, f32[3,2,64,256]{3,2,1,0:T(8,128)} %copy-done.20, f32[3,2,64,256]{3,2,1,0:T(8,128)} %copy-done.21, f32[2,40,384]{2,1,0:T(8,128)} %pad_maximum_fusion.8.refs_3_.refs_2_, f32[2,64,384]{2,1,0:T(8,128)} %pad_maximum_fusion.5.refs_4_.refs_3_, ...), custom_call_target="tpu_custom_call" | custom-call | flops 6000000000 | bytes 8000000 | tf_op jit(solution)/shard_map/sample/pallas_call | solution.py:475
  26.1 3.8 %collective-permute-start.7 = (f32[3,128]{1,0:T(4,128)S(1)}, f32[3,128]{1,0:T(4,128)S(1)}, u32[]{:S(2)}, u32[]{:S(2)}) collective-permute-start(f32[3,128]{1,0:T(4,128)S(1)} %get-tuple-element.48), channel_id=1, source_target_pairs={{1,0},{2,1},{3,2},{0,3},{5,4},{6,5},{7,6},{4,7},{9,8},{10,9},{11,1... | collective-permute-start | bytes 4616 | tf_op jit(solution)/shard_map/ppermute | solution.py:495
  29.9 1.3 collective-permute-start.4
  31.2 1.4 collective-permute-start.5
  32.6 1.3 collective-permute-done.4
  34.0 3.8 %collective-permute-start.9 = (f32[3,128]{1,0:T(4,128)S(1)}, f32[3,128]{1,0:T(4,128)S(1)}, u32[]{:S(2)}, u32[]{:S(2)}) collective-permute-start(f32[3,128]{1,0:T(4,128)S(1)} %add_multiply_fusion.6), channel_id=1, source_target_pairs={{1,0},{2,1},{3,2},{0,3},{5,4},{6,5},{7,6},{4,7},{9,8},{10,9},{11,1... | collective-permute-start | bytes 4616 | tf_op jit(solution)/shard_map/ppermute | solution.py:25
  37.8 2.8 %fusion.6 = (f32[1,256,768]{2,1,0:T(8,128)S(1)}, f32[1,256,768]{2,1,0:T(8,128)S(1)}) fusion(f32[256]{0:T(256)S(1)} %iota_convert_fusion, f32[768]{0:T(1024)S(1)} %get-tuple-element.23, f32[256]{0:T(256)S(1)} %fusion.236), kind=kLoop, calls=%fused_computation.19 | loop fusion | flops 12189696 | bytes 1577984 | tf_op jit(solution)/shard_map/jit(_where)/select_n | solution.py:42
  41.9 1.4 fusion
  44.3 2.6 collective-permute-start.11
  48.8 17.2 %depth_forward.3 = f32[8,3,16,16,128]{4,3,2,1,0:T(8,128)} custom-call(f32[3,32,64,256]{3,2,1,0:T(8,128)} %refs_0_.5, f32[3,32,64,256]{3,2,1,0:T(8,128)} %refs_1_.3, f32[2,40,384]{2,1,0:T(8,128)} %pad_maximum_fusion.8.refs_3_.refs_2_, f32[2,64,384]{2,1,0:T(8,128)} %pad_maximum_fusion.5.refs_4_.refs_3_, ...), custom_call_target="tpu_custom_call" | custom-call | flops 20000000000 | bytes 20000000 | tf_op jit(solution)/shard_map/depth_forward/pallas_call | solution.py:320
  66.0 1.2 slice.173
  67.8 5.1 %all-to-all-start.2 = ((f32[8,3,16,16,128]{4,3,2,1,0:T(8,128)}), f32[8,3,16,16,128]{4,3,2,1,0:T(8,128)S(1)}, u32[]{:S(2)}, u32[]{:S(2)}) async-start(f32[8,3,16,16,128]{4,3,2,1,0:T(8,128)} %depth_forward.3), calls=%async_computation.2 | async-start | bytes 6291456 | tf_op jit(solution)/shard_map/all_to_all | solution.py:839
  80.4 17.2 %depth_forward.2 = f32[8,3,16,16,128]{4,3,2,1,0:T(8,128)} custom-call(f32[3,32,64,256]{3,2,1,0:T(8,128)} %refs_0_.5, f32[3,32,64,256]{3,2,1,0:T(8,128)} %refs_1_.3, f32[2,40,384]{2,1,0:T(8,128)} %pad_maximum_fusion.8.refs_3_.refs_2_, f32[2,64,384]{2,1,0:T(8,128)} %pad_maximum_fusion.5.refs_4_.refs_3_, ...), custom_call_target="tpu_custom_call" | custom-call | flops 20000000000 | bytes 20000000 | tf_op jit(solution)/shard_map/depth_forward/pallas_call | solution.py:320
  97.5 13.3 %all-to-all-done.2.refs_0_ = f32[8,3,16,16,128]{4,3,2,1,0:T(8,128)S(1)} async-done(((f32[8,3,16,16,128]{4,3,2,1,0:T(8,128)}), f32[8,3,16,16,128]{4,3,2,1,0:T(8,128)S(1)}, u32[]{:S(2)}, u32[]{:S(2)}) %all-to-all-start.2) | async-done | bytes 3145760 | tf_op jit(solution)/shard_map/all_to_all | solution.py:839
  110.8 4.5 %all-to-all-start = ((f32[8,3,16,16,128]{4,3,2,1,0:T(8,128)}), f32[8,3,16,16,128]{4,3,2,1,0:T(8,128)}, u32[]{:S(2)}, u32[]{:S(2)}) async-start(f32[8,3,16,16,128]{4,3,2,1,0:T(8,128)} %depth_forward.2), calls=%async_computation | async-start | bytes 6291456 | tf_op jit(solution)/shard_map/all_to_all | solution.py:839
  115.3 1.3 maximum_maximum_fusion.refs_2_
  116.6 5.0 %line_forward.3 = (f32[3,64,2,8,256]{4,3,2,1,0:T(8,128)S(1)}, f32[16,8,256]{2,1,0:T(8,128)S(1)}) custom-call(f32[8,3,16,16,128]{4,3,2,1,0:T(8,128)S(1)} %all-to-all-done.2.refs_0_, f32[18,8,256]{2,1,0:T(8,128)S(1)} %get-tuple-element.120.refs_1_, bf16[768,512]{1,0:T(8,128)(2,1)S(1)} %maximum_maximum_fusion.refs_2_), custom_call_target="tpu_custom_call" | custom-call | flops 8000000000 | bytes 10000000 | tf_op jit(solution)/shard_map/line_forward/pallas_call | solution.py:625
  121.6 1.7 copy-done.6
  123.9 3.3 %collective-permute-start.17 = (f32[16,8,256]{2,1,0:T(8,128)S(1)}, f32[16,8,256]{2,1,0:T(8,128)S(1)}, u32[]{:S(2)}, u32[]{:S(2)}) collective-permute-start(f32[16,8,256]{2,1,0:T(8,128)S(1)} %get-tuple-element.20), channel_id=1, source_target_pairs={{0,3},{1,0},{2,1},{3,2},{4,7},{5,4},{6,5},{7,6},{8,11},{9,8},{10,9... | collective-permute-start | bytes 393224 | tf_op jit(solution)/shard_map/ppermute | solution.py:186
  127.2 4.4 %collective-permute-done.15 = f32[16,8,256]{2,1,0:T(8,128)S(1)} collective-permute-done((f32[16,8,256]{2,1,0:T(8,128)S(1)}, f32[16,8,256]{2,1,0:T(8,128)S(1)}, u32[]{:S(2)}, u32[]{:S(2)}) %collective-permute-start.15) | collective-permute-done | bytes 131104 | tf_op jit(solution)/shard_map/ppermute | solution.py:186
  131.6 4.6 %collective-permute-done.16 = f32[16,8,256]{2,1,0:T(8,128)S(1)} collective-permute-done((f32[16,8,256]{2,1,0:T(8,128)S(1)}, f32[16,8,256]{2,1,0:T(8,128)S(1)}, u32[]{:S(2)}, u32[]{:S(2)}) %collective-permute-start.16) | collective-permute-done | bytes 131104 | tf_op jit(solution)/shard_map/ppermute | solution.py:186
  136.4 9.8 %line_backward.3 = f32[8,3,16,16,128]{4,3,2,1,0:T(8,128)S(1)} custom-call(f32[3,64,2,8,256]{4,3,2,1,0:T(8,128)} %copy-done.6, f32[18,8,256]{2,1,0:T(8,128)S(1)} %get-tuple-element.120.refs_1_, f32[16,8,256]{2,1,0:T(8,128)S(1)} %pad_maximum_fusion.7.refs_2_, bf16[1536,256]{1,0:T(8,128)(2,1)S(1)} %broadcast_multiply_fusion.refs_3_), custom_call_target="tpu_custom_call" | custom-call | flops 12000000000 | bytes 12000000 | tf_op jit(solution)/shard_map/line_backward/pallas_call | solution.py:818
  146.2 1.7 copy-done
  147.8 5.3 %all-to-all-done.refs_0_ = f32[8,3,16,16,128]{4,3,2,1,0:T(8,128)} async-done(((f32[8,3,16,16,128]{4,3,2,1,0:T(8,128)}), f32[8,3,16,16,128]{4,3,2,1,0:T(8,128)}, u32[]{:S(2)}, u32[]{:S(2)}) %all-to-all-start) | async-done | bytes 3145760 | tf_op jit(solution)/shard_map/all_to_all | solution.py:839
  153.2 3.9 %all-to-all-start.3 = ((f32[8,3,16,16,128]{4,3,2,1,0:T(8,128)}), f32[8,3,16,16,128]{4,3,2,1,0:T(8,128)S(1)}, u32[]{:S(2)}, u32[]{:S(2)}) async-start(f32[8,3,16,16,128]{4,3,2,1,0:T(8,128)} %copy-done), calls=%async_computation.3 | async-start | bytes 6291456 | tf_op jit(solution)/shard_map/all_to_all | solution.py:843
  158.2 7.2 %line_forward.2 = (f32[3,64,2,8,256]{4,3,2,1,0:T(8,128)S(1)}, f32[16,8,256]{2,1,0:T(8,128)S(1)}) custom-call(f32[8,3,16,16,128]{4,3,2,1,0:T(8,128)} %all-to-all-done.refs_0_, f32[18,8,256]{2,1,0:T(8,128)S(1)} %get-tuple-element.121.refs_1_, bf16[768,512]{1,0:T(8,128)(2,1)S(1)} %copy-done.5), custom_call_target="tpu_custom_call" | custom-call | flops 8000000000 | bytes 10000000 | tf_op jit(solution)/shard_map/line_forward/pallas_call | solution.py:625
  165.4 1.7 copy-done.7
  167.6 3.3 %collective-permute-start.14 = (f32[16,8,256]{2,1,0:T(8,128)S(1)}, f32[16,8,256]{2,1,0:T(8,128)S(1)}, u32[]{:S(2)}, u32[]{:S(2)}) collective-permute-start(f32[16,8,256]{2,1,0:T(8,128)S(1)} %get-tuple-element.18), channel_id=1, source_target_pairs={{0,3},{1,0},{2,1},{3,2},{4,7},{5,4},{6,5},{7,6},{8,11},{9,8},{10,9... | collective-permute-start | bytes 393224 | tf_op jit(solution)/shard_map/ppermute | solution.py:186
  170.9 4.5 %collective-permute-done.12 = f32[16,8,256]{2,1,0:T(8,128)S(1)} collective-permute-done((f32[16,8,256]{2,1,0:T(8,128)S(1)}, f32[16,8,256]{2,1,0:T(8,128)S(1)}, u32[]{:S(2)}, u32[]{:S(2)}) %collective-permute-start.12) | collective-permute-done | bytes 131104 | tf_op jit(solution)/shard_map/ppermute | solution.py:186
  175.4 4.6 %collective-permute-done.13 = f32[16,8,256]{2,1,0:T(8,128)S(1)} collective-permute-done((f32[16,8,256]{2,1,0:T(8,128)S(1)}, f32[16,8,256]{2,1,0:T(8,128)S(1)}, u32[]{:S(2)}, u32[]{:S(2)}) %collective-permute-start.13) | collective-permute-done | bytes 131104 | tf_op jit(solution)/shard_map/ppermute | solution.py:186
  180.1 10.0 %line_backward.2 = f32[8,3,16,16,128]{4,3,2,1,0:T(8,128)S(1)} custom-call(f32[3,64,2,8,256]{4,3,2,1,0:T(8,128)} %copy-done.7, f32[18,8,256]{2,1,0:T(8,128)S(1)} %get-tuple-element.121.refs_1_, f32[16,8,256]{2,1,0:T(8,128)S(1)} %pad_maximum_fusion.6.refs_2_, bf16[1536,256]{1,0:T(8,128)(2,1)S(1)} %copy-done.3), custom_call_target="tpu_custom_call" | custom-call | flops 12000000000 | bytes 12000000 | tf_op jit(solution)/shard_map/line_backward/pallas_call | solution.py:818
  190.1 1.7 copy-done.1
  191.8 2.8 %all-to-all-done.3.refs_1_ = f32[8,3,16,16,128]{4,3,2,1,0:T(8,128)S(1)} async-done(((f32[8,3,16,16,128]{4,3,2,1,0:T(8,128)}), f32[8,3,16,16,128]{4,3,2,1,0:T(8,128)S(1)}, u32[]{:S(2)}, u32[]{:S(2)}) %all-to-all-start.3) | async-done | bytes 3145760 | tf_op jit(solution)/shard_map/all_to_all | solution.py:843
  194.6 4.5 %all-to-all-start.1 = ((f32[8,3,16,16,128]{4,3,2,1,0:T(8,128)}), f32[8,3,16,16,128]{4,3,2,1,0:T(8,128)}, u32[]{:S(2)}, u32[]{:S(2)}) async-start(f32[8,3,16,16,128]{4,3,2,1,0:T(8,128)} %copy-done.1), calls=%async_computation.1 | async-start | bytes 6291456 | tf_op jit(solution)/shard_map/all_to_all | solution.py:843
  199.3 37.7 %all-to-all-done.1.refs_0_ = f32[8,3,16,16,128]{4,3,2,1,0:T(8,128)} async-done(((f32[8,3,16,16,128]{4,3,2,1,0:T(8,128)}), f32[8,3,16,16,128]{4,3,2,1,0:T(8,128)}, u32[]{:S(2)}, u32[]{:S(2)}) %all-to-all-start.1) | async-done | bytes 3145760 | tf_op jit(solution)/shard_map/all_to_all | solution.py:843
  236.9 5.2 %depth_edges.1 = (f32[3,2,64,256]{3,2,1,0:T(8,128)S(1)}, f32[3,2,64,256]{3,2,1,0:T(8,128)S(1)}) custom-call(f32[8,3,16,16,128]{4,3,2,1,0:T(8,128)} %all-to-all-done.1.refs_0_, f32[8,3,16,16,128]{4,3,2,1,0:T(8,128)S(1)} %all-to-all-done.3.refs_1_, bf16[768,256]{1,0:T(8,128)(2,1)S(1)} %pad_maximum_fusion.3.refs_2_), custom_call_target="tpu_custom_call" | custom-call | flops 8000000000 | bytes 6000000 | tf_op jit(solution)/shard_map/depth_edges/pallas_call | solution.py:418
  242.2 2.6 collective-permute-start.19
  244.9 7.5 %depth_backward.1.refs_0_ = f32[3,32,64,256]{3,2,1,0:T(8,128)} custom-call(f32[8,3,16,16,128]{4,3,2,1,0:T(8,128)} %all-to-all-done.1.refs_0_, f32[8,3,16,16,128]{4,3,2,1,0:T(8,128)S(1)} %all-to-all-done.3.refs_1_, bf16[768,256]{1,0:T(8,128)(2,1)S(1)} %pad_maximum_fusion.3.refs_2_), custom_call_target="tpu_custom_call" | custom-call | flops 16000000000 | bytes 6000000 | tf_op jit(solution)/shard_map/depth_backward/pallas_call | solution.py:368
  252.4 2.2 collective-permute-done.18.refs_1_
  255.3 6.3 %sample.3 = f32[3,1,384]{2,1,0:T(1,128)} custom-call(f32[3,32,64,256]{3,2,1,0:T(8,128)} %depth_backward.1.refs_0_, f32[3,2,64,256]{3,2,1,0:T(8,128)} %copy-done.22, f32[3,2,64,256]{3,2,1,0:T(8,128)} %collective-permute-done.19.refs_2_, f32[2,40,384]{2,1,0:T(8,128)} %pad_maximum_fusion.8.refs_3_.refs_2_, f32[2,64,384]{2,1,0:T(8,128)} %pad_maximum_fusion.5.refs_4_.refs_3_, ...), custom_call_target="tpu_custom_call" | custom-call | flops 6000000000 | bytes 8000000 | tf_op jit(solution)/shard_map/sample/pallas_call | solution.py:475
  262.3 3.8 %collective-permute-start.21 = (f32[3,128]{1,0:T(4,128)S(1)}, f32[3,128]{1,0:T(4,128)S(1)}, u32[]{:S(2)}, u32[]{:S(2)}) collective-permute-start(f32[3,128]{1,0:T(4,128)S(1)} %get-tuple-element.46), channel_id=1, source_target_pairs={{1,0},{2,1},{3,2},{0,3},{5,4},{6,5},{7,6},{4,7},{9,8},{10,9},{11,1... | collective-permute-start | bytes 4616 | tf_op jit(solution)/shard_map/ppermute | solution.py:495
  266.1 1.6 collective-permute-done.20
  (156 shorter events, 22.2 us)
Async XLA Ops:
  1.3 9.9 %collective-permute-start = (f32[3,128]{1,0:T(4,128)S(1)}, f32[3,128]{1,0:T(4,128)S(1)}, u32[]{:S(2)}, u32[]{:S(2)}) collective-permute-start(f32[3,128]{1,0:T(4,128)S(1)} %convert_add_fusion), channel_id=1, source_target_pairs={{0,1},{1,2},{2,3},{3,0},{4,5},{5,6},{6,7},{7,4},{8,9},{9,10},{10,1... | collective-permute-start | bytes 4616 | tf_op jit(solution)/shard_map/ppermute | solution.py:23
  4.4 6.8 %collective-permute-start.1 = (f32[3,128]{1,0:T(4,128)S(1)}, f32[3,128]{1,0:T(4,128)S(1)}, u32[]{:S(2)}, u32[]{:S(2)}) collective-permute-start(f32[3,128]{1,0:T(4,128)S(1)} %convert_add_fusion), channel_id=1, source_target_pairs={{1,0},{2,1},{3,2},{0,3},{5,4},{6,5},{7,6},{4,7},{9,8},{10,9},{11,1... | collective-permute-start | bytes 4616 | tf_op jit(solution)/shard_map/ppermute | solution.py:25
  7.6 10.3 %collective-permute-start.2 = (f32[3,2,64,256]{3,2,1,0:T(8,128)S(1)}, f32[3,2,64,256]{3,2,1,0:T(8,128)S(1)}, u32[]{:S(2)}, u32[]{:S(2)}) collective-permute-start(f32[3,2,64,256]{3,2,1,0:T(8,128)S(1)} %get-tuple-element.30), channel_id=1, source_target_pairs={{0,4},{4,8},{8,12},{12,16},{16,20},{20,24},{24,28},{28,0},{1,5},{5... | collective-permute-start | bytes 1179656 | tf_op jit(solution)/shard_map/ppermute | solution.py:471
  7.7 10.6 %collective-permute-start.3 = (f32[3,2,64,256]{3,2,1,0:T(8,128)S(1)}, f32[3,2,64,256]{3,2,1,0:T(8,128)S(1)}, u32[]{:S(2)}, u32[]{:S(2)}) collective-permute-start(f32[3,2,64,256]{3,2,1,0:T(8,128)S(1)} %get-tuple-element.29), channel_id=1, source_target_pairs={{4,0},{8,4},{12,8},{16,12},{20,16},{24,20},{28,24},{0,28},{5,1},{9... | collective-permute-start | bytes 1179656 | tf_op jit(solution)/shard_map/ppermute | solution.py:472
  17.9 0.7 copy-start.20
  18.3 0.8 copy-start.21
  19.1 13.5 %copy-start.18 = (f32[3,128]{1,0:T(4,128)S(1)}, f32[3,128]{1,0:T(4,128)}, u32[]{:S(2)}) copy-start(f32[3,128]{1,0:T(4,128)} %param.15) | copy-start | bytes 4612
  19.1 13.5 %copy-start.19 = (f32[3,128]{1,0:T(4,128)S(1)}, f32[3,128]{1,0:T(4,128)}, u32[]{:S(2)}) copy-start(f32[3,128]{1,0:T(4,128)} %param.14) | copy-start | bytes 4612
  26.0 6.5 %collective-permute-start.6 = (f32[3,128]{1,0:T(4,128)S(1)}, f32[3,128]{1,0:T(4,128)S(1)}, u32[]{:S(2)}, u32[]{:S(2)}) collective-permute-start(f32[3,128]{1,0:T(4,128)S(1)} %get-tuple-element.47), channel_id=1, source_target_pairs={{0,1},{1,2},{2,3},{3,0},{4,5},{5,6},{6,7},{7,4},{8,9},{9,10},{10,1... | collective-permute-start | bytes 4616 | tf_op jit(solution)/shard_map/ppermute | solution.py:494
  26.1 6.5 %collective-permute-start.7 = (f32[3,128]{1,0:T(4,128)S(1)}, f32[3,128]{1,0:T(4,128)S(1)}, u32[]{:S(2)}, u32[]{:S(2)}) collective-permute-start(f32[3,128]{1,0:T(4,128)S(1)} %get-tuple-element.48), channel_id=1, source_target_pairs={{1,0},{2,1},{3,2},{0,3},{5,4},{6,5},{7,6},{4,7},{9,8},{10,9},{11,1... | collective-permute-start | bytes 4616 | tf_op jit(solution)/shard_map/ppermute | solution.py:495
  29.9 4.0 %collective-permute-start.4 = (f32[3,384]{1,0:T(4,128)S(1)}, f32[3,384]{1,0:T(4,128)S(1)}, u32[]{:S(2)}, u32[]{:S(2)}) collective-permute-start(f32[3,384]{1,0:T(4,128)S(1)} %pad_maximum_fusion.10), channel_id=1, source_target_pairs={{0,4},{4,8},{8,12},{12,16},{16,20},{20,24},{24,28},{28,0},{1,5},{5... | collective-permute-start | bytes 13832 | tf_op jit(solution)/shard_map/ppermute | solution.py:501
  31.2 2.8 %collective-permute-start.5 = (f32[3,384]{1,0:T(4,128)S(1)}, f32[3,384]{1,0:T(4,128)S(1)}, u32[]{:S(2)}, u32[]{:S(2)}) collective-permute-start(f32[3,384]{1,0:T(4,128)S(1)} %pad_maximum_fusion.10), channel_id=1, source_target_pairs={{4,0},{8,4},{12,8},{16,12},{20,16},{24,20},{28,24},{0,28},{5,1},{9... | collective-permute-start | bytes 13832 | tf_op jit(solution)/shard_map/ppermute | solution.py:502
  32.6 11.5 %copy-start.17 = (f32[3,128]{1,0:T(4,128)}, f32[3,128]{1,0:T(4,128)S(1)}, u32[]{:S(2)}) copy-start(f32[3,128]{1,0:T(4,128)S(1)} %add_multiply_fusion.6) | copy-start | bytes 4612
  33.9 10.1 %collective-permute-start.8 = (f32[3,128]{1,0:T(4,128)S(1)}, f32[3,128]{1,0:T(4,128)S(1)}, u32[]{:S(2)}, u32[]{:S(2)}) collective-permute-start(f32[3,128]{1,0:T(4,128)S(1)} %add_multiply_fusion.6), channel_id=1, source_target_pairs={{0,1},{1,2},{2,3},{3,0},{4,5},{5,6},{6,7},{7,4},{8,9},{9,10},{10,1... | collective-permute-start | bytes 4616 | tf_op jit(solution)/shard_map/ppermute | solution.py:23
  34.0 10.1 %collective-permute-start.9 = (f32[3,128]{1,0:T(4,128)S(1)}, f32[3,128]{1,0:T(4,128)S(1)}, u32[]{:S(2)}, u32[]{:S(2)}) collective-permute-start(f32[3,128]{1,0:T(4,128)S(1)} %add_multiply_fusion.6), channel_id=1, source_target_pairs={{1,0},{2,1},{3,2},{0,3},{5,4},{6,5},{7,6},{4,7},{9,8},{10,9},{11,1... | collective-permute-start | bytes 4616 | tf_op jit(solution)/shard_map/ppermute | solution.py:25
  44.1 4.0 %collective-permute-start.10 = (f32[3,384]{1,0:T(4,128)S(1)}, f32[3,384]{1,0:T(4,128)S(1)}, u32[]{:S(2)}, u32[]{:S(2)}) collective-permute-start(f32[3,384]{1,0:T(4,128)S(1)} %constant_dynamic-update-slice_fusion), channel_id=1, source_target_pairs={{0,4},{4,8},{8,12},{12,16},{16,20},{20,24},{24,28},{28,0},{1,5},{5... | collective-permute-start | bytes 13832 | tf_op jit(solution)/shard_map/ppermute | solution.py:501
  44.3 3.9 %collective-permute-start.11 = (f32[3,384]{1,0:T(4,128)S(1)}, f32[3,384]{1,0:T(4,128)S(1)}, u32[]{:S(2)}, u32[]{:S(2)}) collective-permute-start(f32[3,384]{1,0:T(4,128)S(1)} %constant_dynamic-update-slice_fusion), channel_id=1, source_target_pairs={{4,0},{8,4},{12,8},{16,12},{20,16},{24,20},{28,24},{0,28},{5,1},{9... | collective-permute-start | bytes 13832 | tf_op jit(solution)/shard_map/ppermute | solution.py:502
  67.8 43.0 %all-to-all-start.2 = ((f32[8,3,16,16,128]{4,3,2,1,0:T(8,128)}), f32[8,3,16,16,128]{4,3,2,1,0:T(8,128)S(1)}, u32[]{:S(2)}, u32[]{:S(2)}) async-start(f32[8,3,16,16,128]{4,3,2,1,0:T(8,128)} %depth_forward.3), calls=%async_computation.2 | async-start | bytes 6291456 | tf_op jit(solution)/shard_map/all_to_all | solution.py:839
  75.3 1.8 copy-start.15
  76.4 0.7 copy-start.13
  78.7 1.0 copy-start.8
  110.8 42.3 %all-to-all-start = ((f32[8,3,16,16,128]{4,3,2,1,0:T(8,128)}), f32[8,3,16,16,128]{4,3,2,1,0:T(8,128)}, u32[]{:S(2)}, u32[]{:S(2)}) async-start(f32[8,3,16,16,128]{4,3,2,1,0:T(8,128)} %depth_forward.2), calls=%async_computation | async-start | bytes 6291456 | tf_op jit(solution)/shard_map/all_to_all | solution.py:839
  116.6 5.1 %copy-start.4 = (bf16[768,512]{1,0:T(8,128)(2,1)}, bf16[768,512]{1,0:T(8,128)(2,1)S(1)}, u32[]{:S(2)}) copy-start(bf16[768,512]{1,0:T(8,128)(2,1)S(1)} %maximum_maximum_fusion.refs_2_) | copy-start | bytes 2359300
  116.6 10.6 %copy-start.9 = (bf16[1536,256]{1,0:T(8,128)(2,1)S(1)}, bf16[1536,256]{1,0:T(8,128)(2,1)}, u32[]{:S(2)}) copy-start(bf16[1536,256]{1,0:T(8,128)(2,1)} %copy-done.8) | copy-start | bytes 2359300
  121.6 1.7 copy-start.6
  123.3 12.9 %copy-start.14 = (f32[8,8,256]{2,1,0:T(8,128)S(1)}, f32[8,8,256]{2,1,0:T(8,128)}, u32[]{:S(2)}) copy-start(f32[8,8,256]{2,1,0:T(8,128)} %copy-done.13) | copy-start | bytes 196612
  123.3 8.3 %collective-permute-start.15 = (f32[16,8,256]{2,1,0:T(8,128)S(1)}, f32[16,8,256]{2,1,0:T(8,128)S(1)}, u32[]{:S(2)}, u32[]{:S(2)}) collective-permute-start(f32[16,8,256]{2,1,0:T(8,128)S(1)} %get-tuple-element.20), channel_id=1, source_target_pairs={{0,1},{1,2},{2,3},{3,0},{4,5},{5,6},{6,7},{7,4},{8,9},{9,10},{10,1... | collective-permute-start | bytes 393224 | tf_op jit(solution)/shard_map/ppermute | solution.py:186
  123.3 12.9 %collective-permute-start.16 = (f32[16,8,256]{2,1,0:T(8,128)S(1)}, f32[16,8,256]{2,1,0:T(8,128)S(1)}, u32[]{:S(2)}, u32[]{:S(2)}) collective-permute-start(f32[16,8,256]{2,1,0:T(8,128)S(1)} %get-tuple-element.20), channel_id=1, source_target_pairs={{0,2},{1,3},{2,0},{3,1},{4,6},{5,7},{6,4},{7,5},{8,10},{9,11},{10,... | collective-permute-start | bytes 393224 | tf_op jit(solution)/shard_map/ppermute | solution.py:186
  123.9 12.4 %collective-permute-start.17 = (f32[16,8,256]{2,1,0:T(8,128)S(1)}, f32[16,8,256]{2,1,0:T(8,128)S(1)}, u32[]{:S(2)}, u32[]{:S(2)}) collective-permute-start(f32[16,8,256]{2,1,0:T(8,128)S(1)} %get-tuple-element.20), channel_id=1, source_target_pairs={{0,3},{1,0},{2,1},{3,2},{4,7},{5,4},{6,5},{7,6},{8,11},{9,8},{10,9... | collective-permute-start | bytes 393224 | tf_op jit(solution)/shard_map/ppermute | solution.py:186
  127.2 9.1 %copy-start.2 = (bf16[1536,256]{1,0:T(8,128)(2,1)}, bf16[1536,256]{1,0:T(8,128)(2,1)S(1)}, u32[]{:S(2)}) copy-start(bf16[1536,256]{1,0:T(8,128)(2,1)S(1)} %broadcast_multiply_fusion.refs_3_) | copy-start | bytes 2359300
  146.2 1.7 copy-start
  153.2 41.4 %all-to-all-start.3 = ((f32[8,3,16,16,128]{4,3,2,1,0:T(8,128)}), f32[8,3,16,16,128]{4,3,2,1,0:T(8,128)S(1)}, u32[]{:S(2)}, u32[]{:S(2)}) async-start(f32[8,3,16,16,128]{4,3,2,1,0:T(8,128)} %copy-done), calls=%async_computation.3 | async-start | bytes 6291456 | tf_op jit(solution)/shard_map/all_to_all | solution.py:843
  157.0 1.1 copy-start.5
  158.2 21.8 %copy-start.12 = (f32[8,8,256]{2,1,0:T(8,128)S(1)}, f32[8,8,256]{2,1,0:T(8,128)}, u32[]{:S(2)}) copy-start(f32[8,8,256]{2,1,0:T(8,128)} %copy-done.11) | copy-start | bytes 196612
  158.2 21.8 %copy-start.16 = (f32[8,8,256]{2,1,0:T(8,128)S(1)}, f32[8,8,256]{2,1,0:T(8,128)}, u32[]{:S(2)}) copy-start(f32[8,8,256]{2,1,0:T(8,128)} %copy-done.15) | copy-start | bytes 196612
  158.2 21.9 %copy-start.3 = (bf16[1536,256]{1,0:T(8,128)(2,1)S(1)}, bf16[1536,256]{1,0:T(8,128)(2,1)}, u32[]{:S(2)}) copy-start(bf16[1536,256]{1,0:T(8,128)(2,1)} %copy-done.2) | copy-start | bytes 2359300
  165.4 1.7 copy-start.7
  167.1 8.3 %collective-permute-start.12 = (f32[16,8,256]{2,1,0:T(8,128)S(1)}, f32[16,8,256]{2,1,0:T(8,128)S(1)}, u32[]{:S(2)}, u32[]{:S(2)}) collective-permute-start(f32[16,8,256]{2,1,0:T(8,128)S(1)} %get-tuple-element.18), channel_id=1, source_target_pairs={{0,1},{1,2},{2,3},{3,0},{4,5},{5,6},{6,7},{7,4},{8,9},{9,10},{10,1... | collective-permute-start | bytes 393224 | tf_op jit(solution)/shard_map/ppermute | solution.py:186
  167.1 12.9 %collective-permute-start.13 = (f32[16,8,256]{2,1,0:T(8,128)S(1)}, f32[16,8,256]{2,1,0:T(8,128)S(1)}, u32[]{:S(2)}, u32[]{:S(2)}) collective-permute-start(f32[16,8,256]{2,1,0:T(8,128)S(1)} %get-tuple-element.18), channel_id=1, source_target_pairs={{0,2},{1,3},{2,0},{3,1},{4,6},{5,7},{6,4},{7,5},{8,10},{9,11},{10,... | collective-permute-start | bytes 393224 | tf_op jit(solution)/shard_map/ppermute | solution.py:186
  167.6 12.4 %collective-permute-start.14 = (f32[16,8,256]{2,1,0:T(8,128)S(1)}, f32[16,8,256]{2,1,0:T(8,128)S(1)}, u32[]{:S(2)}, u32[]{:S(2)}) collective-permute-start(f32[16,8,256]{2,1,0:T(8,128)S(1)} %get-tuple-element.18), channel_id=1, source_target_pairs={{0,3},{1,0},{2,1},{3,2},{4,7},{5,4},{6,5},{7,6},{8,11},{9,8},{10,9... | collective-permute-start | bytes 393224 | tf_op jit(solution)/shard_map/ppermute | solution.py:186
  190.1 1.7 copy-start.1
  191.8 7.3 %copy-start.10 = (bf16[256,768]{1,0:T(8,128)(2,1)S(1)}, bf16[256,768]{1,0:T(8,128)(2,1)}, u32[]{:S(2)}) copy-start(bf16[256,768]{1,0:T(8,128)(2,1)} %constant.221.clone) | copy-start | bytes 1179652
  194.6 42.3 %all-to-all-start.1 = ((f32[8,3,16,16,128]{4,3,2,1,0:T(8,128)}), f32[8,3,16,16,128]{4,3,2,1,0:T(8,128)}, u32[]{:S(2)}, u32[]{:S(2)}) async-start(f32[8,3,16,16,128]{4,3,2,1,0:T(8,128)} %copy-done.1), calls=%async_computation.1 | async-start | bytes 6291456 | tf_op jit(solution)/shard_map/all_to_all | solution.py:843
  242.2 12.4 %collective-permute-start.18 = (f32[3,2,64,256]{3,2,1,0:T(8,128)S(1)}, f32[3,2,64,256]{3,2,1,0:T(8,128)S(1)}, u32[]{:S(2)}, u32[]{:S(2)}) collective-permute-start(f32[3,2,64,256]{3,2,1,0:T(8,128)S(1)} %get-tuple-element.21), channel_id=1, source_target_pairs={{0,4},{4,8},{8,12},{12,16},{16,20},{20,24},{24,28},{28,0},{1,5},{5... | collective-permute-start | bytes 1179656 | tf_op jit(solution)/shard_map/ppermute | solution.py:471
  242.2 13.1 %collective-permute-start.19 = (f32[3,2,64,256]{3,2,1,0:T(8,128)S(1)}, f32[3,2,64,256]{3,2,1,0:T(8,128)}, u32[]{:S(2)}, u32[]{:S(2)}) collective-permute-start(f32[3,2,64,256]{3,2,1,0:T(8,128)S(1)} %get-tuple-element.22), channel_id=1, source_target_pairs={{4,0},{8,4},{12,8},{16,12},{20,16},{24,20},{28,24},{0,28},{5,1},{9... | collective-permute-start | bytes 1179656 | tf_op jit(solution)/shard_map/ppermute | solution.py:472
  254.5 0.8 copy-start.22
  262.3 5.4 %collective-permute-start.20 = (f32[3,128]{1,0:T(4,128)S(1)}, f32[3,128]{1,0:T(4,128)S(1)}, u32[]{:S(2)}, u32[]{:S(2)}) collective-permute-start(f32[3,128]{1,0:T(4,128)S(1)} %get-tuple-element.45), channel_id=1, source_target_pairs={{0,1},{1,2},{2,3},{3,0},{4,5},{5,6},{6,7},{7,4},{8,9},{9,10},{10,1... | collective-permute-start | bytes 4616 | tf_op jit(solution)/shard_map/ppermute | solution.py:494
  262.3 5.4 %collective-permute-start.21 = (f32[3,128]{1,0:T(4,128)S(1)}, f32[3,128]{1,0:T(4,128)S(1)}, u32[]{:S(2)}, u32[]{:S(2)}) collective-permute-start(f32[3,128]{1,0:T(4,128)S(1)} %get-tuple-element.46), channel_id=1, source_target_pairs={{1,0},{2,1},{3,2},{0,3},{5,4},{6,5},{7,6},{4,7},{9,8},{10,9},{11,1... | collective-permute-start | bytes 4616 | tf_op jit(solution)/shard_map/ppermute | solution.py:495
  (1 other events, 0.6 us)

commit v3 on v2

--- a/solution.py
+++ b/solution.py
@@ -332,6 +332,7 @@
             pltpu.VMEM((plan.y_block * plan.slab, plan.grid), f32),
         ],
         name="depth_forward",
+        compiler_params=pltpu.CompilerParams(vmem_limit_bytes=32 * 1024 * 1024),
         cost_estimate=cost(plan, 20, 20),
     )(velocity, noise, *own, *sides, table)
 
@@ -484,6 +485,7 @@
         out_specs=pl.BlockSpec((1, 1, wide), lambda c: (c, 0, 0)),
         out_shape=jax.ShapeDtypeStruct((3, 1, wide), f32),
         name="sample",
+        compiler_params=pltpu.CompilerParams(vmem_limit_bytes=24 * 1024 * 1024),
         cost_estimate=cost(plan, 6, 8),
     )(field, below, above, *column)[:, 0]
     return found

time: 269 us -> 286 us (1.063)
  other arithmetic: 20 us -> 48.7 us
  Pallas kernels: 91.7 us -> 80.5 us
  waiting for transfers between devices: 84.8 us -> 73.8 us
  local copies, waits for them, and re-layouts: 16.2 us -> 25.4 us
    unnamed x25, other arithmetic: 3.69 us -> 30.6 us
    all_to_all x2, waiting for transfers between devices: 18.6 us -> 5.48 us  [project(): lax.all_to_all(spectrum, 'gx', split_axis=0, concat_axis=0, tiled=True)]
    unnamed x57 -> x137, local copies, waits for them, and re-layouts: 11.1 us -> 21.4 us
    pallas_call x2, Pallas kernels: 12.6 us -> 5.83 us  [sample(): pl.pallas_call(lambda *refs: sample_kernel(plan, *refs), grid=(3,), in_sp...]
    pallas_call x2, Pallas kernels: 34.3 us -> 30 us  [depth_forward(): pl.pallas_call(lambda *refs: depth_forward_kernel(plan, (refs[0], refs[1]...]
  transfers between devices with their start and end apart: 26 -> 26, of which waited for: 13 -> 13; matrix products, arithmetic and copies ran while one was open for 8% -> 17% of each run, Pallas kernels for 21% -> 19%
where the time goes in v3:
time: 286 us; the launch traced here: 285 us
  Pallas kernels  80.5 us (28%)
  waiting for transfers between devices  73.8 us (26%)
  starting transfers between devices  53 us (19%)
  other arithmetic  48.7 us (17%)
  local copies, waits for them, and re-layouts  25.4 us (9%)
  between operations  3.15 us (1%)
    all_to_all x2, waiting for transfers between devices, project(): lax.all_to_all(solved, 'gx', split_axis=0, concat_axis=0, tiled=True)  40.5 us
    unnamed x25, other arithmetic  30.6 us
    pallas_call x2, Pallas kernels, depth_forward(): pl.pallas_call(lambda *refs: depth_forward_kernel(plan, (refs[0], refs[1]...  30 us
    unnamed x137, local copies, waits for them, and re-layouts  21.4 us
    pallas_call x2, Pallas kernels, line_backward(): pl.pallas_call(lambda *refs: line_backward_kernel(plan, chunk, yh_step, *...  19.7 us
    ppermute x6, waiting for transfers between devices, incoming(): lax.ppermute(ends, 'gy', [(i, (i + hop) % gy) for i in range(gy)])  18.1 us
    pallas_call x2, Pallas kernels, line_forward(): pl.pallas_call(lambda *refs: line_forward_kernel(plan, chunk, yh_step, *r...  12.3 us
    all_to_all x2, starting transfers between devices, project(): lax.all_to_all(spectrum, 'gx', split_axis=0, concat_axis=0, tiled=True)  9.6 us
  transfers between devices with their start and end apart: 26, of which 13 were waited for; matrix products, arithmetic and copies ran while one was open for 17% of the time, Pallas kernels for 19%

profile of v3, /device:TPU:0, one launch (start us, length us, event | category | flops | bytes accessed | tf_op | source)
XLA Modules:
  0.0 284.6 jit_solution(295372776819686152)
XLA Ops:
  1.3 3.1 %collective-permute-start = (f32[3,128]{1,0:T(4,128)S(1)}, f32[3,128]{1,0:T(4,128)S(1)}, u32[]{:S(2)}, u32[]{:S(2)}) collective-permute-start(f32[3,128]{1,0:T(4,128)S(1)} %convert_add_fusion), channel_id=1, source_target_pairs={{0,1},{1,2},{2,3},{3,0},{4,5},{5,6},{6,7},{7,4},{8,9},{9,10},{10,1... | collective-permute-start | bytes 4616 | tf_op jit(solution)/shard_map/ppermute | solution.py:23
  4.4 2.0 collective-permute-start.1
  7.7 2.6 collective-permute-start.3
  14.8 3.1 %collective-permute-done.2.refs_1_ = f32[3,2,64,256]{3,2,1,0:T(8,128)S(1)} collective-permute-done((f32[3,2,64,256]{3,2,1,0:T(8,128)S(1)}, f32[3,2,64,256]{3,2,1,0:T(8,128)S(1)}, u32[]{:S(2)}, u32[]{:S(2)}) %collective-permute-start.2) | collective-permute-done | bytes 393248 | tf_op jit(solution)/shard_map/ppermute | solution.py:472
  18.3 2.8 copy-done.28
  21.1 2.9 %sample.2 = f32[3,1,384]{2,1,0:T(1,128)S(1)} custom-call(f32[3,32,64,256]{3,2,1,0:T(8,128)S(1)} %copy-done.28, f32[3,2,64,256]{3,2,1,0:T(8,128)S(1)} %collective-permute-done.2.refs_1_, f32[3,2,64,256]{3,2,1,0:T(8,128)S(1)} %collective-permute-done.3.refs_2_, f32[2,40,384]{2,1,0:T(8,128)S(1)} %pad_maximum_fusion.8.refs_3_.refs_2_, ...), custom_call_target="tpu_custom_call" | custom-call | flops 6000000000 | bytes 8000000 | tf_op jit(solution)/shard_map/sample/pallas_call | solution.py:476
  24.1 3.8 %collective-permute-start.7 = (f32[3,128]{1,0:T(4,128)S(1)}, f32[3,128]{1,0:T(4,128)S(1)}, u32[]{:S(2)}, u32[]{:S(2)}) collective-permute-start(f32[3,128]{1,0:T(4,128)S(1)} %get-tuple-element.48), channel_id=1, source_target_pairs={{1,0},{2,1},{3,2},{0,3},{5,4},{6,5},{7,6},{4,7},{9,8},{10,9},{11,1... | collective-permute-start | bytes 4616 | tf_op jit(solution)/shard_map/ppermute | solution.py:497
  32.6 3.8 %collective-permute-start.9 = (f32[3,128]{1,0:T(4,128)S(1)}, f32[3,128]{1,0:T(4,128)S(1)}, u32[]{:S(2)}, u32[]{:S(2)}) collective-permute-start(f32[3,128]{1,0:T(4,128)S(1)} %add_multiply_fusion.6), channel_id=1, source_target_pairs={{1,0},{2,1},{3,2},{0,3},{5,4},{6,5},{7,6},{4,7},{9,8},{10,9},{11,1... | collective-permute-start | bytes 4616 | tf_op jit(solution)/shard_map/ppermute | solution.py:25
  36.5 2.8 fusion.6
  41.1 2.6 collective-permute-start.11
  45.1 15.4 %depth_forward.3 = f32[8,3,16,16,128]{4,3,2,1,0:T(8,128)} custom-call(f32[3,32,64,256]{3,2,1,0:T(8,128)S(1)} %copy-done.29, f32[3,32,64,256]{3,2,1,0:T(8,128)S(1)} %copy-done.33, f32[2,40,384]{2,1,0:T(8,128)S(1)} %pad_maximum_fusion.8.refs_3_.refs_2_, f32[2,64,384]{2,1,0:T(8,128)S(1)} %pad_maximum_fusion.5.refs_4_.refs_3_, ...), custom_call_target="tpu_custom_call" | custom-call | flops 20000000000 | bytes 20000000 | tf_op jit(solution)/shard_map/depth_forward/pallas_call | solution.py:320
  63.4 5.0 %all-to-all-start.2 = ((f32[8,3,16,16,128]{4,3,2,1,0:T(8,128)}), f32[8,3,16,16,128]{4,3,2,1,0:T(8,128)S(1)}, u32[]{:S(2)}, u32[]{:S(2)}) async-start(f32[8,3,16,16,128]{4,3,2,1,0:T(8,128)} %depth_forward.3), calls=%async_computation.2 | async-start | bytes 6291456 | tf_op jit(solution)/shard_map/all_to_all | solution.py:841
  71.1 1.5 constant_dynamic-update-slice_fusion.65
  73.5 1.5 constant_dynamic-update-slice_fusion.63
  96.3 1.5 constant_dynamic-update-slice_fusion.29
  97.7 1.5 constant_dynamic-update-slice_fusion.70
  107.1 2.8 copy-done.30
  109.9 2.8 copy-done.34
  112.7 14.6 %depth_forward.2 = f32[8,3,16,16,128]{4,3,2,1,0:T(8,128)S(1)} custom-call(f32[3,32,64,256]{3,2,1,0:T(8,128)S(1)} %copy-done.30, f32[3,32,64,256]{3,2,1,0:T(8,128)S(1)} %copy-done.34, f32[2,40,384]{2,1,0:T(8,128)S(1)} %copy-done.26, f32[2,64,384]{2,1,0:T(8,128)S(1)} %copy-done.20, bf16[2,256,384]{2,1,0:T(8,128)(2,1)S(1)} %copy-done.15, ...), custom_call_target="tpu_custom_call" | custom-call | flops 20000000000 | bytes 20000000 | tf_op jit(solution)/shard_map/depth_forward/pallas_call | solution.py:320
  127.4 1.7 copy-done
  129.0 4.6 %all-to-all-start = ((f32[8,3,16,16,128]{4,3,2,1,0:T(8,128)}), f32[8,3,16,16,128]{4,3,2,1,0:T(8,128)}, u32[]{:S(2)}, u32[]{:S(2)}) async-start(f32[8,3,16,16,128]{4,3,2,1,0:T(8,128)} %copy-done), calls=%async_computation | async-start | bytes 6291456 | tf_op jit(solution)/shard_map/all_to_all | solution.py:841
  134.8 5.0 %line_forward.3 = (f32[3,64,2,8,256]{4,3,2,1,0:T(8,128)S(1)}, f32[16,8,256]{2,1,0:T(8,128)S(1)}) custom-call(f32[8,3,16,16,128]{4,3,2,1,0:T(8,128)S(1)} %all-to-all-done.2.refs_0_, f32[18,8,256]{2,1,0:T(8,128)S(1)} %copy-done.23, bf16[768,512]{1,0:T(8,128)(2,1)S(1)} %maximum_maximum_fusion.refs_2_), custom_call_target="tpu_custom_call" | custom-call | flops 8000000000 | bytes 10000000 | tf_op jit(solution)/shard_map/line_forward/pallas_call | solution.py:627
  139.9 1.6 copy-done.38
  142.9 2.4 collective-permute-start.17
  145.4 4.4 %collective-permute-done.15 = f32[16,8,256]{2,1,0:T(8,128)S(1)} collective-permute-done((f32[16,8,256]{2,1,0:T(8,128)S(1)}, f32[16,8,256]{2,1,0:T(8,128)S(1)}, u32[]{:S(2)}, u32[]{:S(2)}) %collective-permute-start.15) | collective-permute-done | bytes 131104 | tf_op jit(solution)/shard_map/ppermute | solution.py:186
  149.8 4.6 %collective-permute-done.16 = f32[16,8,256]{2,1,0:T(8,128)S(1)} collective-permute-done((f32[16,8,256]{2,1,0:T(8,128)S(1)}, f32[16,8,256]{2,1,0:T(8,128)S(1)}, u32[]{:S(2)}, u32[]{:S(2)}) %collective-permute-start.16) | collective-permute-done | bytes 131104 | tf_op jit(solution)/shard_map/ppermute | solution.py:186
  154.6 9.8 %line_backward.3 = f32[8,3,16,16,128]{4,3,2,1,0:T(8,128)S(1)} custom-call(f32[3,64,2,8,256]{4,3,2,1,0:T(8,128)} %copy-done.38, f32[18,8,256]{2,1,0:T(8,128)S(1)} %copy-done.23, f32[16,8,256]{2,1,0:T(8,128)S(1)} %pad_maximum_fusion.7.refs_2_, bf16[1536,256]{1,0:T(8,128)(2,1)S(1)} %broadcast_multiply_fusion.refs_3_), custom_call_target="tpu_custom_call" | custom-call | flops 12000000000 | bytes 12000000 | tf_op jit(solution)/shard_map/line_backward/pallas_call | solution.py:820
  164.4 1.6 copy-done.1
  166.0 5.5 %all-to-all-done.refs_0_ = f32[8,3,16,16,128]{4,3,2,1,0:T(8,128)} async-done(((f32[8,3,16,16,128]{4,3,2,1,0:T(8,128)}), f32[8,3,16,16,128]{4,3,2,1,0:T(8,128)}, u32[]{:S(2)}, u32[]{:S(2)}) %all-to-all-start) | async-done | bytes 3145760 | tf_op jit(solution)/shard_map/all_to_all | solution.py:841
  171.5 3.9 %all-to-all-start.3 = ((f32[8,3,16,16,128]{4,3,2,1,0:T(8,128)}), f32[8,3,16,16,128]{4,3,2,1,0:T(8,128)S(1)}, u32[]{:S(2)}, u32[]{:S(2)}) async-start(f32[8,3,16,16,128]{4,3,2,1,0:T(8,128)} %copy-done.1), calls=%async_computation.3 | async-start | bytes 6291456 | tf_op jit(solution)/shard_map/all_to_all | solution.py:845
  176.5 7.2 %line_forward.2 = (f32[3,64,2,8,256]{4,3,2,1,0:T(8,128)S(1)}, f32[16,8,256]{2,1,0:T(8,128)S(1)}) custom-call(f32[8,3,16,16,128]{4,3,2,1,0:T(8,128)} %all-to-all-done.refs_0_, f32[18,8,256]{2,1,0:T(8,128)S(1)} %copy-done.24, bf16[768,512]{1,0:T(8,128)(2,1)S(1)} %copy-done.6), custom_call_target="tpu_custom_call" | custom-call | flops 8000000000 | bytes 10000000 | tf_op jit(solution)/shard_map/line_forward/pallas_call | solution.py:627
  183.8 1.7 copy-done.39
  186.8 2.4 collective-permute-start.14
  189.2 4.5 %collective-permute-done.12 = f32[16,8,256]{2,1,0:T(8,128)S(1)} collective-permute-done((f32[16,8,256]{2,1,0:T(8,128)S(1)}, f32[16,8,256]{2,1,0:T(8,128)S(1)}, u32[]{:S(2)}, u32[]{:S(2)}) %collective-permute-start.12) | collective-permute-done | bytes 131104 | tf_op jit(solution)/shard_map/ppermute | solution.py:186
  193.7 4.6 %collective-permute-done.13 = f32[16,8,256]{2,1,0:T(8,128)S(1)} collective-permute-done((f32[16,8,256]{2,1,0:T(8,128)S(1)}, f32[16,8,256]{2,1,0:T(8,128)S(1)}, u32[]{:S(2)}, u32[]{:S(2)}) %collective-permute-start.13) | collective-permute-done | bytes 131104 | tf_op jit(solution)/shard_map/ppermute | solution.py:186
  198.5 9.9 %line_backward.2 = f32[8,3,16,16,128]{4,3,2,1,0:T(8,128)S(1)} custom-call(f32[3,64,2,8,256]{4,3,2,1,0:T(8,128)} %copy-done.39, f32[18,8,256]{2,1,0:T(8,128)S(1)} %copy-done.24, f32[16,8,256]{2,1,0:T(8,128)S(1)} %pad_maximum_fusion.6.refs_2_, bf16[1536,256]{1,0:T(8,128)(2,1)S(1)} %copy-done.4), custom_call_target="tpu_custom_call" | custom-call | flops 12000000000 | bytes 12000000 | tf_op jit(solution)/shard_map/line_backward/pallas_call | solution.py:820
  208.4 1.7 copy-done.2
  210.1 2.9 %all-to-all-done.3.refs_1_ = f32[8,3,16,16,128]{4,3,2,1,0:T(8,128)S(1)} async-done(((f32[8,3,16,16,128]{4,3,2,1,0:T(8,128)}), f32[8,3,16,16,128]{4,3,2,1,0:T(8,128)S(1)}, u32[]{:S(2)}, u32[]{:S(2)}) %all-to-all-start.3) | async-done | bytes 3145760 | tf_op jit(solution)/shard_map/all_to_all | solution.py:845
  212.9 4.5 %all-to-all-start.1 = ((f32[8,3,16,16,128]{4,3,2,1,0:T(8,128)}), f32[8,3,16,16,128]{4,3,2,1,0:T(8,128)}, u32[]{:S(2)}, u32[]{:S(2)}) async-start(f32[8,3,16,16,128]{4,3,2,1,0:T(8,128)} %copy-done.2), calls=%async_computation.1 | async-start | bytes 6291456 | tf_op jit(solution)/shard_map/all_to_all | solution.py:845
  217.6 37.7 %all-to-all-done.1.refs_0_ = f32[8,3,16,16,128]{4,3,2,1,0:T(8,128)} async-done(((f32[8,3,16,16,128]{4,3,2,1,0:T(8,128)}), f32[8,3,16,16,128]{4,3,2,1,0:T(8,128)}, u32[]{:S(2)}, u32[]{:S(2)}) %all-to-all-start.1) | async-done | bytes 3145760 | tf_op jit(solution)/shard_map/all_to_all | solution.py:845
  255.3 5.2 %depth_edges.1 = (f32[3,2,64,256]{3,2,1,0:T(8,128)S(1)}, f32[3,2,64,256]{3,2,1,0:T(8,128)S(1)}) custom-call(f32[8,3,16,16,128]{4,3,2,1,0:T(8,128)} %all-to-all-done.1.refs_0_, f32[8,3,16,16,128]{4,3,2,1,0:T(8,128)S(1)} %all-to-all-done.3.refs_1_, bf16[768,256]{1,0:T(8,128)(2,1)S(1)} %pad_maximum_fusion.3.refs_2_), custom_call_target="tpu_custom_call" | custom-call | flops 8000000000 | bytes 6000000 | tf_op jit(solution)/shard_map/depth_edges/pallas_call | solution.py:419
  260.6 2.7 collective-permute-start.19
  263.3 7.5 %depth_backward.1.refs_0_ = f32[3,32,64,256]{3,2,1,0:T(8,128)} custom-call(f32[8,3,16,16,128]{4,3,2,1,0:T(8,128)} %all-to-all-done.1.refs_0_, f32[8,3,16,16,128]{4,3,2,1,0:T(8,128)S(1)} %all-to-all-done.3.refs_1_, bf16[768,256]{1,0:T(8,128)(2,1)S(1)} %pad_maximum_fusion.3.refs_2_), custom_call_target="tpu_custom_call" | custom-call | flops 16000000000 | bytes 6000000 | tf_op jit(solution)/shard_map/depth_backward/pallas_call | solution.py:369
  270.8 2.1 collective-permute-done.18.refs_1_
  272.9 2.8 copy-done.35
  275.6 2.9 %sample.3 = f32[3,1,384]{2,1,0:T(1,128)S(1)} custom-call(f32[3,32,64,256]{3,2,1,0:T(8,128)S(1)} %copy-done.35, f32[3,2,64,256]{3,2,1,0:T(8,128)S(1)} %collective-permute-done.18.refs_1_, f32[3,2,64,256]{3,2,1,0:T(8,128)S(1)} %collective-permute-done.19.refs_2_, f32[2,40,384]{2,1,0:T(8,128)S(1)} %copy-done.27, f32[2,64,384]{2,1,0:T(8,128)S(1)} %copy-done.21, ...), custom_call_target="tpu_custom_call" | custom-call | flops 6000000000 | bytes 8000000 | tf_op jit(solution)/shard_map/sample/pallas_call | solution.py:476
  278.7 3.8 %collective-permute-start.21 = (f32[3,128]{1,0:T(4,128)S(1)}, f32[3,128]{1,0:T(4,128)S(1)}, u32[]{:S(2)}, u32[]{:S(2)}) collective-permute-start(f32[3,128]{1,0:T(4,128)S(1)} %get-tuple-element.46), channel_id=1, source_target_pairs={{1,0},{2,1},{3,2},{0,3},{5,4},{6,5},{7,6},{4,7},{9,8},{10,9},{11,1... | collective-permute-start | bytes 4616 | tf_op jit(solution)/shard_map/ppermute | solution.py:497
  282.5 1.6 collective-permute-done.20
  (236 shorter events, 54.8 us)
Async XLA Ops:
  1.3 11.1 %collective-permute-start = (f32[3,128]{1,0:T(4,128)S(1)}, f32[3,128]{1,0:T(4,128)S(1)}, u32[]{:S(2)}, u32[]{:S(2)}) collective-permute-start(f32[3,128]{1,0:T(4,128)S(1)} %convert_add_fusion), channel_id=1, source_target_pairs={{0,1},{1,2},{2,3},{3,0},{4,5},{5,6},{6,7},{7,4},{8,9},{9,10},{10,1... | collective-permute-start | bytes 4616 | tf_op jit(solution)/shard_map/ppermute | solution.py:23
  4.4 8.0 %collective-permute-start.1 = (f32[3,128]{1,0:T(4,128)S(1)}, f32[3,128]{1,0:T(4,128)S(1)}, u32[]{:S(2)}, u32[]{:S(2)}) collective-permute-start(f32[3,128]{1,0:T(4,128)S(1)} %convert_add_fusion), channel_id=1, source_target_pairs={{1,0},{2,1},{3,2},{0,3},{5,4},{6,5},{7,6},{4,7},{9,8},{10,9},{11,1... | collective-permute-start | bytes 4616 | tf_op jit(solution)/shard_map/ppermute | solution.py:25
  7.6 10.3 %collective-permute-start.2 = (f32[3,2,64,256]{3,2,1,0:T(8,128)S(1)}, f32[3,2,64,256]{3,2,1,0:T(8,128)S(1)}, u32[]{:S(2)}, u32[]{:S(2)}) collective-permute-start(f32[3,2,64,256]{3,2,1,0:T(8,128)S(1)} %get-tuple-element.30), channel_id=1, source_target_pairs={{0,4},{4,8},{8,12},{12,16},{16,20},{20,24},{24,28},{28,0},{1,5},{5... | collective-permute-start | bytes 1179656 | tf_op jit(solution)/shard_map/ppermute | solution.py:472
  7.7 10.6 %collective-permute-start.3 = (f32[3,2,64,256]{3,2,1,0:T(8,128)S(1)}, f32[3,2,64,256]{3,2,1,0:T(8,128)S(1)}, u32[]{:S(2)}, u32[]{:S(2)}) collective-permute-start(f32[3,2,64,256]{3,2,1,0:T(8,128)S(1)} %get-tuple-element.29), channel_id=1, source_target_pairs={{4,0},{8,4},{12,8},{16,12},{20,16},{24,20},{28,24},{0,28},{5,1},{9... | collective-permute-start | bytes 1179656 | tf_op jit(solution)/shard_map/ppermute | solution.py:473
  11.7 16.2 %copy-start.22 = (f32[18,8,256]{2,1,0:T(8,128)}, f32[18,8,256]{2,1,0:T(8,128)S(1)}, u32[]{:S(2)}) copy-start(f32[18,8,256]{2,1,0:T(8,128)S(1)} %constant_dynamic-update-slice_fusion.19) | copy-start | bytes 442372
  12.8 32.2 %copy-start.25 = (f32[2,40,384]{2,1,0:T(8,128)}, f32[2,40,384]{2,1,0:T(8,128)S(1)}, u32[]{:S(2)}) copy-start(f32[2,40,384]{2,1,0:T(8,128)S(1)} %pad_maximum_fusion.8.refs_3_.refs_2_) | copy-start | bytes 368644
  13.2 31.8 %copy-start.19 = (f32[2,64,384]{2,1,0:T(8,128)}, f32[2,64,384]{2,1,0:T(8,128)S(1)}, u32[]{:S(2)}) copy-start(f32[2,64,384]{2,1,0:T(8,128)S(1)} %pad_maximum_fusion.5.refs_4_.refs_3_) | copy-start | bytes 589828
  14.8 30.2 %copy-start.11 = (bf16[2,256,384]{2,1,0:T(8,128)(2,1)}, bf16[2,256,384]{2,1,0:T(8,128)(2,1)S(1)}, u32[]{:S(2)}) copy-start(bf16[2,256,384]{2,1,0:T(8,128)(2,1)S(1)} %get-tuple-element.33.refs_6_.refs_5_) | copy-start | bytes 1179652
  14.8 30.2 %copy-start.14 = (bf16[2,256,384]{2,1,0:T(8,128)(2,1)}, bf16[2,256,384]{2,1,0:T(8,128)(2,1)S(1)}, u32[]{:S(2)}) copy-start(bf16[2,256,384]{2,1,0:T(8,128)(2,1)S(1)} %get-tuple-element.34.refs_5_.refs_4_) | copy-start | bytes 1179652
  21.1 24.0 %copy-start.33 = (f32[3,32,64,256]{3,2,1,0:T(8,128)S(1)}, f32[3,32,64,256]{3,2,1,0:T(8,128)}, u32[]{:S(2)}) copy-start(f32[3,32,64,256]{3,2,1,0:T(8,128)} %refs_1_.3) | copy-start | bytes 18874372
  24.0 7.2 %collective-permute-start.6 = (f32[3,128]{1,0:T(4,128)S(1)}, f32[3,128]{1,0:T(4,128)S(1)}, u32[]{:S(2)}, u32[]{:S(2)}) collective-permute-start(f32[3,128]{1,0:T(4,128)S(1)} %get-tuple-element.47), channel_id=1, source_target_pairs={{0,1},{1,2},{2,3},{3,0},{4,5},{5,6},{6,7},{7,4},{8,9},{9,10},{10,1... | collective-permute-start | bytes 4616 | tf_op jit(solution)/shard_map/ppermute | solution.py:496
  24.1 7.1 %collective-permute-start.7 = (f32[3,128]{1,0:T(4,128)S(1)}, f32[3,128]{1,0:T(4,128)S(1)}, u32[]{:S(2)}, u32[]{:S(2)}) collective-permute-start(f32[3,128]{1,0:T(4,128)S(1)} %get-tuple-element.48), channel_id=1, source_target_pairs={{1,0},{2,1},{3,2},{0,3},{5,4},{6,5},{7,6},{4,7},{9,8},{10,9},{11,1... | collective-permute-start | bytes 4616 | tf_op jit(solution)/shard_map/ppermute | solution.py:497
  28.6 4.0 %collective-permute-start.4 = (f32[3,384]{1,0:T(4,128)S(1)}, f32[3,384]{1,0:T(4,128)S(1)}, u32[]{:S(2)}, u32[]{:S(2)}) collective-permute-start(f32[3,384]{1,0:T(4,128)S(1)} %pad_maximum_fusion.10), channel_id=1, source_target_pairs={{0,4},{4,8},{8,12},{12,16},{16,20},{20,24},{24,28},{28,0},{1,5},{5... | collective-permute-start | bytes 13832 | tf_op jit(solution)/shard_map/ppermute | solution.py:503
  29.8 2.8 collective-permute-start.5
  32.6 8.3 %collective-permute-start.8 = (f32[3,128]{1,0:T(4,128)S(1)}, f32[3,128]{1,0:T(4,128)S(1)}, u32[]{:S(2)}, u32[]{:S(2)}) collective-permute-start(f32[3,128]{1,0:T(4,128)S(1)} %add_multiply_fusion.6), channel_id=1, source_target_pairs={{0,1},{1,2},{2,3},{3,0},{4,5},{5,6},{6,7},{7,4},{8,9},{9,10},{10,1... | collective-permute-start | bytes 4616 | tf_op jit(solution)/shard_map/ppermute | solution.py:23
  32.6 8.3 %collective-permute-start.9 = (f32[3,128]{1,0:T(4,128)S(1)}, f32[3,128]{1,0:T(4,128)S(1)}, u32[]{:S(2)}, u32[]{:S(2)}) collective-permute-start(f32[3,128]{1,0:T(4,128)S(1)} %add_multiply_fusion.6), channel_id=1, source_target_pairs={{1,0},{2,1},{3,2},{0,3},{5,4},{6,5},{7,6},{4,7},{9,8},{10,9},{11,1... | collective-permute-start | bytes 4616 | tf_op jit(solution)/shard_map/ppermute | solution.py:25
  40.8 19.6 %copy-start.7 = (bf16[2,256,768]{2,1,0:T(8,128)(2,1)}, bf16[2,256,768]{2,1,0:T(8,128)(2,1)S(1)}, u32[]{:S(2)}) copy-start(bf16[2,256,768]{2,1,0:T(8,128)(2,1)S(1)} %get-tuple-element.31.refs_10_) | copy-start | bytes 2359300
  40.8 19.6 %copy-start.9 = (bf16[2,256,768]{2,1,0:T(8,128)(2,1)}, bf16[2,256,768]{2,1,0:T(8,128)(2,1)S(1)}, u32[]{:S(2)}) copy-start(bf16[2,256,768]{2,1,0:T(8,128)(2,1)S(1)} %get-tuple-element.32.refs_9_) | copy-start | bytes 2359300
  40.9 4.0 %collective-permute-start.10 = (f32[3,384]{1,0:T(4,128)S(1)}, f32[3,384]{1,0:T(4,128)S(1)}, u32[]{:S(2)}, u32[]{:S(2)}) collective-permute-start(f32[3,384]{1,0:T(4,128)S(1)} %constant_dynamic-update-slice_fusion), channel_id=1, source_target_pairs={{0,4},{4,8},{8,12},{12,16},{16,20},{20,24},{24,28},{28,0},{1,5},{5... | collective-permute-start | bytes 13832 | tf_op jit(solution)/shard_map/ppermute | solution.py:503
  41.1 3.9 %collective-permute-start.11 = (f32[3,384]{1,0:T(4,128)S(1)}, f32[3,384]{1,0:T(4,128)S(1)}, u32[]{:S(2)}, u32[]{:S(2)}) collective-permute-start(f32[3,384]{1,0:T(4,128)S(1)} %constant_dynamic-update-slice_fusion), channel_id=1, source_target_pairs={{4,0},{8,4},{12,8},{16,12},{20,16},{24,20},{28,24},{0,28},{5,1},{9... | collective-permute-start | bytes 13832 | tf_op jit(solution)/shard_map/ppermute | solution.py:504
  43.7 16.8 %copy-start.17 = (f32[2,40,768]{2,1,0:T(8,128)}, f32[2,40,768]{2,1,0:T(8,128)S(1)}, u32[]{:S(2)}) copy-start(f32[2,40,768]{2,1,0:T(8,128)S(1)} %pad_maximum_fusion.4.refs_7_) | copy-start | bytes 737284
  43.7 16.8 %copy-start.31 = (f32[3,1,384]{2,1,0:T(1,128)}, f32[3,1,384]{2,1,0:T(1,128)S(1)}, u32[]{:S(2)}) copy-start(f32[3,1,384]{2,1,0:T(1,128)S(1)} %copy.13.refs_6_) | copy-start | bytes 13828
  63.4 65.6 %all-to-all-start.2 = ((f32[8,3,16,16,128]{4,3,2,1,0:T(8,128)}), f32[8,3,16,16,128]{4,3,2,1,0:T(8,128)S(1)}, u32[]{:S(2)}, u32[]{:S(2)}) async-start(f32[8,3,16,16,128]{4,3,2,1,0:T(8,128)} %depth_forward.3), calls=%async_computation.2 | async-start | bytes 6291456 | tf_op jit(solution)/shard_map/all_to_all | solution.py:841
  68.4 35.0 %copy-start.45 = (pred[8]{0:T(512)(128)(4,1)S(1)}, pred[8]{0:T(512)(128)(4,1)}, u32[]{:S(2)}) copy-start(pred[8]{0:T(512)(128)(4,1)} %get-tuple-element.127) | copy-start | bytes 28
  68.4 35.0 %copy-start.46 = (pred[8]{0:T(512)(128)(4,1)S(1)}, pred[8]{0:T(512)(128)(4,1)}, u32[]{:S(2)}) copy-start(pred[8]{0:T(512)(128)(4,1)} %get-tuple-element.126) | copy-start | bytes 28
  68.4 35.0 %copy-start.61 = (pred[256]{0:T(512)(128)(4,1)S(1)}, pred[256]{0:T(512)(128)(4,1)}, u32[]{:S(2)}) copy-start(pred[256]{0:T(512)(128)(4,1)} %get-tuple-element.130) | copy-start | bytes 772
  68.5 35.0 %copy-start.62 = (pred[256]{0:T(512)(128)(4,1)S(1)}, pred[256]{0:T(512)(128)(4,1)}, u32[]{:S(2)}) copy-start(pred[256]{0:T(512)(128)(4,1)} %get-tuple-element.131) | copy-start | bytes 772
  68.5 35.7 %copy-start.44 = (pred[256]{0:T(512)(128)(4,1)S(1)}, pred[256]{0:T(512)(128)(4,1)}, u32[]{:S(2)}) copy-start(pred[256]{0:T(512)(128)(4,1)} %get-tuple-element.129) | copy-start | bytes 772
  68.5 36.3 %copy-start.55 = (pred[256]{0:T(512)(128)(4,1)S(1)}, pred[256]{0:T(512)(128)(4,1)}, u32[]{:S(2)}) copy-start(pred[256]{0:T(512)(128)(4,1)} %get-tuple-element.128) | copy-start | bytes 772
  86.3 20.0 %copy-start.53 = (f32[8,8,256]{2,1,0:T(8,128)}, f32[8,8,256]{2,1,0:T(8,128)S(1)}, u32[]{:S(2)}) copy-start(f32[8,8,256]{2,1,0:T(8,128)S(1)} %get-tuple-element.64) | copy-start | bytes 196612
  129.0 42.5 %all-to-all-start = ((f32[8,3,16,16,128]{4,3,2,1,0:T(8,128)}), f32[8,3,16,16,128]{4,3,2,1,0:T(8,128)}, u32[]{:S(2)}, u32[]{:S(2)}) async-start(f32[8,3,16,16,128]{4,3,2,1,0:T(8,128)} %copy-done), calls=%async_computation | async-start | bytes 6291456 | tf_op jit(solution)/shard_map/all_to_all | solution.py:841
  141.5 12.9 %copy-start.52 = (f32[8,8,256]{2,1,0:T(8,128)S(1)}, f32[8,8,256]{2,1,0:T(8,128)}, u32[]{:S(2)}) copy-start(f32[8,8,256]{2,1,0:T(8,128)} %copy-done.51) | copy-start | bytes 196612
  141.5 8.3 %collective-permute-start.15 = (f32[16,8,256]{2,1,0:T(8,128)S(1)}, f32[16,8,256]{2,1,0:T(8,128)S(1)}, u32[]{:S(2)}, u32[]{:S(2)}) collective-permute-start(f32[16,8,256]{2,1,0:T(8,128)S(1)} %get-tuple-element.20), channel_id=1, source_target_pairs={{0,1},{1,2},{2,3},{3,0},{4,5},{5,6},{6,7},{7,4},{8,9},{9,10},{10,1... | collective-permute-start | bytes 393224 | tf_op jit(solution)/shard_map/ppermute | solution.py:186
  141.5 12.9 %collective-permute-start.16 = (f32[16,8,256]{2,1,0:T(8,128)S(1)}, f32[16,8,256]{2,1,0:T(8,128)S(1)}, u32[]{:S(2)}, u32[]{:S(2)}) collective-permute-start(f32[16,8,256]{2,1,0:T(8,128)S(1)} %get-tuple-element.20), channel_id=1, source_target_pairs={{0,2},{1,3},{2,0},{3,1},{4,6},{5,7},{6,4},{7,5},{8,10},{9,11},{10,... | collective-permute-start | bytes 393224 | tf_op jit(solution)/shard_map/ppermute | solution.py:186
  142.9 11.5 %collective-permute-start.17 = (f32[16,8,256]{2,1,0:T(8,128)S(1)}, f32[16,8,256]{2,1,0:T(8,128)S(1)}, u32[]{:S(2)}, u32[]{:S(2)}) collective-permute-start(f32[16,8,256]{2,1,0:T(8,128)S(1)} %get-tuple-element.20), channel_id=1, source_target_pairs={{0,3},{1,0},{2,1},{3,2},{4,7},{5,4},{6,5},{7,6},{8,11},{9,8},{10,9... | collective-permute-start | bytes 393224 | tf_op jit(solution)/shard_map/ppermute | solution.py:186
  171.5 41.4 %all-to-all-start.3 = ((f32[8,3,16,16,128]{4,3,2,1,0:T(8,128)}), f32[8,3,16,16,128]{4,3,2,1,0:T(8,128)S(1)}, u32[]{:S(2)}, u32[]{:S(2)}) async-start(f32[8,3,16,16,128]{4,3,2,1,0:T(8,128)} %copy-done.1), calls=%async_computation.3 | async-start | bytes 6291456 | tf_op jit(solution)/shard_map/all_to_all | solution.py:845
  176.5 21.8 %copy-start.50 = (f32[8,8,256]{2,1,0:T(8,128)S(1)}, f32[8,8,256]{2,1,0:T(8,128)}, u32[]{:S(2)}) copy-start(f32[8,8,256]{2,1,0:T(8,128)} %copy-done.49) | copy-start | bytes 196612
  176.5 21.8 %copy-start.54 = (f32[8,8,256]{2,1,0:T(8,128)S(1)}, f32[8,8,256]{2,1,0:T(8,128)}, u32[]{:S(2)}) copy-start(f32[8,8,256]{2,1,0:T(8,128)} %copy-done.53) | copy-start | bytes 196612
  176.5 21.9 %copy-start.4 = (bf16[1536,256]{1,0:T(8,128)(2,1)S(1)}, bf16[1536,256]{1,0:T(8,128)(2,1)}, u32[]{:S(2)}) copy-start(bf16[1536,256]{1,0:T(8,128)(2,1)} %copy-done.3) | copy-start | bytes 2359300
  185.4 8.3 %collective-permute-start.12 = (f32[16,8,256]{2,1,0:T(8,128)S(1)}, f32[16,8,256]{2,1,0:T(8,128)S(1)}, u32[]{:S(2)}, u32[]{:S(2)}) collective-permute-start(f32[16,8,256]{2,1,0:T(8,128)S(1)} %get-tuple-element.18), channel_id=1, source_target_pairs={{0,1},{1,2},{2,3},{3,0},{4,5},{5,6},{6,7},{7,4},{8,9},{9,10},{10,1... | collective-permute-start | bytes 393224 | tf_op jit(solution)/shard_map/ppermute | solution.py:186
  185.4 12.9 %collective-permute-start.13 = (f32[16,8,256]{2,1,0:T(8,128)S(1)}, f32[16,8,256]{2,1,0:T(8,128)S(1)}, u32[]{:S(2)}, u32[]{:S(2)}) collective-permute-start(f32[16,8,256]{2,1,0:T(8,128)S(1)} %get-tuple-element.18), channel_id=1, source_target_pairs={{0,2},{1,3},{2,0},{3,1},{4,6},{5,7},{6,4},{7,5},{8,10},{9,11},{10,... | collective-permute-start | bytes 393224 | tf_op jit(solution)/shard_map/ppermute | solution.py:186
  186.8 11.5 %collective-permute-start.14 = (f32[16,8,256]{2,1,0:T(8,128)S(1)}, f32[16,8,256]{2,1,0:T(8,128)S(1)}, u32[]{:S(2)}, u32[]{:S(2)}) collective-permute-start(f32[16,8,256]{2,1,0:T(8,128)S(1)} %get-tuple-element.18), channel_id=1, source_target_pairs={{0,3},{1,0},{2,1},{3,2},{4,7},{5,4},{6,5},{7,6},{8,11},{9,8},{10,9... | collective-permute-start | bytes 393224 | tf_op jit(solution)/shard_map/ppermute | solution.py:186
  212.9 42.3 %all-to-all-start.1 = ((f32[8,3,16,16,128]{4,3,2,1,0:T(8,128)}), f32[8,3,16,16,128]{4,3,2,1,0:T(8,128)}, u32[]{:S(2)}, u32[]{:S(2)}) async-start(f32[8,3,16,16,128]{4,3,2,1,0:T(8,128)} %copy-done.2), calls=%async_computation.1 | async-start | bytes 6291456 | tf_op jit(solution)/shard_map/all_to_all | solution.py:845
  260.5 12.3 %collective-permute-start.18 = (f32[3,2,64,256]{3,2,1,0:T(8,128)S(1)}, f32[3,2,64,256]{3,2,1,0:T(8,128)S(1)}, u32[]{:S(2)}, u32[]{:S(2)}) collective-permute-start(f32[3,2,64,256]{3,2,1,0:T(8,128)S(1)} %get-tuple-element.21), channel_id=1, source_target_pairs={{0,4},{4,8},{8,12},{12,16},{16,20},{20,24},{24,28},{28,0},{1,5},{5... | collective-permute-start | bytes 1179656 | tf_op jit(solution)/shard_map/ppermute | solution.py:472
  260.6 12.2 %collective-permute-start.19 = (f32[3,2,64,256]{3,2,1,0:T(8,128)S(1)}, f32[3,2,64,256]{3,2,1,0:T(8,128)S(1)}, u32[]{:S(2)}, u32[]{:S(2)}) collective-permute-start(f32[3,2,64,256]{3,2,1,0:T(8,128)S(1)} %get-tuple-element.22), channel_id=1, source_target_pairs={{4,0},{8,4},{12,8},{16,12},{20,16},{24,20},{28,24},{0,28},{5,1},{9... | collective-permute-start | bytes 1179656 | tf_op jit(solution)/shard_map/ppermute | solution.py:473
  263.3 20.8 %copy-start.60 = (f32[128]{0:T(128)S(1)}, f32[128]{0:T(128)}, u32[]{:S(2)}) copy-start(f32[128]{0:T(128)} %copy-done.59) | copy-start | bytes 1540
  278.6 5.4 %collective-permute-start.20 = (f32[3,128]{1,0:T(4,128)S(1)}, f32[3,128]{1,0:T(4,128)S(1)}, u32[]{:S(2)}, u32[]{:S(2)}) collective-permute-start(f32[3,128]{1,0:T(4,128)S(1)} %get-tuple-element.45), channel_id=1, source_target_pairs={{0,1},{1,2},{2,3},{3,0},{4,5},{5,6},{6,7},{7,4},{8,9},{9,10},{10,1... | collective-permute-start | bytes 4616 | tf_op jit(solution)/shard_map/ppermute | solution.py:496
  278.7 5.4 %collective-permute-start.21 = (f32[3,128]{1,0:T(4,128)S(1)}, f32[3,128]{1,0:T(4,128)S(1)}, u32[]{:S(2)}, u32[]{:S(2)}) collective-permute-start(f32[3,128]{1,0:T(4,128)S(1)} %get-tuple-element.46), channel_id=1, source_target_pairs={{1,0},{2,1},{3,2},{0,3},{5,4},{6,5},{7,6},{4,7},{9,8},{10,9},{11,1... | collective-permute-start | bytes 4616 | tf_op jit(solution)/shard_map/ppermute | solution.py:497
  (41 other events, 253.7 us)
